TPU v7x, 32 devices: a whole 2x2x4 slice. The times are simulated.
32 devices in a mesh: group: 2 (over y), phi: 4 (over z), eta: 2 (over x), half: 2 (over core).
Axes of the slice: x: 2, y: 2, z: 4, core: 2. Of those that a mesh axis runs over, the one named last changes fastest.
Arguments:
- feats: bfloat16 [8, 2, 512, 512], P(('group', 'phi'), 'eta', 'half'), parts along dimension 0, may hold values from -6 to 6
- cotangent: bfloat16 [8, 2, 512, 512], P(('group', 'phi'), 'eta', 'half'), parts along dimension 0, may hold values from -6 to 6
- tiles: bfloat16 [8, 2, 24, 128, 128], P(('group', 'phi'), 'eta', 'half'), parts along dimension 0, may hold values from -0.21875 to 0.21875
- tile_src: int32 [8, 2, 24], P(('group', 'phi'), 'eta', 'half'), parts along dimension 0, may hold values from 0 to 5
- tile_dst: int32 [8, 2, 24], P(('group', 'phi'), 'eta', 'half'), parts along dimension 0, may hold values from -1 to 3, as said below
- weights: bfloat16 [2, 512, 512], replicated, may hold values from -0.25 to 0.25
- mask: int32 [2, 8, 8], replicated, may hold values 0 or 1
- counts: int32 [8, 2], P(('group', 'phi'), 'eta'), parts along dimension 0, may hold values from 128 to 512, as said below
Outputs:
- final: bfloat16 [8, 2, 512, 512], P(('group', 'phi'), 'eta', 'half'), parts along dimension 0
- grad_w: float32 [4, 512, 512], P('group', 'phi'), parts along dimension 0
There are 2 independent parts, one for each index of `group`. A program takes and returns all parts, laid end to end along the dimension named above; an argument that names none is the same for every part. Nothing has to cross between parts.
Inputs may be any that keep to these rules, and one draw needn't show every extreme that they name: `tile_dst`: in each region half the live tiles fill the first slots and the rest hold -1; some region half has all 12 slots live. `counts`: some region is full and some holds a quarter of its hits.
All inputs are finite; a program needn't handle non-finite values.
Results may differ from a plain program's by a relative error of at most 0.017.
Values may be sent and summed in bfloat16 or wider, within the bound.
No kernel may reach another device: no remote copies, remote signals or barrier semaphores. Data moves between devices by JAX's collectives and lax.ppermute only.
A program may use at most 64 MiB of HBM per device.

v0:
```python
import jax
import jax.numpy as jnp
from jax import lax
from jax.sharding import PartitionSpec as P


def with_halo(block, sides, width, periodic):
    for axis, dim in sides:
        count = lax.axis_size(axis)
        forward = [(i, i + 1) for i in range(count - 1)]
        if periodic:
            forward.append((count - 1, 0))
        backward = [(target, source) for source, target in forward]
        low = lax.ppermute(
            lax.slice_in_dim(block, block.shape[dim] - width, None, axis=dim), axis, forward
        )
        high = lax.ppermute(lax.slice_in_dim(block, 0, width, axis=dim), axis, backward)
        block = jnp.concatenate([low, block, high], axis=dim)
    return block


def silu_slope(pre):
    sigma = jax.nn.sigmoid(pre)
    return sigma * (1.0 + pre * (1.0 - sigma))


def body(feats, cotangent, tiles, tile_src, tile_dst, weights, mask, counts):
    rows = feats.shape[2]
    width = feats.shape[3]
    block = tiles.shape[3]
    own_blocks = rows // block
    halves = lax.axis_size("half")
    region_blocks = own_blocks * halves
    slots = own_blocks + 4
    layers = weights.shape[0]
    grid = mask.shape[1]
    side = width // grid
    tile_set = tiles[0, 0]
    sources_of = tile_src[0, 0]
    targets = tile_dst[0, 0]
    first_row = lax.axis_index("half") * rows
    live = (first_row + jnp.arange(rows, dtype=jnp.int32) < counts[0, 0]).astype(jnp.float32)[
        :, None
    ]
    eta_here = lax.axis_index("eta")
    lower_eta = (eta_here > 0).astype(jnp.bfloat16)
    upper_eta = (eta_here < lax.axis_size("eta") - 1).astype(jnp.bfloat16)
    mask_full = (
        jnp.broadcast_to(mask[:, :, None, :, None], (layers, grid, side, grid, side))
        .reshape(layers, width, width)
        .astype(jnp.float32)
    )
    masked = (weights.astype(jnp.float32) * mask_full).astype(jnp.bfloat16)
    block_ids = jnp.arange(region_blocks, dtype=jnp.int32)
    slot_ids = jnp.arange(slots, dtype=jnp.int32)
    state = feats[0, 0]
    inputs = []
    pres = []
    for layer in range(layers):
        edge = state[:block][None, None]
        padded = with_halo(edge, (("phi", 0), ("eta", 1)), 1, True)
        rims = jnp.stack(
            [padded[0, 1], padded[2, 1], padded[1, 0] * lower_eta, padded[1, 2] * upper_eta]
        )
        messages_picked = jnp.take(
            jnp.concatenate([state.reshape(own_blocks, block, width), rims], axis=0),
            sources_of,
            axis=0,
        )
        messages_parts = jnp.einsum(
            "tij,tjd->tid", tile_set, messages_picked, preferred_element_type=jnp.float32
        )
        messages_onehot = (targets[None, :] == block_ids[:, None]).astype(jnp.float32)
        messages_total = jnp.einsum(
            "bt,tid->bid", messages_onehot, messages_parts, precision=lax.Precision.HIGHEST
        )
        region = messages_total.reshape(region_blocks * block, width)
        gathered = lax.psum_scatter(
            region.astype(jnp.bfloat16), "half", scatter_dimension=0, tiled=True
        ).astype(jnp.float32)
        hfloat = state.astype(jnp.float32)
        mixed = (hfloat + gathered).astype(jnp.bfloat16)
        pre = jnp.dot(mixed, masked[layer], preferred_element_type=jnp.float32)
        state = (live * (hfloat + jax.nn.silu(pre))).astype(jnp.bfloat16)
        inputs.append(mixed)
        pres.append(pre)
    upstream = cotangent[0, 0].astype(jnp.float32)
    partials = [None] * layers
    for layer in reversed(range(layers)):
        delta = (upstream * live * silu_slope(pres[layer])).astype(jnp.bfloat16)
        partials[layer] = (
            jnp.einsum("rd,re->de", inputs[layer], delta, preferred_element_type=jnp.float32)
            * mask_full[layer]
        )
        if layer > 0:
            back = jnp.einsum(
                "re,de->rd", delta, masked[layer], preferred_element_type=jnp.float32
            ).astype(jnp.bfloat16)
            whole = lax.all_gather(back, "half", axis=0, tiled=True)
            valid = (targets >= 0).astype(jnp.bfloat16)
            picked = (
                jnp.take(
                    whole.reshape(region_blocks, block, width), jnp.maximum(targets, 0), axis=0
                )
                * valid[:, None, None]
            )
            parts = jnp.einsum("tji,tjd->tid", tile_set, picked, preferred_element_type=jnp.float32)
            onehot = (sources_of[None, :] == slot_ids[:, None]).astype(jnp.float32)
            total = jnp.einsum("st,tid->sid", onehot, parts, precision=lax.Precision.HIGHEST)
            returned_phi = with_halo(
                total[own_blocks : own_blocks + 2].astype(jnp.bfloat16), (("phi", 0),), 1, True
            ).astype(jnp.float32)
            returned_eta = with_halo(
                total[own_blocks + 2 :].astype(jnp.bfloat16), (("eta", 0),), 1, False
            ).astype(jnp.float32)
            extra = returned_phi[0] + returned_phi[3] + returned_eta[0] + returned_eta[3]
            own = total[:own_blocks].reshape(rows, width)
            own = jnp.concatenate([own[:block] + extra, own[block:]], axis=0)
            upstream = live * upstream + back.astype(jnp.float32) + own
    stacked = jnp.stack(partials)
    shares = lax.psum_scatter(stacked.astype(jnp.bfloat16), "phi", scatter_dimension=1, tiled=True)
    result = lax.psum(shares, ("eta", "half")).astype(jnp.float32)
    return (state[None, None], result)


def solution(mesh):
    in_specs = (
        P(("group", "phi"), "eta", "half", None),
        P(("group", "phi"), "eta", "half", None),
        P(("group", "phi"), "eta", "half", None, None),
        P(("group", "phi"), "eta", "half"),
        P(("group", "phi"), "eta", "half"),
        P(),
        P(),
        P(("group", "phi"), "eta"),
    )
    out_specs = (P(("group", "phi"), "eta", "half", None), P("group", "phi", None))
    return jax.shard_map(body, mesh=mesh, in_specs=in_specs, out_specs=out_specs, check_vma=False)
```

profile of v0, /device:TPU:0, one launch (start us, length us, event | category | flops | bytes accessed | tf_op | source)
XLA Modules:
  0.0 213.0 jit_solution(10340029275667400948)
XLA Ops:
  7.2 1.0 slice.89
  8.2 3.1 %collective-permute-start = (bf16[1,1,128,512]{3,2,1,0:T(8,128)(2,1)S(1)}, bf16[1,1,128,512]{3,2,1,0:T(8,128)(2,1)S(1)}, u32[]{:S(2)}, u32[]{:S(2)}) collective-permute-start(bf16[1,1,128,512]{3,2,1,0:T(8,128)(2,1)S(1)} %slice.89), channel_id=1, source_target_pairs={{0,4},{4,8},{8,12},{12,0},{1,5},{5,9},{9,13},{13,1},{2,6},{6,10},{... | collective-permute-start | bytes 393224 | tf_op jit(solution)/shard_map/ppermute | solution.py:14
  11.3 2.1 collective-permute-start.1
  13.4 0.7 compare_select_fusion
  14.0 0.7 compare_and_fusion
  14.7 1.0 constant_dynamic-update-slice_fusion
  15.7 1.9 collective-permute-done
  17.6 1.4 collective-permute-done.1
  19.1 1.6 collective-permute-start.2
  20.6 0.5 collective-permute-start.3
  21.2 10.0 %collective-permute-done.2 = bf16[3,1,128,512]{3,2,1,0:T(8,128)(2,1)S(1)} collective-permute-done((bf16[3,1,128,512]{3,2,1,0:T(8,128)(2,1)S(1)}, bf16[3,1,128,512]{3,2,1,0:T(8,128)(2,1)S(1)}, u32[]{:S(2)}, u32[]{:S(2)}) %collective-permute-start.2) | collective-permute-done | bytes 393248 | tf_op jit(solution)/shard_map/ppermute | solution.py:14
  31.2 6.8 %collective-permute-done.3 = bf16[3,1,128,512]{3,2,1,0:T(8,128)(2,1)S(1)} collective-permute-done((bf16[3,1,128,512]{3,2,1,0:T(8,128)(2,1)S(1)}, bf16[3,1,128,512]{3,2,1,0:T(8,128)(2,1)S(1)}, u32[]{:S(2)}, u32[]{:S(2)}) %collective-permute-start.3) | collective-permute-done | bytes 393248 | tf_op jit(solution)/shard_map/ppermute | solution.py:17
  38.0 1.9 gather_fusion.1
  39.9 2.1 fusion.8
  42.0 3.5 %copy.19 = f32[12,512,128]{1,0,2:T(8,128)} copy(f32[12,512,128]{2,1,0:T(8,128)S(1)} %fusion.8) | data formatting | bytes 6291456 | tf_op jit(solution)/shard_map/tij,tjd->tid/dot_general | solution.py:70
  45.5 3.8 %fusion.16 = bf16[4,128,512]{2,0,1:T(4,128)(2,1)S(1)} fusion(f32[12,512,128]{1,0,2:T(8,128)} %copy.19, s32[12]{0:T(128)S(1)} %bitcast.122), kind=kOutput, calls=%fused_computation.22 | convolution fusion | flops 38010928 | bytes 3670064 | tf_op jit(solution)/shard_map/bt,tid->bid/dot_general | solution.py:74
  49.3 0.9 copy.14
  50.3 2.3 %broadcast_in_dim.41 = f32[2,8,64,8,64]{4,3,2,1,0:T(8,128)} broadcast(f32[2,8,8]{2,1,0:T(8,128)S(1)} %convert_element_type.115), dimensions={0,1,3} | broadcast | bytes 2097664 | tf_op jit(solution)/shard_map/broadcast_in_dim | solution.py:49
  52.6 3.5 %convert_element_type.116 = f32[2,512,512]{2,1,0:T(8,128)S(1)} reshape(f32[2,8,64,8,64]{4,3,2,1,0:T(8,128)} %broadcast_in_dim.41) | data formatting | bytes 4194304 | tf_op jit(solution)/shard_map/convert_element_type | solution.py:51
  56.8 0.6 compare_convert_fusion.1
  57.3 1.3 multiply_convert_fusion
  58.7 2.4 %fusion.35 = (bf16[256,512]{1,0:T(8,128)(2,1)S(1)}, f32[256,512]{1,0:T(8,128)}) fusion(bf16[1,1,256,512]{3,2,1,0:T(8,128)(2,1)} %param.10, f32[256]{0:T(256)} %compare_convert_fusion.1, bf16[2,512,512]{2,1,0:T(8,128)(2,1)} %multiply_convert_fusion, bf16[256,512]{1,0:T(8,128)(2,1)} %reduce-scatter.4.cloned.1.call-done), kind=kOutput, calls=%fused_computation.43 | convolution fusion | flops 135790592 | bytes 2098176 | tf_op jit(solution)/shard_map/dot_general | solution.py:83
  61.1 1.8 collective-permute-start.4
  62.9 2.1 collective-permute-start.5
  65.0 4.4 %collective-permute-done.4 = bf16[1,1,128,512]{3,2,1,0:T(8,128)(2,1)S(1)} collective-permute-done((bf16[1,1,128,512]{3,2,1,0:T(8,128)(2,1)S(1)}, bf16[1,1,128,512]{3,2,1,0:T(8,128)(2,1)S(1)}, u32[]{:S(2)}, u32[]{:S(2)}) %collective-permute-start.4) | collective-permute-done | bytes 131104 | tf_op jit(solution)/shard_map/ppermute | solution.py:14
  69.4 1.1 collective-permute-done.5
  70.5 1.5 collective-permute-start.6
  72.0 0.6 collective-permute-start.7
  72.6 10.0 %collective-permute-done.6 = bf16[3,1,128,512]{3,2,1,0:T(8,128)(2,1)S(1)} collective-permute-done((bf16[3,1,128,512]{3,2,1,0:T(8,128)(2,1)S(1)}, bf16[3,1,128,512]{3,2,1,0:T(8,128)(2,1)S(1)}, u32[]{:S(2)}, u32[]{:S(2)}) %collective-permute-start.6) | collective-permute-done | bytes 393248 | tf_op jit(solution)/shard_map/ppermute | solution.py:14
  82.7 6.9 %collective-permute-done.7 = bf16[3,1,128,512]{3,2,1,0:T(8,128)(2,1)S(1)} collective-permute-done((bf16[3,1,128,512]{3,2,1,0:T(8,128)(2,1)S(1)}, bf16[3,1,128,512]{3,2,1,0:T(8,128)(2,1)S(1)}, u32[]{:S(2)}, u32[]{:S(2)}) %collective-permute-start.7) | collective-permute-done | bytes 393248 | tf_op jit(solution)/shard_map/ppermute | solution.py:17
  89.6 1.9 gather_fusion.2
  91.5 2.1 fusion.6
  93.6 3.5 %copy.20 = f32[12,512,128]{1,0,2:T(8,128)} copy(f32[12,512,128]{2,1,0:T(8,128)S(1)} %fusion.6) | data formatting | bytes 6291456 | tf_op jit(solution)/shard_map/tij,tjd->tid/dot_general | solution.py:70
  97.1 3.8 %fusion.19 = bf16[4,128,512]{2,0,1:T(4,128)(2,1)S(1)} fusion(f32[12,512,128]{1,0,2:T(8,128)} %copy.20, s32[12]{0:T(128)S(1)} %bitcast.123), kind=kOutput, calls=%fused_computation.23 | convolution fusion | flops 38010928 | bytes 3670064 | tf_op jit(solution)/shard_map/bt,tid->bid/dot_general | solution.py:74
  100.9 0.9 copy.15
  101.8 0.0 reduce-scatter.8.cloned.1.call-start
  101.8 0.2 broadcast_in_dim.46
  102.0 1.5 squeeze.38
  103.5 0.2 broadcast_in_dim.47
  103.8 1.5 squeeze.39
  105.3 4.0 %reduce-scatter.6.cloned.1.call-done = bf16[256,512]{1,0:T(8,128)(2,1)} async-done(((bf16[512,512]{1,0:T(8,128)(2,1)}), bf16[256,512]{1,0:T(8,128)(2,1)}) %reduce-scatter.6.cloned.1.call-update) | async-done | bytes 262160 | tf_op jit(solution)/shard_map/reduce_scatter | solution.py:78
  109.3 2.4 %fusion.42 = (bf16[256,512]{1,0:T(8,128)(2,1)S(1)}, bf16[1,1,256,512]{3,2,1,0:T(8,128)(2,1)}) fusion(bf16[1,1,256,512]{3,2,1,0:T(8,128)(2,1)S(1)} %copy-done.19, f32[256]{0:T(256)S(1)} %copy-done.17, bf16[256,512]{1,0:T(8,128)(2,1)S(1)} %copy-done.3, bf16[2,512,512]{2,1,0:T(8,128)(2,1)} %multiply_convert_fusion, ...), kind=kOutput, calls=%fused_computation.54 | convolution fusion | flops 136839168 | bytes 2098176 | tf_op jit(solution)/shard_map/dot_general | solution.py:83
  111.7 0.3 convolution_convert_fusion
  112.0 0.7 copy-done.9
  112.7 2.3 %all_gather.3 = bf16[512,512]{1,0:T(8,128)(2,1)S(1)} all-gather(bf16[256,512]{1,0:T(8,128)(2,1)S(1)} %convolution_convert_fusion), channel_id=1, replica_groups=mesh['group'=2,'phi'=4,'eta'=2,'half'=2] {'half'}, dimensions={0}, use_global_device_ids=true | all-gather | bytes 786432 | tf_op jit(solution)/shard_map/all_gather | solution.py:99
  115.1 1.9 gather_fusion
  116.9 2.1 %fusion.10 = f32[12,512,128]{2,1,0:T(8,128)S(1)} fusion(bf16[12,128,512]{2,1,0:T(8,128)(2,1)} %gather_fusion, pred[12]{0:T(512)(128)(4,1)S(1)} %get-tuple-element.18, bf16[12]{0:T(256)(128)(2,1)S(1)} %get-tuple-element.17, bf16[1,1,12,128,128]{4,3,2,1,0:T(8,128)(2,1)S(1)} %copy-done), kind=kOutput, calls=%fused_computation.14 | convolution fusion | flops 202899456 | bytes 5111844 | tf_op jit(solution)/shard_map/tji,tjd->tid/dot_general | solution.py:107
  119.1 3.5 %copy.21 = f32[12,512,128]{1,0,2:T(8,128)} copy(f32[12,512,128]{2,1,0:T(8,128)S(1)} %fusion.10) | data formatting | bytes 6291456 | tf_op jit(solution)/shard_map/tji,tjd->tid/dot_general | solution.py:107
  122.6 3.7 %fusion = f32[6,128,512]{2,0,1:T(8,128)S(1)} fusion(f32[12,512,128]{1,0,2:T(8,128)} %copy.21, s32[12]{0:T(128)S(1)} %bitcast.124), kind=kOutput, calls=%fused_computation.3 | convolution fusion | flops 56623176 | bytes 4718640 | tf_op jit(solution)/shard_map/st,tid->sid/dot_general | solution.py:109
  126.3 0.9 fusion.80
  127.4 3.8 %collective-permute-start.10 = (bf16[1,128,512]{2,1,0:T(8,128)(2,1)S(1)}, bf16[1,128,512]{2,1,0:T(8,128)(2,1)S(1)}, u32[]{:S(2)}, u32[]{:S(2)}) collective-permute-start(bf16[1,128,512]{2,1,0:T(8,128)(2,1)S(1)} %get-tuple-element.9), channel_id=1, source_target_pairs={{0,2},{1,3},{4,6},{5,7},{8,10},{9,11},{12,14},{13,15},{16,18},{17,... | collective-permute-start | bytes 393224 | tf_op jit(solution)/shard_map/ppermute | solution.py:14
  131.1 1.3 collective-permute-start.11
  132.4 1.5 collective-permute-start.8
  134.0 2.3 %collective-permute-start.9 = (bf16[1,128,512]{2,1,0:T(8,128)(2,1)S(1)}, bf16[1,128,512]{2,1,0:T(8,128)(2,1)S(1)}, u32[]{:S(2)}, u32[]{:S(2)}) collective-permute-start(bf16[1,128,512]{2,1,0:T(8,128)(2,1)S(1)} %get-tuple-element.10), channel_id=1, source_target_pairs={{4,0},{8,4},{12,8},{0,12},{5,1},{9,5},{13,9},{1,13},{6,2},{10,6},{... | collective-permute-start | bytes 393224 | tf_op jit(solution)/shard_map/ppermute | solution.py:17
  136.3 0.3 fusion.24
  136.7 1.7 collective-permute-done.11
  138.5 2.2 %collective-permute-done.8 = bf16[1,128,512]{2,1,0:T(8,128)(2,1)S(1)} collective-permute-done((bf16[1,128,512]{2,1,0:T(8,128)(2,1)S(1)}, bf16[1,128,512]{2,1,0:T(8,128)(2,1)S(1)}, u32[]{:S(2)}, u32[]{:S(2)}) %collective-permute-start.8) | collective-permute-done | bytes 131104 | tf_op jit(solution)/shard_map/ppermute | solution.py:14
  140.7 1.3 collective-permute-done.9
  141.9 0.1 fusion.50
  142.1 0.6 fusion.25
  142.7 1.1 pad_maximum_fusion
  143.9 27.9 %reduce-scatter.8.cloned.1.call-done = bf16[2,128,512]{2,1,0:T(8,128)(2,1)} async-done(((bf16[2,512,512]{2,1,0:T(8,128)(2,1)}), bf16[2,128,512]{2,1,0:T(8,128)(2,1)}) %reduce-scatter.8.cloned.1.call-update) | async-done | bytes 262160 | tf_op jit(solution)/shard_map/reduce_scatter | solution.py:121
  171.8 32.9 %all-reduce.2.cloned.1.call-done = bf16[2,128,512]{2,1,0:T(8,128)(2,1)} async-done(((bf16[2,128,512]{2,1,0:T(8,128)(2,1)}), bf16[2,128,512]{2,1,0:T(8,128)(2,1)}) %all-reduce.2.cloned.1.call-update) | async-done | bytes 262160 | tf_op jit(solution)/shard_map/psum | solution.py:122
  204.6 1.8 convert_element_type.134
  (74 shorter events, 0.7 us)
Async XLA Ops:
  7.2 32.7 %copy-start = (bf16[1,1,12,128,128]{4,3,2,1,0:T(8,128)(2,1)S(1)}, bf16[1,1,12,128,128]{4,3,2,1,0:T(8,128)(2,1)}, u32[]{:S(2)}) copy-start(bf16[1,1,12,128,128]{4,3,2,1,0:T(8,128)(2,1)} %param.12) | copy-start | bytes 1179652
  7.2 51.5 %reduce-scatter.4.cloned.1.call-start = ((), (), s32[]{:S(2)}) async-start(), calls=%async_computation.3 | async-start | bytes 786432 | tf_op jit(solution)/shard_map/reduce_scatter | solution.py:78
  8.2 9.4 %collective-permute-start = (bf16[1,1,128,512]{3,2,1,0:T(8,128)(2,1)S(1)}, bf16[1,1,128,512]{3,2,1,0:T(8,128)(2,1)S(1)}, u32[]{:S(2)}, u32[]{:S(2)}) collective-permute-start(bf16[1,1,128,512]{3,2,1,0:T(8,128)(2,1)S(1)} %slice.89), channel_id=1, source_target_pairs={{0,4},{4,8},{8,12},{12,0},{1,5},{5,9},{9,13},{13,1},{2,6},{6,10},{... | collective-permute-start | bytes 393224 | tf_op jit(solution)/shard_map/ppermute | solution.py:14
  11.3 7.8 %collective-permute-start.1 = (bf16[1,1,128,512]{3,2,1,0:T(8,128)(2,1)S(1)}, bf16[1,1,128,512]{3,2,1,0:T(8,128)(2,1)S(1)}, u32[]{:S(2)}, u32[]{:S(2)}) collective-permute-start(bf16[1,1,128,512]{3,2,1,0:T(8,128)(2,1)S(1)} %slice.89), channel_id=1, source_target_pairs={{4,0},{8,4},{12,8},{0,12},{5,1},{9,5},{13,9},{1,13},{6,2},{10,6},{... | collective-permute-start | bytes 393224 | tf_op jit(solution)/shard_map/ppermute | solution.py:17
  14.7 25.2 %copy-start.16 = (pred[12]{0:T(512)(128)(4,1)}, pred[12]{0:T(512)(128)(4,1)S(1)}, u32[]{:S(2)}) copy-start(pred[12]{0:T(512)(128)(4,1)S(1)} %compare_and_fusion) | copy-start | bytes 40
  19.1 12.1 %collective-permute-start.2 = (bf16[3,1,128,512]{3,2,1,0:T(8,128)(2,1)S(1)}, bf16[3,1,128,512]{3,2,1,0:T(8,128)(2,1)S(1)}, u32[]{:S(2)}, u32[]{:S(2)}) collective-permute-start(bf16[3,1,128,512]{3,2,1,0:T(8,128)(2,1)S(1)} %pad_maximum_fusion.1), channel_id=1, source_target_pairs={{0,2},{2,0},{1,3},{3,1},{4,6},{6,4},{5,7},{7,5},{8,10},{10,8},{9,1... | collective-permute-start | bytes 1179656 | tf_op jit(solution)/shard_map/ppermute | solution.py:14
  20.6 17.4 %collective-permute-start.3 = (bf16[3,1,128,512]{3,2,1,0:T(8,128)(2,1)S(1)}, bf16[3,1,128,512]{3,2,1,0:T(8,128)(2,1)S(1)}, u32[]{:S(2)}, u32[]{:S(2)}) collective-permute-start(bf16[3,1,128,512]{3,2,1,0:T(8,128)(2,1)S(1)} %pad_maximum_fusion.1), channel_id=1, source_target_pairs={{2,0},{0,2},{3,1},{1,3},{6,4},{4,6},{7,5},{5,7},{10,8},{8,10},{11,... | collective-permute-start | bytes 1179656 | tf_op jit(solution)/shard_map/ppermute | solution.py:17
  42.0 3.5 %copy-start.15 = (s32[1,1,12]{2,1,0:T(1,128)S(1)}, s32[1,1,12]{2,1,0:T(1,128)}, u32[]{:S(2)}) copy-start(s32[1,1,12]{2,1,0:T(1,128)} %param.14) | copy-start | bytes 148
  49.3 1.0 copy-start.14
  50.2 59.1 %reduce-scatter.6.cloned.1.call-start = ((), (), s32[]{:S(2)}) async-start(), calls=%async_computation.4 | async-start | bytes 786432 | tf_op jit(solution)/shard_map/reduce_scatter | solution.py:78
  52.6 4.7 %copy-start.6 = (bf16[2,512,512]{2,1,0:T(8,128)(2,1)S(1)}, bf16[2,512,512]{2,1,0:T(8,128)(2,1)}, u32[]{:S(2)}) copy-start(bf16[2,512,512]{2,1,0:T(8,128)(2,1)} %param.15) | copy-start | bytes 3145732
  61.1 21.6 %copy-start.2 = (bf16[256,512]{1,0:T(8,128)(2,1)}, bf16[256,512]{1,0:T(8,128)(2,1)S(1)}, u32[]{:S(2)}) copy-start(bf16[256,512]{1,0:T(8,128)(2,1)S(1)} %get-tuple-element.19) | copy-start | bytes 786436
  61.1 8.3 %collective-permute-start.4 = (bf16[1,1,128,512]{3,2,1,0:T(8,128)(2,1)S(1)}, bf16[1,1,128,512]{3,2,1,0:T(8,128)(2,1)S(1)}, u32[]{:S(2)}, u32[]{:S(2)}) collective-permute-start(bf16[1,1,128,512]{3,2,1,0:T(8,128)(2,1)S(1)} %slice_bitcast_fusion.6), channel_id=1, source_target_pairs={{0,4},{4,8},{8,12},{12,0},{1,5},{5,9},{9,13},{13,1},{2,6},{6,10},{... | collective-permute-start | bytes 393224 | tf_op jit(solution)/shard_map/ppermute | solution.py:14
  62.9 7.6 %collective-permute-start.5 = (bf16[1,1,128,512]{3,2,1,0:T(8,128)(2,1)S(1)}, bf16[1,1,128,512]{3,2,1,0:T(8,128)(2,1)S(1)}, u32[]{:S(2)}, u32[]{:S(2)}) collective-permute-start(bf16[1,1,128,512]{3,2,1,0:T(8,128)(2,1)S(1)} %slice_bitcast_fusion.6), channel_id=1, source_target_pairs={{4,0},{8,4},{12,8},{0,12},{5,1},{9,5},{13,9},{1,13},{6,2},{10,6},{... | collective-permute-start | bytes 393224 | tf_op jit(solution)/shard_map/ppermute | solution.py:17
  70.5 12.1 %collective-permute-start.6 = (bf16[3,1,128,512]{3,2,1,0:T(8,128)(2,1)S(1)}, bf16[3,1,128,512]{3,2,1,0:T(8,128)(2,1)S(1)}, u32[]{:S(2)}, u32[]{:S(2)}) collective-permute-start(bf16[3,1,128,512]{3,2,1,0:T(8,128)(2,1)S(1)} %pad_maximum_fusion.2), channel_id=1, source_target_pairs={{0,2},{2,0},{1,3},{3,1},{4,6},{6,4},{5,7},{7,5},{8,10},{10,8},{9,1... | collective-permute-start | bytes 1179656 | tf_op jit(solution)/shard_map/ppermute | solution.py:14
  72.0 17.5 %collective-permute-start.7 = (bf16[3,1,128,512]{3,2,1,0:T(8,128)(2,1)S(1)}, bf16[3,1,128,512]{3,2,1,0:T(8,128)(2,1)S(1)}, u32[]{:S(2)}, u32[]{:S(2)}) collective-permute-start(bf16[3,1,128,512]{3,2,1,0:T(8,128)(2,1)S(1)} %pad_maximum_fusion.2), channel_id=1, source_target_pairs={{2,0},{0,2},{3,1},{1,3},{6,4},{4,6},{7,5},{5,7},{10,8},{8,10},{11,... | collective-permute-start | bytes 1179656 | tf_op jit(solution)/shard_map/ppermute | solution.py:17
  101.8 70.0 %reduce-scatter.8.cloned.1.call-start = ((), (), s32[]{:S(2)}) async-start(), calls=%async_computation.5 | async-start | bytes 1310720 | tf_op jit(solution)/shard_map/reduce_scatter | solution.py:121
  103.7 5.6 %copy-start.3 = (bf16[256,512]{1,0:T(8,128)(2,1)S(1)}, bf16[256,512]{1,0:T(8,128)(2,1)}, u32[]{:S(2)}) copy-start(bf16[256,512]{1,0:T(8,128)(2,1)} %copy-done.2) | copy-start | bytes 786436
  103.7 5.6 %copy-start.17 = (f32[256]{0:T(256)S(1)}, f32[256]{0:T(256)}, u32[]{:S(2)}) copy-start(f32[256]{0:T(256)} %compare_convert_fusion.1) | copy-start | bytes 3076
  103.7 5.6 %copy-start.19 = (bf16[1,1,256,512]{3,2,1,0:T(8,128)(2,1)S(1)}, bf16[1,1,256,512]{3,2,1,0:T(8,128)(2,1)}, u32[]{:S(2)}) copy-start(bf16[1,1,256,512]{3,2,1,0:T(8,128)(2,1)} %param.11) | copy-start | bytes 786436
  105.2 6.4 %copy-start.7 = (bf16[2,512,512]{2,1,0:T(8,128)(2,1)S(1)}, bf16[2,512,512]{2,1,0:T(8,128)(2,1)}, u32[]{:S(2)}) copy-start(bf16[2,512,512]{2,1,0:T(8,128)(2,1)} %multiply_convert_fusion) | copy-start | bytes 3145732
  111.7 5.3 %copy-start.12 = (bf16[256,512]{1,0:T(8,128)(2,1)}, bf16[256,512]{1,0:T(8,128)(2,1)S(1)}, u32[]{:S(2)}) copy-start(bf16[256,512]{1,0:T(8,128)(2,1)S(1)} %get-tuple-element.13) | copy-start | bytes 786436
  112.0 0.7 copy-start.9
  119.1 3.5 %copy-start.18 = (s32[1,1,12]{2,1,0:T(1,128)S(1)}, s32[1,1,12]{2,1,0:T(1,128)}, u32[]{:S(2)}) copy-start(s32[1,1,12]{2,1,0:T(1,128)} %param.13) | copy-start | bytes 148
  127.3 9.1 %copy-start.1 = (f32[512,512]{1,0:T(8,128)S(1)}, f32[512,512]{1,0:T(8,128)}, u32[]{:S(2)}) copy-start(f32[512,512]{1,0:T(8,128)} %squeeze.39) | copy-start | bytes 3145732
  127.3 9.1 %copy-start.4 = (bf16[256,512]{1,0:T(8,128)(2,1)S(1)}, bf16[256,512]{1,0:T(8,128)(2,1)}, u32[]{:S(2)}) copy-start(bf16[256,512]{1,0:T(8,128)(2,1)} %copy-done.2) | copy-start | bytes 786436
  127.3 9.1 %copy-start.11 = (bf16[256,512]{1,0:T(8,128)(2,1)S(1)}, bf16[256,512]{1,0:T(8,128)(2,1)}, u32[]{:S(2)}) copy-start(bf16[256,512]{1,0:T(8,128)(2,1)} %reduce-scatter.6.cloned.1.call-done) | copy-start | bytes 786436
  127.3 9.0 %copy-start.13 = (bf16[256,512]{1,0:T(8,128)(2,1)S(1)}, bf16[256,512]{1,0:T(8,128)(2,1)}, u32[]{:S(2)}) copy-start(bf16[256,512]{1,0:T(8,128)(2,1)} %copy-done.12) | copy-start | bytes 786436
  127.4 9.4 %collective-permute-start.10 = (bf16[1,128,512]{2,1,0:T(8,128)(2,1)S(1)}, bf16[1,128,512]{2,1,0:T(8,128)(2,1)S(1)}, u32[]{:S(2)}, u32[]{:S(2)}) collective-permute-start(bf16[1,128,512]{2,1,0:T(8,128)(2,1)S(1)} %get-tuple-element.9), channel_id=1, source_target_pairs={{0,2},{1,3},{4,6},{5,7},{8,10},{9,11},{12,14},{13,15},{16,18},{17,... | collective-permute-start | bytes 393224 | tf_op jit(solution)/shard_map/ppermute | solution.py:14
  131.1 7.3 %collective-permute-start.11 = (bf16[1,128,512]{2,1,0:T(8,128)(2,1)S(1)}, bf16[1,128,512]{2,1,0:T(8,128)(2,1)S(1)}, u32[]{:S(2)}, u32[]{:S(2)}) collective-permute-start(bf16[1,128,512]{2,1,0:T(8,128)(2,1)S(1)} %get-tuple-element.8), channel_id=1, source_target_pairs={{2,0},{3,1},{6,4},{7,5},{10,8},{11,9},{14,12},{15,13},{18,16},{19,... | collective-permute-start | bytes 393224 | tf_op jit(solution)/shard_map/ppermute | solution.py:17
  132.4 8.2 %collective-permute-start.8 = (bf16[1,128,512]{2,1,0:T(8,128)(2,1)S(1)}, bf16[1,128,512]{2,1,0:T(8,128)(2,1)S(1)}, u32[]{:S(2)}, u32[]{:S(2)}) collective-permute-start(bf16[1,128,512]{2,1,0:T(8,128)(2,1)S(1)} %get-tuple-element.7), channel_id=1, source_target_pairs={{0,4},{4,8},{8,12},{12,0},{1,5},{5,9},{9,13},{13,1},{2,6},{6,10},{... | collective-permute-start | bytes 393224 | tf_op jit(solution)/shard_map/ppermute | solution.py:14
  134.0 8.0 %collective-permute-start.9 = (bf16[1,128,512]{2,1,0:T(8,128)(2,1)S(1)}, bf16[1,128,512]{2,1,0:T(8,128)(2,1)S(1)}, u32[]{:S(2)}, u32[]{:S(2)}) collective-permute-start(bf16[1,128,512]{2,1,0:T(8,128)(2,1)S(1)} %get-tuple-element.10), channel_id=1, source_target_pairs={{4,0},{8,4},{12,8},{0,12},{5,1},{9,5},{13,9},{1,13},{6,2},{10,6},{... | collective-permute-start | bytes 393224 | tf_op jit(solution)/shard_map/ppermute | solution.py:17
  136.3 5.7 %copy-start.22 = (f32[256,512]{1,0:T(8,128)S(1)}, f32[256,512]{1,0:T(8,128)}, u32[]{:S(2)}) copy-start(f32[256,512]{1,0:T(8,128)} %get-tuple-element.20) | copy-start | bytes 1572868
  136.7 5.4 %copy-start.5 = (f32[512,512]{1,0:T(8,128)S(1)}, f32[512,512]{1,0:T(8,128)}, u32[]{:S(2)}) copy-start(f32[512,512]{1,0:T(8,128)} %squeeze.38) | copy-start | bytes 3145732
  136.7 5.4 %copy-start.8 = (bf16[1,1,256,512]{3,2,1,0:T(8,128)(2,1)S(1)}, bf16[1,1,256,512]{3,2,1,0:T(8,128)(2,1)}, u32[]{:S(2)}) copy-start(bf16[1,1,256,512]{3,2,1,0:T(8,128)(2,1)} %param.10) | copy-start | bytes 786436
  136.7 5.4 %copy-start.10 = (bf16[256,512]{1,0:T(8,128)(2,1)S(1)}, bf16[256,512]{1,0:T(8,128)(2,1)}, u32[]{:S(2)}) copy-start(bf16[256,512]{1,0:T(8,128)(2,1)} %copy-done.9) | copy-start | bytes 786436
  136.7 5.4 %copy-start.20 = (bf16[1,1,256,512]{3,2,1,0:T(8,128)(2,1)S(1)}, bf16[1,1,256,512]{3,2,1,0:T(8,128)(2,1)}, u32[]{:S(2)}) copy-start(bf16[1,1,256,512]{3,2,1,0:T(8,128)(2,1)} %param.11) | copy-start | bytes 786436
  136.7 5.4 %copy-start.21 = (bf16[256,512]{1,0:T(8,128)(2,1)S(1)}, bf16[256,512]{1,0:T(8,128)(2,1)}, u32[]{:S(2)}) copy-start(bf16[256,512]{1,0:T(8,128)(2,1)} %reduce-scatter.4.cloned.1.call-done) | copy-start | bytes 786436
  143.8 60.8 %all-reduce.2.cloned.1.call-start = ((), (), s32[]{:S(2)}) async-start(), calls=%async_computation.6 | async-start | bytes 524288 | tf_op jit(solution)/shard_map/psum | solution.py:122
Sparse Core Ops, SparseCore 0:
  50.3 7.6 reduce-scatter.3
  101.9 7.3 reduce-scatter.5
  143.9 27.7 reduce-scatter.7
  174.0 30.5 all-reduce.1
where the time goes:
time: 214 us; the launch traced here: 213 us
  waiting for transfers between devices  113 us (53%)
  local copies, waits for them, and re-layouts  29.8 us (14%)
  matrix products  23.7 us (11%)
  starting transfers between devices  22.3 us (10%)
  between operations  14.9 us (7%)
  other arithmetic  7.39 us (3%)
  blocking collectives  2.35 us (1%)
    psum x1, waiting for transfers between devices, body(): result = lax.psum(shares, ('eta', 'half')).astype(jnp.float32)  32.9 us
    ppermute x6, waiting for transfers between devices, with_halo(): lax.ppermute(lax.slice_in_dim(block, block.shape[dim] - width, None, axis...  28.5 us
    reduce_scatter x1, waiting for transfers between devices, body(): lax.psum_scatter(stacked.astype(jnp.bfloat16), 'phi', scatter_dimension=1...  27.9 us
    ppermute x6, waiting for transfers between devices, with_halo(): lax.ppermute(lax.slice_in_dim(block, 0, width, axis=dim), axis, backward)  19.2 us
    ppermute x6, starting transfers between devices, with_halo(): lax.ppermute(lax.slice_in_dim(block, block.shape[dim] - width, None, axis...  13.3 us
    ppermute x6, starting transfers between devices, with_halo(): lax.ppermute(lax.slice_in_dim(block, 0, width, axis=dim), axis, backward)  8.89 us
    dot_general x2, matrix products, body(): jnp.einsum('bt,tid->bid', messages_onehot, messages_parts, precision=lax....  7.58 us
    dot_general x2, local copies, waits for them, and re-layouts, body(): jnp.einsum('tij,tjd->tid', tile_set, messages_picked, preferred_element_t...  6.92 us
  transfers between devices with their start and end apart: 16, of which 14 were waited for; matrix products, arithmetic and copies ran while one was open for 7% of the time, Pallas kernels for 0%

commit v1 on v0

v1 whole, which is shorter than its diff:
```python
import functools

import jax
import jax.numpy as jnp
from jax import lax
from jax.experimental import pallas as pl
from jax.experimental.pallas import tpu as pltpu
from jax.sharding import PartitionSpec as P

BF16 = jnp.bfloat16
F32 = jnp.float32
VMEM = pl.BlockSpec(memory_space=pltpu.VMEM)
SMEM = pl.BlockSpec(memory_space=pltpu.SMEM)


def call(kernel, ins, outs, scratch=(), flops=0, name=None):
    moved = sum(a.size * a.dtype.itemsize for a in ins)
    moved += sum(a.size * a.dtype.itemsize for a in outs)
    return pl.pallas_call(
        kernel,
        out_shape=outs,
        in_specs=[SMEM if a.dtype == jnp.int32 and a.ndim == 1 else VMEM for a in ins],
        out_specs=[VMEM] * len(outs),
        scratch_shapes=list(scratch),
        compiler_params=pltpu.CompilerParams(vmem_limit_bytes=32 << 20),
        cost_estimate=pl.CostEstimate(flops=flops, bytes_accessed=moved, transcendentals=0),
        name=name,
    )(*ins)


def shaped(shape, dtype):
    return jax.ShapeDtypeStruct(shape, dtype)


def dot(a, b, contract=((1,), (0,))):
    return lax.dot_general(a, b, (contract, ((), ())), preferred_element_type=F32)


def ring(axis, step, periodic):
    count = lax.axis_size(axis)
    pairs = [(i, i + step) for i in range(count) if 0 <= i + step < count]
    if periodic:
        pairs = [(i, (i + step) % count) for i in range(count)]
    return pairs


def swap_half(value):
    return lax.ppermute(value, "half", [(0, 1), (1, 0)])


def to_neighbours(low_phi, high_phi, low_eta, high_eta):
    from_high = lax.ppermute(low_phi, "phi", ring("phi", -1, True))
    from_low = lax.ppermute(high_phi, "phi", ring("phi", 1, True))
    if lax.axis_size("eta") == 2:
        return [from_low, from_high, lax.ppermute(low_eta, "eta", [(0, 1), (1, 0)])]
    from_upper = lax.ppermute(low_eta, "eta", ring("eta", -1, False))
    from_lower = lax.ppermute(high_eta, "eta", ring("eta", 1, False))
    return [from_low, from_high, from_lower, from_upper]


def build_kernel(own, pair, src, dst, info, tiles, weights, mask, m_out, mt_out, w_out, acc, acct):
    block = tiles.shape[1]
    slots = tiles.shape[0]
    acc[...] = jnp.zeros_like(acc)
    acct[...] = jnp.zeros_like(acct)
    half = info[0]
    eta = info[1]
    for t in range(slots):
        source = src[t]
        target = dst[t]
        column = jnp.where(source > own + 2, own + 2, source) if pair else source
        live = target >= 0
        if pair:
            outside = ((source == own + 2) & (eta == 0)) | ((source == own + 3) & (eta == 1))
            live = live & jnp.logical_not(outside)
        row = jnp.where(target >= half * own, target - half * own, target - half * own + 2 * own)

        @pl.when(live)
        def _():
            tile = tiles[t].astype(F32)
            rows = pl.ds(pl.multiple_of(row * block, block), block)
            columns = pl.ds(pl.multiple_of(column * block, block), block)
            acc[rows, columns] += tile
            acct[columns, rows] += tile.T

    m_out[...] = acc[...].astype(BF16)
    mt_out[...] = acct[...].astype(BF16)
    layers, width, grid = weights.shape[0], weights.shape[1], mask.shape[1]
    side = width // grid
    spread = (
        lax.broadcasted_iota(jnp.int32, (width, grid), 0) // side
        == lax.broadcasted_iota(jnp.int32, (width, grid), 1)
    ).astype(F32)
    for layer in range(layers):
        keep = mask[layer].astype(F32)
        full = dot(dot(spread, keep), spread, ((1,), (1,)))
        w_out[layer] = (weights[layer].astype(F32) * full).astype(BF16)


def gather_kernel(count, matrix, *refs):
    sources, (own_out, other_out) = refs[:count], refs[count:]
    rows = own_out.shape[0]
    stacked = jnp.concatenate([r[...] for r in sources], axis=0)
    total = dot(matrix[...], stacked)
    own_out[...] = total[:rows]
    other_out[...] = total[rows:].astype(BF16)


def live_rows(info, rows, width):
    first = info[0] * rows
    row = first + lax.broadcasted_iota(jnp.int32, (rows, width), 0)
    return (row < info[2]).astype(F32)


def forward_kernel(info, state, own, other, weight, x_out, edge_out, rest_out, slope_out):
    rows, width = x_out.shape
    block = edge_out.shape[0]
    hfloat = state[...].astype(F32)
    mixed = (hfloat + own[...].astype(BF16).astype(F32) + other[...].astype(F32)).astype(BF16)
    x_out[...] = mixed
    pre = dot(mixed, weight[...])
    live = live_rows(info, rows, width)
    sigma = jax.nn.sigmoid(pre)
    new = (live * (hfloat + pre * sigma)).astype(BF16)
    edge_out[...] = new[:block]
    rest_out[...] = new[block:]
    slope_out[...] = live * sigma * (1.0 + pre * (1.0 - sigma))


def last_kernel(
    info, edge, rest, own, other, weight, cot, x_out, final_out, dz_out, dzo_out, dx_out
):
    rows, width = x_out.shape
    hfloat = jnp.concatenate([edge[...], rest[...]], axis=0).astype(F32)
    mixed = (hfloat + own[...].astype(BF16).astype(F32) + other[...].astype(F32)).astype(BF16)
    x_out[...] = mixed
    pre = dot(mixed, weight[...])
    live = live_rows(info, rows, width)
    sigma = jax.nn.sigmoid(pre)
    final_out[...] = (live * (hfloat + pre * sigma)).astype(BF16)
    delta = cot[...].astype(F32) * live * sigma * (1.0 + pre * (1.0 - sigma))
    delta = delta.astype(BF16)
    split_columns(info, delta, dz_out, dzo_out)
    dx_out[...] = dot(delta, weight[...], ((1,), (1,))).astype(BF16)


def split_columns(info, delta, mine_out, theirs_out):
    middle = delta.shape[1] // 2
    first = info[0] == 0
    left, right = delta[:, :middle], delta[:, middle:]
    mine_out[...] = jnp.where(first, left, right)
    theirs_out[...] = jnp.where(first, right, left)


def spread_kernel(mt, dx, dx_other, *outs):
    block = outs[0].shape[0]
    whole = jnp.concatenate([dx[...], dx_other[...]], axis=0)
    start = mt.shape[0] - block * len(outs)
    total = dot(mt[start:, :], whole).astype(BF16)
    for i, out in enumerate(outs):
        out[...] = total[i * block : (i + 1) * block]


def own_kernel(info, mt, dx, dx_other, cot, up_out):
    rows, width = up_out.shape
    whole = jnp.concatenate([dx[...], dx_other[...]], axis=0)
    live = live_rows(info, rows, width)
    up_out[...] = live * cot[...].astype(F32) + dx[...].astype(F32) + dot(mt[:rows, :], whole)


def delta_kernel(info, up, slope, *refs):
    arrived, (dz_out, dzo_out) = refs[:-2], refs[-2:]
    block = arrived[0].shape[0]
    extra = arrived[0][...].astype(F32)
    for r in arrived[1:]:
        extra = extra + r[...].astype(F32)
    upstream = jnp.concatenate([up[:block, :] + extra, up[block:, :]], axis=0)
    delta = (upstream * slope[...]).astype(BF16)
    split_columns(info, delta, dz_out, dzo_out)


def grad_kernel(parts, info, x, x_other, dz, dz_other, own_out, *refs):
    sends, total = refs[:-1], refs[-1]
    total[...] = dot(x[...], dz[...], ((0,), (0,))) + dot(x_other[...], dz_other[...], ((0,), (0,)))
    span = own_out.shape[0]
    place = info[3]
    for step in range(parts):
        target = lax.rem(place + step, parts)
        part = total[pl.ds(pl.multiple_of(target * span, span), span), :]
        if step == 0:
            own_out[...] = part
        else:
            sends[step - 1][...] = part.astype(BF16)


def sum_kernel(own, *refs):
    total = own[...].astype(F32)
    for r in refs[:-1]:
        total = total + r[...].astype(F32)
    refs[-1][...] = total.astype(BF16)


def finish_kernel(info, *refs):
    ins, out = refs[:-1], refs[-1]
    layers, rows, width = out.shape
    mask_rows = ins[-1]
    middle = width // 2
    first = info[0] == 0
    for layer in range(layers):
        mine, theirs = ins[2 * layer][...].astype(F32), ins[2 * layer + 1][...].astype(F32)
        keep = mask_rows[layer]
        out[layer, :, :middle] = jnp.where(first, mine, theirs) * keep[:, :middle]
        out[layer, :, middle:] = jnp.where(first, theirs, mine) * keep[:, middle:]


def phi_share(info, x, x_other, dz, dz_other):
    parts = lax.axis_size("phi")
    width, columns = x.shape[1], dz.shape[1]
    span = width // parts
    flops = 4 * x.shape[0] * width * columns
    if parts > 8:
        whole = call(
            functools.partial(grad_kernel, 1),
            (info, x, x_other, dz, dz_other),
            [shaped((width, columns), F32)],
            [pltpu.VMEM((width, columns), F32)],
            flops,
            "grad_whole",
        )[0]
        return lax.psum_scatter(whole.astype(BF16), "phi", scatter_dimension=0, tiled=True)
    own, *sends = call(
        functools.partial(grad_kernel, parts),
        (info, x, x_other, dz, dz_other),
        [shaped((span, columns), F32)] + [shaped((span, columns), BF16)] * (parts - 1),
        [pltpu.VMEM((width, columns), F32)],
        flops,
        "grad",
    )
    arrived = [
        lax.ppermute(sends[step - 1], "phi", ring("phi", step, True)) for step in range(1, parts)
    ]
    return call(
        sum_kernel, (own, *arrived), [shaped((span, columns), BF16)], name="phi_sum"
    )[0]


def eta_sum(share):
    if lax.axis_size("eta") == 2:
        arrived = [lax.ppermute(share, "eta", [(0, 1), (1, 0)])]
        return call(sum_kernel, (share, *arrived), [shaped(share.shape, BF16)], name="eta_sum")[0]
    gathered = lax.all_gather(share, "eta", axis=0)
    return jnp.sum(gathered.astype(F32), axis=0).astype(BF16)


def body(feats, cotangent, tiles, tile_src, tile_dst, weights, mask, counts):
    rows, width = feats.shape[2], feats.shape[3]
    block = tiles.shape[3]
    own = rows // block
    pair = lax.axis_size("eta") == 2
    rims = 3 if pair else 4
    layers, grid = weights.shape[0], mask.shape[1]
    side = width // grid
    info = jnp.stack(
        [lax.axis_index("half"), lax.axis_index("eta"), counts[0, 0], lax.axis_index("phi")]
    ).astype(jnp.int32)
    state = feats[0, 0]
    cot = cotangent[0, 0]
    height, depth = 2 * rows, rows + rims * block

    edge = state[:block]
    arrived = to_neighbours(edge, edge, edge, edge)
    matrix, matrix_t, masked = call(
        functools.partial(build_kernel, own, pair),
        (tile_src[0, 0], tile_dst[0, 0], info, tiles[0, 0], weights, mask),
        [shaped((height, depth), BF16), shaped((depth, height), BF16), shaped(weights.shape, BF16)],
        [pltpu.VMEM((height, depth), F32), pltpu.VMEM((depth, height), F32)],
        10_000_000,
        "build",
    )
    agg_flops = 2 * height * depth * width
    dense_flops = 2 * rows * width * width

    own_part, other_part = call(
        functools.partial(gather_kernel, 1 + rims),
        (matrix, state, *arrived),
        [shaped((rows, width), F32), shaped((rows, width), BF16)],
        flops=agg_flops,
        name="gather0",
    )
    received = swap_half(other_part)
    x0, edge, rest, slope0 = call(
        forward_kernel,
        (info, state, own_part, received, masked[0]),
        [
            shaped((rows, width), BF16),
            shaped((block, width), BF16),
            shaped((rows - block, width), BF16),
            shaped((rows, width), F32),
        ],
        flops=dense_flops,
        name="forward0",
    )
    arrived = to_neighbours(edge, edge, edge, edge)
    x0_other = swap_half(x0)
    own_part, other_part = call(
        functools.partial(gather_kernel, 2 + rims),
        (matrix, edge, rest, *arrived),
        [shaped((rows, width), F32), shaped((rows, width), BF16)],
        flops=agg_flops,
        name="gather1",
    )
    received = swap_half(other_part)
    x1, final, dz1, dz1_send, dx = call(
        last_kernel,
        (info, edge, rest, own_part, received, masked[1], cot),
        [
            shaped((rows, width), BF16),
            shaped((rows, width), BF16),
            shaped((rows, width // 2), BF16),
            shaped((rows, width // 2), BF16),
            shaped((rows, width), BF16),
        ],
        flops=2 * dense_flops,
        name="last",
    )
    dx_other = swap_half(dx)
    dz1_other = swap_half(dz1_send)
    x1_other = swap_half(x1)
    back = call(
        spread_kernel,
        (matrix_t, dx, dx_other),
        [shaped((block, width), BF16)] * rims,
        flops=2 * rims * block * height * width,
        name="spread",
    )
    if pair:
        arrived = to_neighbours(back[0], back[1], back[2], back[2])
    else:
        arrived = to_neighbours(*back)
    upstream = call(
        own_kernel,
        (info, matrix_t, dx, dx_other, cot),
        [shaped((rows, width), F32)],
        flops=2 * rows * height * width,
        name="own",
    )[0]
    share1 = phi_share(info, x1, x1_other, dz1, dz1_other)
    dz0, dz0_send = call(
        delta_kernel,
        (info, upstream, slope0, *arrived),
        [shaped((rows, width // 2), BF16), shaped((rows, width // 2), BF16)],
        name="delta",
    )
    dz0_other = swap_half(dz0_send)
    share0 = phi_share(info, x0, x0_other, dz0, dz0_other)
    total1 = eta_sum(share1)
    total0 = eta_sum(share0)
    other1 = swap_half(total1)
    other0 = swap_half(total0)

    span = width // lax.axis_size("phi")
    row_ids = (lax.axis_index("phi") * span + jnp.arange(span, dtype=jnp.int32)) // side
    chosen = jnp.take(mask, row_ids, axis=1)
    keep = jnp.broadcast_to(chosen[..., None], (layers, span, grid, side)).reshape(
        layers, span, width
    )
    result = call(
        finish_kernel,
        (info, total0, other0, total1, other1, keep.astype(F32)),
        [shaped((layers, span, width), F32)],
        name="finish",
    )[0]
    return final[None, None], result


def solution(mesh):
    in_specs = (
        P(("group", "phi"), "eta", "half", None),
        P(("group", "phi"), "eta", "half", None),
        P(("group", "phi"), "eta", "half", None, None),
        P(("group", "phi"), "eta", "half"),
        P(("group", "phi"), "eta", "half"),
        P(),
        P(),
        P(("group", "phi"), "eta"),
    )
    out_specs = (P(("group", "phi"), "eta", "half", None), P("group", "phi", None))
    return jax.shard_map(body, mesh=mesh, in_specs=in_specs, out_specs=out_specs, check_vma=False)
```

time: 214 us -> 65.7 us (0.31)
  waiting for transfers between devices: 113 us -> 20.6 us
  local copies, waits for them, and re-layouts: 29.8 us -> 4.93 us
  matrix products: 23.7 us -> 0 us
  between operations: 14.9 us -> 1.58 us
  Pallas kernels: 0 us -> 11.1 us
  other arithmetic: 7.39 us -> 0.2 us
  starting transfers between devices: 22.3 us -> 27.1 us
  blocking collectives: 2.35 us -> 0 us
    psum x1 -> x0, waiting for transfers between devices: 32.9 us -> none  [body(): result = lax.psum(shares, ('eta', 'half')).astype(jnp.float32)]
    reduce_scatter x3 -> x0, waiting for transfers between devices: 31.9 us -> none  [the longest x1 27.9 us: body(): lax.psum_scatter(stacked.astype(jnp.bfloat16), 'phi', scatter_dimension=1...]
    ppermute x12 -> x26, waiting for transfers between devices: 47.7 us -> 20.6 us  [the longest x3 6.81 us: to_neighbours(): from_low = lax.ppermute(high_phi, 'phi', ring('phi', 1, True))]
    dot_general x11 -> x0, matrix products: 23.7 us -> none  [the longest x2 7.58 us: body(): jnp.einsum('bt,tid->bid', messages_onehot, messages_parts, precision=lax....]
    pallas_call x0 -> x15, Pallas kernels: none -> 11.1 us  [call(): pl.pallas_call(kernel, out_shape=outs, in_specs=[SMEM if a.dtype == jnp.i...]
    dot_general x3 -> x0, local copies, waits for them, and re-layouts: 10.4 us -> none  [the longest x2 6.92 us: body(): jnp.einsum('tij,tjd->tid', tile_set, messages_picked, preferred_element_t...]
    convert_element_type x3 -> x2, local copies, waits for them, and re-layouts: 5.27 us -> 0.25 us  [body(): keep.astype(F32)]
    ppermute x12 -> x26, starting transfers between devices: 22.1 us -> 27.1 us  [the longest x6 8.94 us: phi_share(): lax.ppermute(sends[step - 1], 'phi', ring('phi', step, True))]
  transfers between devices with their start and end apart: 16 -> 26, of which waited for: 14 -> 12; matrix products, arithmetic and copies ran while one was open for 7% -> 2% of each run, Pallas kernels for 0% -> 8%
where the time goes in v1:
time: 65.7 us; the launch traced here: 65.5 us
  starting transfers between devices  27.1 us (41%)
  waiting for transfers between devices  20.6 us (31%)
  Pallas kernels  11.1 us (17%)
  local copies, waits for them, and re-layouts  4.93 us (8%)
  between operations  1.58 us (2%)
    pallas_call x15, Pallas kernels, call(): pl.pallas_call(kernel, out_shape=outs, in_specs=[SMEM if a.dtype == jnp.i...  11.1 us
    ppermute x6, starting transfers between devices, phi_share(): lax.ppermute(sends[step - 1], 'phi', ring('phi', step, True))  8.94 us
    ppermute x3, starting transfers between devices, to_neighbours(): from_high = lax.ppermute(low_phi, 'phi', ring('phi', -1, True))  8.54 us
    ppermute x3, waiting for transfers between devices, to_neighbours(): from_low = lax.ppermute(high_phi, 'phi', ring('phi', 1, True))  6.81 us
    ppermute x9, waiting for transfers between devices, swap_half(): return lax.ppermute(value, 'half', [(0, 1), (1, 0)])  5.2 us
    ppermute x3, starting transfers between devices, to_neighbours(): from_low = lax.ppermute(high_phi, 'phi', ring('phi', 1, True))  4.37 us
    ppermute x2, waiting for transfers between devices, eta_sum(): arrived = [lax.ppermute(share, 'eta', [(0, 1), (1, 0)])]  3.6 us
    ppermute x3, starting transfers between devices, to_neighbours(): return [from_low, from_high, lax.ppermute(low_eta, 'eta', [(0, 1), (1, 0)])]  3.51 us
  transfers between devices with their start and end apart: 26, of which 12 were waited for; matrix products, arithmetic and copies ran while one was open for 2% of the time, Pallas kernels for 8%

profile of v1, /device:TPU:0, one launch (start us, length us, event | category | flops | bytes accessed | tf_op | source)
XLA Modules:
  0.0 65.5 jit_solution(3466522887979457242)
XLA Ops:
  0.6 0.9 %slice_bitcast_fusion.2 = bf16[128,512]{1,0:T(8,128)(2,1)S(1)} fusion(bf16[1,1,256,512]{3,2,1,0:T(8,128)(2,1)} %param.8), kind=kLoop, calls=%fused_computation.4 | loop fusion | bytes 262144 | tf_op jit(solution)/shard_map/slice | solution.py:270
  1.5 3.1 %collective-permute-start = (bf16[128,512]{1,0:T(8,128)(2,1)S(1)}, bf16[128,512]{1,0:T(8,128)(2,1)S(1)}, u32[]{:S(2)}, u32[]{:S(2)}) collective-permute-start(bf16[128,512]{1,0:T(8,128)(2,1)S(1)} %slice_bitcast_fusion.2), channel_id=1, source_target_pairs={{0,4},{4,8},{8,12},{12,0},{1,5},{5,9},{9,13},{13,1},{2,6},{6,10},{... | collective-permute-start | bytes 393224 | tf_op jit(solution)/shard_map/ppermute | solution.py:53
  4.6 2.1 %collective-permute-start.1 = (bf16[128,512]{1,0:T(8,128)(2,1)S(1)}, bf16[128,512]{1,0:T(8,128)(2,1)S(1)}, u32[]{:S(2)}, u32[]{:S(2)}) collective-permute-start(bf16[128,512]{1,0:T(8,128)(2,1)S(1)} %slice_bitcast_fusion.2), channel_id=1, source_target_pairs={{0,12},{4,0},{8,4},{12,8},{1,13},{5,1},{9,5},{13,9},{2,14},{6,2},{... | collective-permute-start | bytes 393224 | tf_op jit(solution)/shard_map/ppermute | solution.py:52
  6.7 1.6 %collective-permute-start.2 = (bf16[128,512]{1,0:T(8,128)(2,1)S(1)}, bf16[128,512]{1,0:T(8,128)(2,1)S(1)}, u32[]{:S(2)}, u32[]{:S(2)}) collective-permute-start(bf16[128,512]{1,0:T(8,128)(2,1)S(1)} %slice_bitcast_fusion.2), channel_id=1, source_target_pairs={{0,2},{2,0},{1,3},{3,1},{4,6},{6,4},{5,7},{7,5},{8,10},{10,8},{9,1... | collective-permute-start | bytes 393224 | tf_op jit(solution)/shard_map/ppermute | solution.py:55
  9.0 0.0 copy-start
  9.0 0.1 pad_add_fusion.info
  9.1 0.6 copy-done
  9.7 0.0 copy-done.5
  9.8 0.0 copy-done.6
  9.8 1.2 %copy-done.2 = bf16[2,512,512]{2,1,0:T(8,128)(2,1)S(1)} copy-done((bf16[2,512,512]{2,1,0:T(8,128)(2,1)S(1)}, bf16[2,512,512]{2,1,0:T(8,128)(2,1)}, u32[]{:S(2)}) %copy-start.2) | copy-done | bytes 1048600
  11.0 1.0 %copy-done.4 = bf16[1,1,12,128,128]{4,3,2,1,0:T(8,128)(2,1)S(1)} copy-done((bf16[1,1,12,128,128]{4,3,2,1,0:T(8,128)(2,1)S(1)}, bf16[1,1,12,128,128]{4,3,2,1,0:T(8,128)(2,1)}, u32[]{:S(2)}) %copy-start.4) | copy-done | bytes 393240
  12.0 1.9 %build.1 = (bf16[512,640]{1,0:T(8,128)(2,1)S(1)}, bf16[640,512]{1,0:T(8,128)(2,1)S(1)}, bf16[2,512,512]{2,1,0:T(8,128)(2,1)S(1)}) custom-call(s32[12]{0:T(128)S(1)} %bitcast.27, s32[12]{0:T(128)S(1)} %bitcast.28, s32[4]{0:T(128)S(1)} %pad_add_fusion.info, bf16[12,128,128]{2,1,0:T(8,128)(2,1)S(1)} %bitcast.26, bf16[2,512,512]{2,1,0:T(8,128)(2,1)S(1)} %copy-done.2, ...), custom_call_target="tpu_custom_call" | custom-call | flops 10000000 | bytes 3801712 | tf_op jit(solution)/shard_map/build/pallas_call | solution.py:19
  13.9 0.0 collective-permute-done.1.refs_2_
  13.9 0.0 collective-permute-done.2.refs_3_
  13.9 0.6 gather0.1
  14.5 0.1 collective-permute-start.3
  14.6 0.1 slice_bitcast_fusion
  14.7 1.4 %collective-permute-done.3.other = bf16[256,512]{1,0:T(8,128)(2,1)S(1)} collective-permute-done((bf16[256,512]{1,0:T(8,128)(2,1)S(1)}, bf16[256,512]{1,0:T(8,128)(2,1)S(1)}, u32[]{:S(2)}, u32[]{:S(2)}) %collective-permute-start.3) | collective-permute-done | bytes 262176 | tf_op jit(solution)/shard_map/ppermute | solution.py:48
  16.1 1.0 %forward0.1 = (bf16[256,512]{1,0:T(8,128)(2,1)S(1)}, bf16[128,512]{1,0:T(8,128)(2,1)S(1)}, bf16[128,512]{1,0:T(8,128)(2,1)S(1)}, f32[256,512]{1,0:T(8,128)S(1)}) custom-call(s32[4]{0:T(128)S(1)} %pad_add_fusion.info, bf16[256,512]{1,0:T(8,128)(2,1)S(1)} %bitcast.23, f32[256,512]{1,0:T(8,128)S(1)} %get-tuple-element.32.own, ...), custom_call_target="tpu_custom_call" | custom-call | flops 134217728 | bytes 2621456 | tf_op jit(solution)/shard_map/forward0/pallas_call | solution.py:19
  17.1 0.1 collective-permute-start.4
  17.2 3.8 %collective-permute-start.5 = (bf16[128,512]{1,0:T(8,128)(2,1)S(1)}, bf16[128,512]{1,0:T(8,128)(2,1)S(1)}, u32[]{:S(2)}, u32[]{:S(2)}) collective-permute-start(bf16[128,512]{1,0:T(8,128)(2,1)S(1)} %get-tuple-element.35.refs_0_.edge), channel_id=1, source_target_pairs={{0,12},{4,0},{8,4},{12,8},{1,13},{5,1},{9,5},{13,9},{2,14},{6,2},{... | collective-permute-start | bytes 393224 | tf_op jit(solution)/shard_map/ppermute | solution.py:52
  21.0 0.9 %collective-permute-start.6 = (bf16[128,512]{1,0:T(8,128)(2,1)S(1)}, bf16[128,512]{1,0:T(8,128)(2,1)S(1)}, u32[]{:S(2)}, u32[]{:S(2)}) collective-permute-start(bf16[128,512]{1,0:T(8,128)(2,1)S(1)} %get-tuple-element.35.refs_0_.edge), channel_id=1, source_target_pairs={{0,2},{2,0},{1,3},{3,1},{4,6},{6,4},{5,7},{7,5},{8,10},{10,8},{9,1... | collective-permute-start | bytes 393224 | tf_op jit(solution)/shard_map/ppermute | solution.py:55
  21.9 3.4 %collective-permute-done.4.refs_2_ = bf16[128,512]{1,0:T(8,128)(2,1)S(1)} collective-permute-done((bf16[128,512]{1,0:T(8,128)(2,1)S(1)}, bf16[128,512]{1,0:T(8,128)(2,1)S(1)}, u32[]{:S(2)}, u32[]{:S(2)}) %collective-permute-start.4) | collective-permute-done | bytes 131104 | tf_op jit(solution)/shard_map/ppermute | solution.py:53
  25.4 0.2 collective-permute-done.5.refs_3_
  25.6 0.4 collective-permute-done.6.refs_4_
  26.0 0.6 gather1.1
  26.5 0.1 collective-permute-start.7
  26.6 1.5 %collective-permute-done.7.other = bf16[256,512]{1,0:T(8,128)(2,1)S(1)} collective-permute-done((bf16[256,512]{1,0:T(8,128)(2,1)S(1)}, bf16[256,512]{1,0:T(8,128)(2,1)S(1)}, u32[]{:S(2)}, u32[]{:S(2)}) %collective-permute-start.7) | collective-permute-done | bytes 262176 | tf_op jit(solution)/shard_map/ppermute | solution.py:48
  28.2 1.8 %last.1 = (bf16[256,512]{1,0:T(8,128)(2,1)S(1)}, bf16[256,512]{1,0:T(8,128)(2,1)}, bf16[256,256]{1,0:T(8,128)(2,1)S(1)}, bf16[256,256]{1,0:T(8,128)(2,1)S(1)}, bf16[256,512]{1,0:T(8,128)(2,1)S(1)}) custom-call(s32[4]{0:T(128)S(1)} %pad_add_fusion.info, bf16[128,512]{1,0:T(8,128)(2,1)S(1)} %get-tuple-element.35.refs_0_.edge, ...), custom_call_target="tpu_custom_call" | custom-call | flops 268435456 | bytes 2883600 | tf_op jit(solution)/shard_map/last/pallas_call | solution.py:19
  30.0 0.1 collective-permute-start.9
  30.1 1.4 %collective-permute-done.9.dx_other = bf16[256,512]{1,0:T(8,128)(2,1)S(1)} collective-permute-done((bf16[256,512]{1,0:T(8,128)(2,1)S(1)}, bf16[256,512]{1,0:T(8,128)(2,1)S(1)}, u32[]{:S(2)}, u32[]{:S(2)}) %collective-permute-start.9) | collective-permute-done | bytes 262176 | tf_op jit(solution)/shard_map/ppermute | solution.py:48
  31.5 0.4 spread.1
  31.9 1.2 %collective-permute-start.10 = (bf16[128,512]{1,0:T(8,128)(2,1)S(1)}, bf16[128,512]{1,0:T(8,128)(2,1)S(1)}, u32[]{:S(2)}, u32[]{:S(2)}) collective-permute-start(bf16[128,512]{1,0:T(8,128)(2,1)S(1)} %get-tuple-element.44), channel_id=1, source_target_pairs={{0,4},{4,8},{8,12},{12,0},{1,5},{5,9},{9,13},{13,1},{2,6},{6,10},{... | collective-permute-start | bytes 393224 | tf_op jit(solution)/shard_map/ppermute | solution.py:53
  33.1 2.6 %collective-permute-start.11 = (bf16[128,512]{1,0:T(8,128)(2,1)S(1)}, bf16[128,512]{1,0:T(8,128)(2,1)S(1)}, u32[]{:S(2)}, u32[]{:S(2)}) collective-permute-start(bf16[128,512]{1,0:T(8,128)(2,1)S(1)} %get-tuple-element.45), channel_id=1, source_target_pairs={{0,12},{4,0},{8,4},{12,8},{1,13},{5,1},{9,5},{13,9},{2,14},{6,2},{... | collective-permute-start | bytes 393224 | tf_op jit(solution)/shard_map/ppermute | solution.py:52
  35.8 0.9 %collective-permute-start.12 = (bf16[128,512]{1,0:T(8,128)(2,1)S(1)}, bf16[128,512]{1,0:T(8,128)(2,1)S(1)}, u32[]{:S(2)}, u32[]{:S(2)}) collective-permute-start(bf16[128,512]{1,0:T(8,128)(2,1)S(1)} %get-tuple-element.46), channel_id=1, source_target_pairs={{0,2},{2,0},{1,3},{3,1},{4,6},{6,4},{5,7},{7,5},{8,10},{10,8},{9,1... | collective-permute-start | bytes 393224 | tf_op jit(solution)/shard_map/ppermute | solution.py:55
  36.7 3.4 %collective-permute-done.10.refs_0_ = bf16[128,512]{1,0:T(8,128)(2,1)S(1)} collective-permute-done((bf16[128,512]{1,0:T(8,128)(2,1)S(1)}, bf16[128,512]{1,0:T(8,128)(2,1)S(1)}, u32[]{:S(2)}, u32[]{:S(2)}) %collective-permute-start.10) | collective-permute-done | bytes 131104 | tf_op jit(solution)/shard_map/ppermute | solution.py:53
  40.1 0.0 collective-permute-start.20
  40.1 0.8 %own.1.up = f32[256,512]{1,0:T(8,128)S(1)} custom-call(s32[4]{0:T(128)S(1)} %pad_add_fusion.info, bf16[640,512]{1,0:T(8,128)(2,1)S(1)} %get-tuple-element.41.mt, bf16[256,512]{1,0:T(8,128)(2,1)S(1)} %get-tuple-element.42.dx, bf16[256,512]{1,0:T(8,128)(2,1)S(1)} %collective-permute-done.9.dx_other, bf16[256,512]{1,0:T(8,128)(2,1)S(1)} %bitcast.25), custom_call_target="tpu_custom_call" | custom-call | flops 134217728 | bytes 1966096 | tf_op jit(solution)/shard_map/own/pallas_call | solution.py:19
  40.9 0.9 %collective-permute-done.11.refs_1_ = bf16[128,512]{1,0:T(8,128)(2,1)S(1)} collective-permute-done((bf16[128,512]{1,0:T(8,128)(2,1)S(1)}, bf16[128,512]{1,0:T(8,128)(2,1)S(1)}, u32[]{:S(2)}, u32[]{:S(2)}) %collective-permute-start.11) | collective-permute-done | bytes 131104 | tf_op jit(solution)/shard_map/ppermute | solution.py:52
  41.8 0.0 collective-permute-done.12.refs_2_
  41.8 0.6 delta.1
  42.5 0.1 collective-permute-start.13
  42.6 0.0 collective-permute-done.20.dz_other
  42.6 0.9 %grad.3 = (f32[128,256]{1,0:T(8,128)S(1)}, bf16[128,256]{1,0:T(8,128)(2,1)S(1)}, bf16[128,256]{1,0:T(8,128)(2,1)S(1)}, bf16[128,256]{1,0:T(8,128)(2,1)S(1)}) custom-call(s32[4]{0:T(128)S(1)} %pad_add_fusion.info, bf16[256,512]{1,0:T(8,128)(2,1)S(1)} %get-tuple-element.53.x, bf16[256,512]{1,0:T(8,128)(2,1)S(1)} %collective-permute-done.19.x_other, ...), custom_call_target="tpu_custom_call" | custom-call | flops 134217728 | bytes 1114128 | tf_op jit(solution)/shard_map/grad/pallas_call | solution.py:19
  43.6 0.9 %collective-permute-start.21 = (bf16[128,256]{1,0:T(8,128)(2,1)S(1)}, bf16[128,256]{1,0:T(8,128)(2,1)S(1)}, u32[]{:S(2)}, u32[]{:S(2)}) collective-permute-start(bf16[128,256]{1,0:T(8,128)(2,1)S(1)} %get-tuple-element.57), channel_id=1, source_target_pairs={{0,4},{4,8},{8,12},{12,0},{1,5},{5,9},{9,13},{13,1},{2,6},{6,10},{... | collective-permute-start | bytes 196616 | tf_op jit(solution)/shard_map/ppermute | solution.py:240
  44.5 1.4 %collective-permute-start.22 = (bf16[128,256]{1,0:T(8,128)(2,1)S(1)}, bf16[128,256]{1,0:T(8,128)(2,1)S(1)}, u32[]{:S(2)}, u32[]{:S(2)}) collective-permute-start(bf16[128,256]{1,0:T(8,128)(2,1)S(1)} %get-tuple-element.58), channel_id=1, source_target_pairs={{0,8},{4,12},{8,0},{12,4},{1,9},{5,13},{9,1},{13,5},{2,10},{6,14},... | collective-permute-start | bytes 196616 | tf_op jit(solution)/shard_map/ppermute | solution.py:240
  45.9 1.7 %collective-permute-start.23 = (bf16[128,256]{1,0:T(8,128)(2,1)S(1)}, bf16[128,256]{1,0:T(8,128)(2,1)S(1)}, u32[]{:S(2)}, u32[]{:S(2)}) collective-permute-start(bf16[128,256]{1,0:T(8,128)(2,1)S(1)} %get-tuple-element.59), channel_id=1, source_target_pairs={{0,12},{4,0},{8,4},{12,8},{1,13},{5,1},{9,5},{13,9},{2,14},{6,2},{... | collective-permute-start | bytes 196616 | tf_op jit(solution)/shard_map/ppermute | solution.py:240
  47.6 0.9 %grad.2 = (f32[128,256]{1,0:T(8,128)S(1)}, bf16[128,256]{1,0:T(8,128)(2,1)S(1)}, bf16[128,256]{1,0:T(8,128)(2,1)S(1)}, bf16[128,256]{1,0:T(8,128)(2,1)S(1)}) custom-call(s32[4]{0:T(128)S(1)} %pad_add_fusion.info, bf16[256,512]{1,0:T(8,128)(2,1)S(1)} %get-tuple-element.40.x, bf16[256,512]{1,0:T(8,128)(2,1)S(1)} %collective-permute-done.8.x_other, ...), custom_call_target="tpu_custom_call" | custom-call | flops 134217728 | bytes 1114128 | tf_op jit(solution)/shard_map/grad/pallas_call | solution.py:19
  48.5 0.6 collective-permute-start.14
  49.1 1.5 %collective-permute-start.15 = (bf16[128,256]{1,0:T(8,128)(2,1)S(1)}, bf16[128,256]{1,0:T(8,128)(2,1)S(1)}, u32[]{:S(2)}, u32[]{:S(2)}) collective-permute-start(bf16[128,256]{1,0:T(8,128)(2,1)S(1)} %get-tuple-element.51), channel_id=1, source_target_pairs={{0,8},{4,12},{8,0},{12,4},{1,9},{5,13},{9,1},{13,5},{2,10},{6,14},... | collective-permute-start | bytes 196616 | tf_op jit(solution)/shard_map/ppermute | solution.py:240
  50.6 2.8 %collective-permute-start.16 = (bf16[128,256]{1,0:T(8,128)(2,1)S(1)}, bf16[128,256]{1,0:T(8,128)(2,1)S(1)}, u32[]{:S(2)}, u32[]{:S(2)}) collective-permute-start(bf16[128,256]{1,0:T(8,128)(2,1)S(1)} %get-tuple-element.52), channel_id=1, source_target_pairs={{0,12},{4,0},{8,4},{12,8},{1,13},{5,1},{9,5},{13,9},{2,14},{6,2},{... | collective-permute-start | bytes 196616 | tf_op jit(solution)/shard_map/ppermute | solution.py:240
  53.5 0.7 %gather_fusion = s32[128,2,8]{2,0,1:T(8,128)S(1)} fusion(s32[2,8,8]{2,1,0:T(8,128)S(1)} %copy-done, s32[1024]{0:T(1024)S(1)} %pad_clamp_fusion), kind=kCustom, calls=%fused_computation | custom fusion | bytes 16896 | tf_op jit(solution)/shard_map/jit(_take)/gather | solution.py:363
  54.3 0.6 collective-permute-start.24
  54.9 0.5 collective-permute-done.14.refs_0_
  55.4 3.0 %collective-permute-done.15.refs_1_ = bf16[128,256]{1,0:T(8,128)(2,1)S(1)} collective-permute-done((bf16[128,256]{1,0:T(8,128)(2,1)S(1)}, bf16[128,256]{1,0:T(8,128)(2,1)S(1)}, u32[]{:S(2)}, u32[]{:S(2)}) %collective-permute-start.15) | collective-permute-done | bytes 65568 | tf_op jit(solution)/shard_map/ppermute | solution.py:240
  58.4 0.6 collective-permute-start.17
  59.1 0.1 collective-permute-start.25
  59.1 3.6 %collective-permute-done.17.refs_0_ = bf16[128,256]{1,0:T(8,128)(2,1)S(1)} collective-permute-done((bf16[128,256]{1,0:T(8,128)(2,1)S(1)}, bf16[128,256]{1,0:T(8,128)(2,1)S(1)}, u32[]{:S(2)}, u32[]{:S(2)}) %collective-permute-start.17) | collective-permute-done | bytes 65568 | tf_op jit(solution)/shard_map/ppermute | solution.py:249
  62.8 0.1 collective-permute-start.18
  62.8 0.1 convert_bitcast_fusion
  62.9 0.1 copy.10
  63.0 0.2 copy.11.refs_4_
  63.3 0.8 %collective-permute-done.18.refs_1_ = bf16[128,256]{1,0:T(8,128)(2,1)S(1)} collective-permute-done((bf16[128,256]{1,0:T(8,128)(2,1)S(1)}, bf16[128,256]{1,0:T(8,128)(2,1)S(1)}, u32[]{:S(2)}, u32[]{:S(2)}) %collective-permute-start.18) | collective-permute-done | bytes 65568 | tf_op jit(solution)/shard_map/ppermute | solution.py:48
  64.1 1.4 %finish.1 = f32[2,128,512]{2,1,0:T(8,128)} custom-call(s32[4]{0:T(128)S(1)} %pad_add_fusion.info, bf16[128,256]{1,0:T(8,128)(2,1)S(1)} %eta_sum.2.refs_0_, bf16[128,256]{1,0:T(8,128)(2,1)S(1)} %collective-permute-done.18.refs_1_, bf16[128,256]{1,0:T(8,128)(2,1)S(1)} %eta_sum.3.refs_2_, bf16[128,256]{1,0:T(8,128)(2,1)S(1)} %collective-permute-done.25.refs_3_, ...), custom_call_target="tpu_custom_call" | custom-call | bytes 1310736 | tf_op jit(solution)/shard_map/finish/pallas_call | solution.py:19
  (28 shorter events, 0.2 us)
Async XLA Ops:
  1.5 12.3 %collective-permute-start = (bf16[128,512]{1,0:T(8,128)(2,1)S(1)}, bf16[128,512]{1,0:T(8,128)(2,1)S(1)}, u32[]{:S(2)}, u32[]{:S(2)}) collective-permute-start(bf16[128,512]{1,0:T(8,128)(2,1)S(1)} %slice_bitcast_fusion.2), channel_id=1, source_target_pairs={{0,4},{4,8},{8,12},{12,0},{1,5},{5,9},{9,13},{13,1},{2,6},{6,10},{... | collective-permute-start | bytes 393224 | tf_op jit(solution)/shard_map/ppermute | solution.py:53
  4.6 9.3 %collective-permute-start.1 = (bf16[128,512]{1,0:T(8,128)(2,1)S(1)}, bf16[128,512]{1,0:T(8,128)(2,1)S(1)}, u32[]{:S(2)}, u32[]{:S(2)}) collective-permute-start(bf16[128,512]{1,0:T(8,128)(2,1)S(1)} %slice_bitcast_fusion.2), channel_id=1, source_target_pairs={{0,12},{4,0},{8,4},{12,8},{1,13},{5,1},{9,5},{13,9},{2,14},{6,2},{... | collective-permute-start | bytes 393224 | tf_op jit(solution)/shard_map/ppermute | solution.py:52
  6.7 7.2 %collective-permute-start.2 = (bf16[128,512]{1,0:T(8,128)(2,1)S(1)}, bf16[128,512]{1,0:T(8,128)(2,1)S(1)}, u32[]{:S(2)}, u32[]{:S(2)}) collective-permute-start(bf16[128,512]{1,0:T(8,128)(2,1)S(1)} %slice_bitcast_fusion.2), channel_id=1, source_target_pairs={{0,2},{2,0},{1,3},{3,1},{4,6},{6,4},{5,7},{7,5},{8,10},{10,8},{9,1... | collective-permute-start | bytes 393224 | tf_op jit(solution)/shard_map/ppermute | solution.py:55
  9.0 0.7 %copy-start = (s32[2,8,8]{2,1,0:T(8,128)S(1)}, s32[2,8,8]{2,1,0:T(8,128)}, u32[]{:S(2)}) copy-start(s32[2,8,8]{2,1,0:T(8,128)} %mask.1) | copy-start | bytes 1540
  9.1 0.7 %copy-start.5 = (s32[1,1,12]{2,1,0:T(1,128)S(1)}, s32[1,1,12]{2,1,0:T(1,128)}, u32[]{:S(2)}) copy-start(s32[1,1,12]{2,1,0:T(1,128)} %param.11) | copy-start | bytes 148
  9.1 0.7 %copy-start.6 = (s32[1,1,12]{2,1,0:T(1,128)S(1)}, s32[1,1,12]{2,1,0:T(1,128)}, u32[]{:S(2)}) copy-start(s32[1,1,12]{2,1,0:T(1,128)} %param.12) | copy-start | bytes 148
  9.8 1.2 %copy-start.2 = (bf16[2,512,512]{2,1,0:T(8,128)(2,1)S(1)}, bf16[2,512,512]{2,1,0:T(8,128)(2,1)}, u32[]{:S(2)}) copy-start(bf16[2,512,512]{2,1,0:T(8,128)(2,1)} %weights.1) | copy-start | bytes 3145732
  11.0 1.0 %copy-start.4 = (bf16[1,1,12,128,128]{4,3,2,1,0:T(8,128)(2,1)S(1)}, bf16[1,1,12,128,128]{4,3,2,1,0:T(8,128)(2,1)}, u32[]{:S(2)}) copy-start(bf16[1,1,12,128,128]{4,3,2,1,0:T(8,128)(2,1)} %param.10) | copy-start | bytes 1179652
  12.0 1.9 %copy-start.1 = (bf16[1,1,256,512]{3,2,1,0:T(8,128)(2,1)S(1)}, bf16[1,1,256,512]{3,2,1,0:T(8,128)(2,1)}, u32[]{:S(2)}) copy-start(bf16[1,1,256,512]{3,2,1,0:T(8,128)(2,1)} %param.8) | copy-start | bytes 786436
  14.5 1.6 %collective-permute-start.3 = (bf16[256,512]{1,0:T(8,128)(2,1)S(1)}, bf16[256,512]{1,0:T(8,128)(2,1)S(1)}, u32[]{:S(2)}, u32[]{:S(2)}) collective-permute-start(bf16[256,512]{1,0:T(8,128)(2,1)S(1)} %get-tuple-element.33), channel_id=1, source_target_pairs={{0,1},{1,0},{2,3},{3,2},{4,5},{5,4},{6,7},{7,6},{8,9},{9,8},{10,11... | collective-permute-start | bytes 786440 | tf_op jit(solution)/shard_map/ppermute | solution.py:48
  17.1 8.2 %collective-permute-start.4 = (bf16[128,512]{1,0:T(8,128)(2,1)S(1)}, bf16[128,512]{1,0:T(8,128)(2,1)S(1)}, u32[]{:S(2)}, u32[]{:S(2)}) collective-permute-start(bf16[128,512]{1,0:T(8,128)(2,1)S(1)} %get-tuple-element.35.refs_0_.edge), channel_id=1, source_target_pairs={{0,4},{4,8},{8,12},{12,0},{1,5},{5,9},{9,13},{13,1},{2,6},{6,10},{... | collective-permute-start | bytes 393224 | tf_op jit(solution)/shard_map/ppermute | solution.py:53
  17.2 8.4 %collective-permute-start.5 = (bf16[128,512]{1,0:T(8,128)(2,1)S(1)}, bf16[128,512]{1,0:T(8,128)(2,1)S(1)}, u32[]{:S(2)}, u32[]{:S(2)}) collective-permute-start(bf16[128,512]{1,0:T(8,128)(2,1)S(1)} %get-tuple-element.35.refs_0_.edge), channel_id=1, source_target_pairs={{0,12},{4,0},{8,4},{12,8},{1,13},{5,1},{9,5},{13,9},{2,14},{6,2},{... | collective-permute-start | bytes 393224 | tf_op jit(solution)/shard_map/ppermute | solution.py:52
  21.0 5.0 %collective-permute-start.6 = (bf16[128,512]{1,0:T(8,128)(2,1)S(1)}, bf16[128,512]{1,0:T(8,128)(2,1)S(1)}, u32[]{:S(2)}, u32[]{:S(2)}) collective-permute-start(bf16[128,512]{1,0:T(8,128)(2,1)S(1)} %get-tuple-element.35.refs_0_.edge), channel_id=1, source_target_pairs={{0,2},{2,0},{1,3},{3,1},{4,6},{6,4},{5,7},{7,5},{8,10},{10,8},{9,1... | collective-permute-start | bytes 393224 | tf_op jit(solution)/shard_map/ppermute | solution.py:55
  26.0 2.2 %copy-start.3 = (bf16[1,1,256,512]{3,2,1,0:T(8,128)(2,1)S(1)}, bf16[1,1,256,512]{3,2,1,0:T(8,128)(2,1)}, u32[]{:S(2)}) copy-start(bf16[1,1,256,512]{3,2,1,0:T(8,128)(2,1)} %param.9) | copy-start | bytes 786436
  26.5 1.6 %collective-permute-start.7 = (bf16[256,512]{1,0:T(8,128)(2,1)S(1)}, bf16[256,512]{1,0:T(8,128)(2,1)S(1)}, u32[]{:S(2)}, u32[]{:S(2)}) collective-permute-start(bf16[256,512]{1,0:T(8,128)(2,1)S(1)} %get-tuple-element.38), channel_id=1, source_target_pairs={{0,1},{1,0},{2,3},{3,2},{4,5},{5,4},{6,7},{7,6},{8,9},{9,8},{10,11... | collective-permute-start | bytes 786440 | tf_op jit(solution)/shard_map/ppermute | solution.py:48
  30.0 1.5 %collective-permute-start.9 = (bf16[256,512]{1,0:T(8,128)(2,1)S(1)}, bf16[256,512]{1,0:T(8,128)(2,1)S(1)}, u32[]{:S(2)}, u32[]{:S(2)}) collective-permute-start(bf16[256,512]{1,0:T(8,128)(2,1)S(1)} %get-tuple-element.42.dx), channel_id=1, source_target_pairs={{0,1},{1,0},{2,3},{3,2},{4,5},{5,4},{6,7},{7,6},{8,9},{9,8},{10,11... | collective-permute-start | bytes 786440 | tf_op jit(solution)/shard_map/ppermute | solution.py:48
  31.9 8.2 %collective-permute-start.10 = (bf16[128,512]{1,0:T(8,128)(2,1)S(1)}, bf16[128,512]{1,0:T(8,128)(2,1)S(1)}, u32[]{:S(2)}, u32[]{:S(2)}) collective-permute-start(bf16[128,512]{1,0:T(8,128)(2,1)S(1)} %get-tuple-element.44), channel_id=1, source_target_pairs={{0,4},{4,8},{8,12},{12,0},{1,5},{5,9},{9,13},{13,1},{2,6},{6,10},{... | collective-permute-start | bytes 393224 | tf_op jit(solution)/shard_map/ppermute | solution.py:53
  33.1 9.5 %collective-permute-start.19 = (bf16[256,512]{1,0:T(8,128)(2,1)S(1)}, bf16[256,512]{1,0:T(8,128)(2,1)S(1)}, u32[]{:S(2)}, u32[]{:S(2)}) collective-permute-start(bf16[256,512]{1,0:T(8,128)(2,1)S(1)} %get-tuple-element.53.x), channel_id=1, source_target_pairs={{0,1},{1,0},{2,3},{3,2},{4,5},{5,4},{6,7},{7,6},{8,9},{9,8},{10,11... | collective-permute-start | bytes 786440 | tf_op jit(solution)/shard_map/ppermute | solution.py:48
  33.1 8.7 %collective-permute-start.11 = (bf16[128,512]{1,0:T(8,128)(2,1)S(1)}, bf16[128,512]{1,0:T(8,128)(2,1)S(1)}, u32[]{:S(2)}, u32[]{:S(2)}) collective-permute-start(bf16[128,512]{1,0:T(8,128)(2,1)S(1)} %get-tuple-element.45), channel_id=1, source_target_pairs={{0,12},{4,0},{8,4},{12,8},{1,13},{5,1},{9,5},{13,9},{2,14},{6,2},{... | collective-permute-start | bytes 393224 | tf_op jit(solution)/shard_map/ppermute | solution.py:52
  35.8 6.1 %collective-permute-start.12 = (bf16[128,512]{1,0:T(8,128)(2,1)S(1)}, bf16[128,512]{1,0:T(8,128)(2,1)S(1)}, u32[]{:S(2)}, u32[]{:S(2)}) collective-permute-start(bf16[128,512]{1,0:T(8,128)(2,1)S(1)} %get-tuple-element.46), channel_id=1, source_target_pairs={{0,2},{2,0},{1,3},{3,1},{4,6},{6,4},{5,7},{7,5},{8,10},{10,8},{9,1... | collective-permute-start | bytes 393224 | tf_op jit(solution)/shard_map/ppermute | solution.py:55
  36.7 10.9 %collective-permute-start.8 = (bf16[256,512]{1,0:T(8,128)(2,1)S(1)}, bf16[256,512]{1,0:T(8,128)(2,1)S(1)}, u32[]{:S(2)}, u32[]{:S(2)}) collective-permute-start(bf16[256,512]{1,0:T(8,128)(2,1)S(1)} %get-tuple-element.40.x), channel_id=1, source_target_pairs={{0,1},{1,0},{2,3},{3,2},{4,5},{5,4},{6,7},{7,6},{8,9},{9,8},{10,11... | collective-permute-start | bytes 786440 | tf_op jit(solution)/shard_map/ppermute | solution.py:48
  40.1 2.5 %collective-permute-start.20 = (bf16[256,256]{1,0:T(8,128)(2,1)S(1)}, bf16[256,256]{1,0:T(8,128)(2,1)S(1)}, u32[]{:S(2)}, u32[]{:S(2)}) collective-permute-start(bf16[256,256]{1,0:T(8,128)(2,1)S(1)} %get-tuple-element.55), channel_id=1, source_target_pairs={{0,1},{1,0},{2,3},{3,2},{4,5},{5,4},{6,7},{7,6},{8,9},{9,8},{10,11... | collective-permute-start | bytes 393224 | tf_op jit(solution)/shard_map/ppermute | solution.py:48
  42.5 5.1 %collective-permute-start.13 = (bf16[256,256]{1,0:T(8,128)(2,1)S(1)}, bf16[256,256]{1,0:T(8,128)(2,1)S(1)}, u32[]{:S(2)}, u32[]{:S(2)}) collective-permute-start(bf16[256,256]{1,0:T(8,128)(2,1)S(1)} %get-tuple-element.48), channel_id=1, source_target_pairs={{0,1},{1,0},{2,3},{3,2},{4,5},{5,4},{6,7},{7,6},{8,9},{9,8},{10,11... | collective-permute-start | bytes 393224 | tf_op jit(solution)/shard_map/ppermute | solution.py:48
  43.6 7.1 %collective-permute-start.21 = (bf16[128,256]{1,0:T(8,128)(2,1)S(1)}, bf16[128,256]{1,0:T(8,128)(2,1)S(1)}, u32[]{:S(2)}, u32[]{:S(2)}) collective-permute-start(bf16[128,256]{1,0:T(8,128)(2,1)S(1)} %get-tuple-element.57), channel_id=1, source_target_pairs={{0,4},{4,8},{8,12},{12,0},{1,5},{5,9},{9,13},{13,1},{2,6},{6,10},{... | collective-permute-start | bytes 196616 | tf_op jit(solution)/shard_map/ppermute | solution.py:240
  44.5 9.8 %collective-permute-start.22 = (bf16[128,256]{1,0:T(8,128)(2,1)S(1)}, bf16[128,256]{1,0:T(8,128)(2,1)S(1)}, u32[]{:S(2)}, u32[]{:S(2)}) collective-permute-start(bf16[128,256]{1,0:T(8,128)(2,1)S(1)} %get-tuple-element.58), channel_id=1, source_target_pairs={{0,8},{4,12},{8,0},{12,4},{1,9},{5,13},{9,1},{13,5},{2,10},{6,14},... | collective-permute-start | bytes 196616 | tf_op jit(solution)/shard_map/ppermute | solution.py:240
  45.9 8.4 %collective-permute-start.23 = (bf16[128,256]{1,0:T(8,128)(2,1)S(1)}, bf16[128,256]{1,0:T(8,128)(2,1)S(1)}, u32[]{:S(2)}, u32[]{:S(2)}) collective-permute-start(bf16[128,256]{1,0:T(8,128)(2,1)S(1)} %get-tuple-element.59), channel_id=1, source_target_pairs={{0,12},{4,0},{8,4},{12,8},{1,13},{5,1},{9,5},{13,9},{2,14},{6,2},{... | collective-permute-start | bytes 196616 | tf_op jit(solution)/shard_map/ppermute | solution.py:240
  48.5 6.8 %collective-permute-start.14 = (bf16[128,256]{1,0:T(8,128)(2,1)S(1)}, bf16[128,256]{1,0:T(8,128)(2,1)S(1)}, u32[]{:S(2)}, u32[]{:S(2)}) collective-permute-start(bf16[128,256]{1,0:T(8,128)(2,1)S(1)} %get-tuple-element.50), channel_id=1, source_target_pairs={{0,4},{4,8},{8,12},{12,0},{1,5},{5,9},{9,13},{13,1},{2,6},{6,10},{... | collective-permute-start | bytes 196616 | tf_op jit(solution)/shard_map/ppermute | solution.py:240
  49.1 9.3 %collective-permute-start.15 = (bf16[128,256]{1,0:T(8,128)(2,1)S(1)}, bf16[128,256]{1,0:T(8,128)(2,1)S(1)}, u32[]{:S(2)}, u32[]{:S(2)}) collective-permute-start(bf16[128,256]{1,0:T(8,128)(2,1)S(1)} %get-tuple-element.51), channel_id=1, source_target_pairs={{0,8},{4,12},{8,0},{12,4},{1,9},{5,13},{9,1},{13,5},{2,10},{6,14},... | collective-permute-start | bytes 196616 | tf_op jit(solution)/shard_map/ppermute | solution.py:240
  50.6 7.7 %collective-permute-start.16 = (bf16[128,256]{1,0:T(8,128)(2,1)S(1)}, bf16[128,256]{1,0:T(8,128)(2,1)S(1)}, u32[]{:S(2)}, u32[]{:S(2)}) collective-permute-start(bf16[128,256]{1,0:T(8,128)(2,1)S(1)} %get-tuple-element.52), channel_id=1, source_target_pairs={{0,12},{4,0},{8,4},{12,8},{1,13},{5,1},{9,5},{13,9},{2,14},{6,2},{... | collective-permute-start | bytes 196616 | tf_op jit(solution)/shard_map/ppermute | solution.py:240
  54.3 4.7 %collective-permute-start.24 = (bf16[128,256]{1,0:T(8,128)(2,1)S(1)}, bf16[128,256]{1,0:T(8,128)(2,1)S(1)}, u32[]{:S(2)}, u32[]{:S(2)}) collective-permute-start(bf16[128,256]{1,0:T(8,128)(2,1)S(1)} %phi_sum.3.own), channel_id=1, source_target_pairs={{0,2},{2,0},{1,3},{3,1},{4,6},{6,4},{5,7},{7,5},{8,10},{10,8},{9,1... | collective-permute-start | bytes 196616 | tf_op jit(solution)/shard_map/ppermute | solution.py:249
  58.4 4.3 %collective-permute-start.17 = (bf16[128,256]{1,0:T(8,128)(2,1)S(1)}, bf16[128,256]{1,0:T(8,128)(2,1)S(1)}, u32[]{:S(2)}, u32[]{:S(2)}) collective-permute-start(bf16[128,256]{1,0:T(8,128)(2,1)S(1)} %phi_sum.2.own), channel_id=1, source_target_pairs={{0,2},{2,0},{1,3},{3,1},{4,6},{6,4},{5,7},{7,5},{8,10},{10,8},{9,1... | collective-permute-start | bytes 196616 | tf_op jit(solution)/shard_map/ppermute | solution.py:249
  59.1 4.2 %collective-permute-start.25 = (bf16[128,256]{1,0:T(8,128)(2,1)S(1)}, bf16[128,256]{1,0:T(8,128)(2,1)S(1)}, u32[]{:S(2)}, u32[]{:S(2)}) collective-permute-start(bf16[128,256]{1,0:T(8,128)(2,1)S(1)} %eta_sum.3.refs_2_), channel_id=1, source_target_pairs={{0,1},{1,0},{2,3},{3,2},{4,5},{5,4},{6,7},{7,6},{8,9},{9,8},{10,11... | collective-permute-start | bytes 196616 | tf_op jit(solution)/shard_map/ppermute | solution.py:48
  62.8 1.3 %collective-permute-start.18 = (bf16[128,256]{1,0:T(8,128)(2,1)S(1)}, bf16[128,256]{1,0:T(8,128)(2,1)S(1)}, u32[]{:S(2)}, u32[]{:S(2)}) collective-permute-start(bf16[128,256]{1,0:T(8,128)(2,1)S(1)} %eta_sum.2.refs_0_), channel_id=1, source_target_pairs={{0,1},{1,0},{2,3},{3,2},{4,5},{5,4},{6,7},{7,6},{8,9},{9,8},{10,11... | collective-permute-start | bytes 196616 | tf_op jit(solution)/shard_map/ppermute | solution.py:48

commit v2 on v1

v2 whole, which is shorter than its diff:
```python
import functools

import jax
import jax.numpy as jnp
from jax import lax
from jax.experimental import pallas as pl
from jax.experimental.pallas import tpu as pltpu
from jax.sharding import PartitionSpec as P

BF16 = jnp.bfloat16
F32 = jnp.float32
VMEM = pl.BlockSpec(memory_space=pltpu.VMEM)
SMEM = pl.BlockSpec(memory_space=pltpu.SMEM)
ANY = pl.BlockSpec(memory_space=pl.ANY)
NOTE = 16


def call(kernel, ins, outs, scratch=(), flops=0, name=None, far=()):
    moved = sum(a.size * a.dtype.itemsize for a in ins)
    moved += sum(a.size * a.dtype.itemsize for a in outs)
    return pl.pallas_call(
        kernel,
        out_shape=outs,
        in_specs=[
            ANY if i in far else SMEM if a.dtype == jnp.int32 and a.ndim == 1 else VMEM
            for i, a in enumerate(ins)
        ],
        out_specs=[VMEM] * len(outs),
        scratch_shapes=list(scratch),
        compiler_params=pltpu.CompilerParams(vmem_limit_bytes=32 << 20),
        cost_estimate=pl.CostEstimate(flops=flops, bytes_accessed=moved, transcendentals=0),
        name=name,
    )(*ins)


def shaped(shape, dtype):
    return jax.ShapeDtypeStruct(shape, dtype)


def dot(a, b, contract=((1,), (0,))):
    return lax.dot_general(a, b, (contract, ((), ())), preferred_element_type=F32)


def ring(axis, step, periodic):
    count = lax.axis_size(axis)
    pairs = [(i, i + step) for i in range(count) if 0 <= i + step < count]
    if periodic:
        pairs = [(i, (i + step) % count) for i in range(count)]
    return pairs


def swap_half(value):
    return lax.ppermute(value, "half", [(0, 1), (1, 0)])


def to_neighbours(low_phi, high_phi, low_eta, high_eta):
    from_high = lax.ppermute(low_phi, "phi", ring("phi", -1, True))
    from_low = lax.ppermute(high_phi, "phi", ring("phi", 1, True))
    if lax.axis_size("eta") == 2:
        return [from_low, from_high, lax.ppermute(low_eta, "eta", [(0, 1), (1, 0)])]
    from_upper = lax.ppermute(low_eta, "eta", ring("eta", -1, False))
    from_lower = lax.ppermute(high_eta, "eta", ring("eta", 1, False))
    return [from_low, from_high, from_lower, from_upper]


def keep_full(mask, side):
    grid = mask.shape[0]
    width = grid * side
    spread = (
        lax.broadcasted_iota(jnp.int32, (width, grid), 0) // side
        == lax.broadcasted_iota(jnp.int32, (width, grid), 1)
    ).astype(F32)
    return dot(dot(spread, mask.astype(F32)), spread, ((1,), (1,)))


def build_kernel(own, pair, src, dst, info, tiles, weights, mask, m_out, w_out, tbuf, wbuf, kbuf, acc, sem):
    copies = [
        pltpu.make_async_copy(tiles, tbuf, sem.at[0]),
        pltpu.make_async_copy(mask, kbuf, sem.at[1]),
        pltpu.make_async_copy(weights.at[0], wbuf, sem.at[2]),
    ]
    for copy in copies:
        copy.start()
    slots, block = tbuf.shape[0], tbuf.shape[1]
    acc[...] = jnp.zeros_like(acc)
    half = info[0]
    eta = info[1]
    copies[0].wait()
    for t in range(slots):
        source = src[t]
        target = dst[t]
        column = jnp.where(source > own + 2, own + 2, source) if pair else source
        live = target >= 0
        if pair:
            outside = ((source == own + 2) & (eta == 0)) | ((source == own + 3) & (eta == 1))
            live = live & jnp.logical_not(outside)
        row = jnp.where(target >= half * own, target - half * own, target - half * own + 2 * own)

        @pl.when(live)
        def _():
            rows = pl.ds(pl.multiple_of(row * block, block), block)
            columns = pl.ds(pl.multiple_of(column * block, block), block)
            acc[rows, columns] += tbuf[t].astype(F32)

    m_out[...] = acc[...].astype(BF16)
    copies[1].wait()
    full = keep_full(kbuf[0], wbuf.shape[0] // kbuf.shape[1])
    copies[2].wait()
    w_out[...] = (wbuf[...].astype(F32) * full).astype(BF16)


def later_kernel(matrix, weights, mask, mt_out, w_out):
    mt_out[...] = matrix[...].T
    layers, width = weights.shape[0], weights.shape[1]
    for layer in range(1, layers):
        full = keep_full(mask[layer], width // mask.shape[1])
        w_out[layer - 1] = (weights[layer].astype(F32) * full).astype(BF16)


def gather_kernel(count, matrix, *refs):
    sources, (own_out, other_out) = refs[:count], refs[count:]
    rows, block = own_out.shape[0], refs[1].shape[0] - NOTE
    parts = [sources[0][...]] + [r[:block, :] for r in sources[1:]]
    total = dot(matrix[...], jnp.concatenate(parts, axis=0)).astype(BF16)
    own_out[...] = total[:rows]
    other_out[...] = total[rows:]


def mix(state, own, other):
    hfloat = state.astype(F32)
    return hfloat, (hfloat + own.astype(F32) + other.astype(F32)).astype(BF16)


def edge_kernel(state, own, other, out):
    block = out.shape[0]
    out[...] = mix(state[:block, :], own[:block, :], other[:block, :])[1]


def live_rows(info, rows, width):
    first = info[0] * rows
    row = first + lax.broadcasted_iota(jnp.int32, (rows, width), 0)
    return (row < info[2]).astype(F32)


def forward_kernel(info, state, own, other, weight, x_out, new_out, slope_out):
    rows, width = x_out.shape
    hfloat, mixed = mix(state[...], own[...], other[...])
    x_out[...] = mixed
    pre = dot(mixed, weight[...])
    live = live_rows(info, rows, width)
    sigma = jax.nn.sigmoid(pre)
    new_out[...] = (live * (hfloat + pre * sigma)).astype(BF16)
    slope_out[...] = live * sigma * (1.0 + pre * (1.0 - sigma))


def rim_kernel(count, matrix, weight, new, *refs):
    starts, mixes = refs[:count], refs[count : 2 * count]
    own_out, other_out, slope_out = refs[2 * count :]
    block, width = mixes[0].shape
    rows = own_out.shape[0]
    pre_all = dot(jnp.concatenate([r[...] for r in mixes], axis=0), weight[...])
    parts = [new[...]]
    for i in range(count):
        pre = pre_all[i * block : (i + 1) * block]
        note = starts[i][block : block + NOTE, :].astype(F32)[:1, :]
        row = lax.broadcasted_iota(jnp.int32, (block, width), 0).astype(F32)
        live = (row < note).astype(F32)
        sigma = jax.nn.sigmoid(pre)
        hfloat = starts[i][:block, :].astype(F32)
        parts.append((live * (hfloat + pre * sigma)).astype(BF16))
        slope_out[i * block : (i + 1) * block, :] = live * sigma * (1.0 + pre * (1.0 - sigma))
    total = dot(matrix[...], jnp.concatenate(parts, axis=0)).astype(BF16)
    own_out[...] = total[:rows]
    other_out[...] = total[rows:]


def last_kernel(info, state, own, other, weight, cot, x_out, final_out, dz_out, dx_out):
    rows, width = x_out.shape
    hfloat, mixed = mix(state[...], own[...], other[...])
    x_out[...] = mixed
    pre = dot(mixed, weight[...])
    live = live_rows(info, rows, width)
    sigma = jax.nn.sigmoid(pre)
    delta = cot[...].astype(F32) * live * sigma * (1.0 + pre * (1.0 - sigma))
    delta = delta.astype(BF16)
    dz_out[...] = delta
    dx_out[...] = dot(delta, weight[...], ((1,), (1,))).astype(BF16)
    final_out[...] = (live * (hfloat + pre * sigma)).astype(BF16)


def split_columns(info, value, mine_out, theirs_out):
    middle = value.shape[1] // 2
    first = info[0] == 0
    left, right = value[:, :middle], value[:, middle:]
    mine_out[...] = jnp.where(first, left, right)
    theirs_out[...] = jnp.where(first, right, left).astype(BF16)


def grad_kernel(info, x, dz, mine_out, theirs_out):
    split_columns(info, dot(x[...], dz[...], ((0,), (0,))), mine_out, theirs_out)


def back_kernel(count, info, mt, dx, dx_other, cot, slope, slope_rim, x, *refs):
    mixes, (mine_out, theirs_out) = refs[:count], refs[count:]
    rows = dx.shape[0]
    whole = jnp.concatenate([dx[...], dx_other[...]], axis=0)
    total = dot(mt[...], whole)
    upstream = cot[...].astype(F32) + dx[...].astype(F32) + total[:rows]
    delta = (upstream * slope[...]).astype(BF16)
    delta_rim = (total[rows:] * slope_rim[...]).astype(BF16)
    sources = jnp.concatenate([x[...]] + [r[...] for r in mixes], axis=0)
    deltas = jnp.concatenate([delta, delta_rim], axis=0)
    split_columns(info, dot(sources, deltas, ((0,), (0,))), mine_out, theirs_out)


def share_kernel(parts, layers, info, *refs):
    ins, outs = refs[: 2 * layers], refs[2 * layers :]
    span = outs[0].shape[0] // layers
    for step in range(parts):
        target = lax.rem(info[3] + step, parts)
        place = pl.ds(pl.multiple_of(target * span, span), span)
        for layer in range(layers):
            mine, arrived = ins[2 * layer], ins[2 * layer + 1]
            part = mine[place, :] + arrived[place, :].astype(F32)
            outs[step][layer * span : (layer + 1) * span, :] = part.astype(outs[step].dtype)


def sum_kernel(own, *refs):
    total = own[...].astype(F32)
    for r in refs[:-1]:
        total = total + r[...].astype(F32)
    refs[-1][...] = total.astype(BF16)


def finish_kernel(info, mine_ref, theirs_ref, keep, out):
    layers, rows, width = out.shape
    middle = width // 2
    first = info[0] == 0
    for layer in range(layers):
        part = slice(layer * rows, (layer + 1) * rows)
        mine, theirs = mine_ref[part, :].astype(F32), theirs_ref[part, :].astype(F32)
        kept = keep[layer]
        out[layer, :, :middle] = jnp.where(first, mine, theirs) * kept[:, :middle]
        out[layer, :, middle:] = jnp.where(first, theirs, mine) * kept[:, middle:]


def phi_share(info, pieces, layers):
    parts = lax.axis_size("phi")
    width, columns = pieces[0].shape
    span = width // parts
    if parts > 8:
        totals = [
            (pieces[2 * i] + pieces[2 * i + 1].astype(F32)).astype(BF16) for i in range(layers)
        ]
        shares = lax.psum_scatter(jnp.stack(totals), "phi", scatter_dimension=1, tiled=True)
        return shares.reshape(layers * span, columns)
    own, *sends = call(
        functools.partial(share_kernel, parts, layers),
        (info, *pieces),
        [shaped((layers * span, columns), F32)]
        + [shaped((layers * span, columns), BF16)] * (parts - 1),
        name="share",
    )
    arrived = [
        lax.ppermute(sends[step - 1], "phi", ring("phi", step, True)) for step in range(1, parts)
    ]
    return call(sum_kernel, (own, *arrived), [shaped(own.shape, BF16)], name="phi_sum")[0]


def eta_sum(share):
    if lax.axis_size("eta") == 2:
        arrived = lax.ppermute(share, "eta", [(0, 1), (1, 0)])
        return call(sum_kernel, (share, arrived), [shaped(share.shape, BF16)], name="eta_sum")[0]
    gathered = lax.all_gather(share, "eta", axis=0)
    return jnp.sum(gathered.astype(F32), axis=0).astype(BF16)


def body(feats, cotangent, tiles, tile_src, tile_dst, weights, mask, counts):
    rows, width = feats.shape[2], feats.shape[3]
    block = tiles.shape[3]
    own = rows // block
    pair = lax.axis_size("eta") == 2
    rims = 3 if pair else 4
    layers, grid = weights.shape[0], mask.shape[1]
    side = width // grid
    half_here = lax.axis_index("half")
    count = counts[0, 0]
    info = jnp.stack([half_here, lax.axis_index("eta"), count, lax.axis_index("phi")])
    info = info.astype(jnp.int32)
    state = feats[0, 0]
    cot = cotangent[0, 0]
    height, depth = 2 * rows, rows + rims * block

    note = jnp.clip(count - half_here * rows, 0, block).astype(BF16)
    edge = jnp.concatenate([state[:block], jnp.full((NOTE, width), note, BF16)], axis=0)
    starts = to_neighbours(edge, edge, edge, edge)
    matrix, masked0 = call(
        functools.partial(build_kernel, own, pair),
        (tile_src[0, 0], tile_dst[0, 0], info, tiles[0, 0], weights, mask),
        [shaped((height, depth), BF16), shaped((width, width), BF16)],
        [
            pltpu.VMEM(tiles.shape[2:], BF16),
            pltpu.VMEM((width, width), BF16),
            pltpu.VMEM(mask.shape, jnp.int32),
            pltpu.VMEM((height, depth), F32),
            pltpu.SemaphoreType.DMA((3,)),
        ],
        10_000_000,
        "build",
        (3, 4, 5),
    )
    agg_flops = 2 * height * depth * width
    dense_flops = 2 * rows * width * width
    wide = shaped((rows, width), BF16)

    own_part, other_part = call(
        functools.partial(gather_kernel, 1 + rims),
        (matrix, state, *starts),
        [wide, wide],
        flops=agg_flops,
        name="gather",
    )
    received = swap_half(other_part)
    edge = call(
        edge_kernel, (state, own_part, received), [shaped((block, width), BF16)], name="edge"
    )[0]
    mixes = to_neighbours(edge, edge, edge, edge)
    x0, new, slope0 = call(
        forward_kernel,
        (info, state, own_part, received, masked0),
        [wide, wide, shaped((rows, width), F32)],
        flops=dense_flops,
        name="forward",
    )
    matrix_t, masked = call(
        later_kernel,
        (matrix, weights, mask),
        [shaped((depth, height), BF16), shaped((layers - 1, width, width), BF16)],
        flops=10_000_000,
        name="later",
    )
    own_part, other_part, slope_rim = call(
        functools.partial(rim_kernel, rims),
        (matrix, masked0, new, *starts, *mixes),
        [wide, wide, shaped((rims * block, width), F32)],
        flops=agg_flops + 2 * dense_flops,
        name="rim",
    )
    received = swap_half(other_part)
    x1, final, dz1, dx = call(
        last_kernel,
        (info, new, own_part, received, masked[0], cot),
        [wide, wide, wide, wide],
        flops=2 * dense_flops,
        name="last",
    )
    dx_other = swap_half(dx)
    halves = [shaped((width, width // 2), F32), shaped((width, width // 2), BF16)]
    mine1, theirs1 = call(
        grad_kernel, (info, x1, dz1), halves, flops=dense_flops, name="grad"
    )
    arrived1 = swap_half(theirs1)
    mine0, theirs0 = call(
        functools.partial(back_kernel, rims),
        (info, matrix_t, dx, dx_other, cot, slope0, slope_rim, x0, *mixes),
        halves,
        flops=2 * agg_flops,
        name="back",
    )
    arrived0 = swap_half(theirs0)
    share = phi_share(info, (mine0, arrived0, mine1, arrived1), layers)
    total = eta_sum(share)
    theirs = swap_half(total)

    span = width // lax.axis_size("phi")
    row_ids = (lax.axis_index("phi") * span + jnp.arange(span, dtype=jnp.int32)) // side
    chosen = jnp.take(mask, row_ids, axis=1)
    keep = jnp.broadcast_to(chosen[..., None], (layers, span, grid, side)).reshape(
        layers, span, width
    )
    result = call(
        finish_kernel,
        (info, total, theirs, keep.astype(F32)),
        [shaped((layers, span, width), F32)],
        name="finish",
    )[0]
    return final[None, None], result


def solution(mesh):
    in_specs = (
        P(("group", "phi"), "eta", "half", None),
        P(("group", "phi"), "eta", "half", None),
        P(("group", "phi"), "eta", "half", None, None),
        P(("group", "phi"), "eta", "half"),
        P(("group", "phi"), "eta", "half"),
        P(),
        P(),
        P(("group", "phi"), "eta"),
    )
    out_specs = (P(("group", "phi"), "eta", "half", None), P("group", "phi", None))
    return jax.shard_map(body, mesh=mesh, in_specs=in_specs, out_specs=out_specs, check_vma=False)
```

time: 65.7 us -> 56.6 us (0.86)
  starting transfers between devices: 27.1 us -> 19.3 us
  local copies, waits for them, and re-layouts: 4.93 us -> 4.03 us
    ppermute x6 -> x3, waiting for transfers between devices: 3.49 us -> 8.6 us  [phi_share(): lax.ppermute(sends[step - 1], 'phi', ring('phi', step, True))]
    ppermute x3 -> x2, waiting for transfers between devices: 6.81 us -> 1.85 us  [to_neighbours(): from_low = lax.ppermute(high_phi, 'phi', ring('phi', 1, True))]
    ppermute x6 -> x3, starting transfers between devices: 8.94 us -> 4.53 us  [phi_share(): lax.ppermute(sends[step - 1], 'phi', ring('phi', step, True))]
    ppermute x3 -> x2, starting transfers between devices: 8.54 us -> 4.79 us  [to_neighbours(): from_high = lax.ppermute(low_phi, 'phi', ring('phi', -1, True))]
    ppermute x3 -> x2, waiting for transfers between devices: 1.14 us -> 2.12 us  [to_neighbours(): from_high = lax.ppermute(low_phi, 'phi', ring('phi', -1, True))]
    ppermute x2 -> x1, waiting for transfers between devices: 3.6 us -> 2.69 us  [eta_sum(): arrived = lax.ppermute(share, 'eta', [(0, 1), (1, 0)])]
    unnamed x14 -> x16, local copies, waits for them, and re-layouts: 2.9 us -> 2.06 us
    ppermute x2 -> x1, starting transfers between devices: 1.19 us -> 1.56 us  [eta_sum(): arrived = lax.ppermute(share, 'eta', [(0, 1), (1, 0)])]
  transfers between devices with their start and end apart: 26 -> 16, of which waited for: 12 -> 11; matrix products, arithmetic and copies ran while one was open for 2% -> 2% of each run, Pallas kernels for 8% -> 10%
where the time goes in v2:
time: 56.6 us; the launch traced here: 56.2 us
  waiting for transfers between devices  20.2 us (36%)
  starting transfers between devices  19.3 us (34%)
  Pallas kernels  11 us (19%)
  local copies, waits for them, and re-layouts  4.03 us (7%)
  between operations  1.52 us (3%)
    pallas_call x13, Pallas kernels, call(): pl.pallas_call(kernel, out_shape=outs, in_specs=[ANY if i in far else SME...  11 us
    ppermute x3, waiting for transfers between devices, phi_share(): lax.ppermute(sends[step - 1], 'phi', ring('phi', step, True))  8.6 us
    ppermute x6, waiting for transfers between devices, swap_half(): return lax.ppermute(value, 'half', [(0, 1), (1, 0)])  4.91 us
    ppermute x2, starting transfers between devices, to_neighbours(): from_high = lax.ppermute(low_phi, 'phi', ring('phi', -1, True))  4.79 us
    ppermute x3, starting transfers between devices, phi_share(): lax.ppermute(sends[step - 1], 'phi', ring('phi', step, True))  4.53 us
    ppermute x2, starting transfers between devices, to_neighbours(): from_low = lax.ppermute(high_phi, 'phi', ring('phi', 1, True))  4.26 us
    ppermute x2, starting transfers between devices, to_neighbours(): return [from_low, from_high, lax.ppermute(low_eta, 'eta', [(0, 1), (1, 0)])]  3.14 us
    ppermute x1, waiting for transfers between devices, eta_sum(): arrived = lax.ppermute(share, 'eta', [(0, 1), (1, 0)])  2.69 us
  transfers between devices with their start and end apart: 16, of which 11 were waited for; matrix products, arithmetic and copies ran while one was open for 2% of the time, Pallas kernels for 10%

profile of v2, /device:TPU:0, one launch (start us, length us, event | category | flops | bytes accessed | tf_op | source)
XLA Modules:
  0.0 56.2 jit_solution(13375983843918151349)
XLA Ops:
  0.6 0.0 copy-start.5
  1.4 0.9 %slice_bitcast_fusion = bf16[128,512]{1,0:T(8,128)(2,1)S(1)} fusion(bf16[1,1,256,512]{3,2,1,0:T(8,128)(2,1)} %param.8), kind=kLoop, calls=%fused_computation.2 | loop fusion | bytes 262144 | tf_op jit(solution)/shard_map/slice | solution.py:295
  2.3 3.1 %collective-permute-start = (bf16[144,512]{1,0:T(8,128)(2,1)S(1)}, bf16[144,512]{1,0:T(8,128)(2,1)S(1)}, u32[]{:S(2)}, u32[]{:S(2)}) collective-permute-start(bf16[144,512]{1,0:T(8,128)(2,1)S(1)} %concatenate.3), channel_id=1, source_target_pairs={{0,4},{4,8},{8,12},{12,0},{1,5},{5,9},{9,13},{13,1},{2,6},{6,10},{... | collective-permute-start | bytes 442376 | tf_op jit(solution)/shard_map/ppermute | solution.py:58
  5.4 2.1 %collective-permute-start.1 = (bf16[144,512]{1,0:T(8,128)(2,1)S(1)}, bf16[144,512]{1,0:T(8,128)(2,1)S(1)}, u32[]{:S(2)}, u32[]{:S(2)}) collective-permute-start(bf16[144,512]{1,0:T(8,128)(2,1)S(1)} %concatenate.3), channel_id=1, source_target_pairs={{0,12},{4,0},{8,4},{12,8},{1,13},{5,1},{9,5},{13,9},{2,14},{6,2},{... | collective-permute-start | bytes 442376 | tf_op jit(solution)/shard_map/ppermute | solution.py:57
  7.5 1.6 %collective-permute-start.2 = (bf16[144,512]{1,0:T(8,128)(2,1)S(1)}, bf16[144,512]{1,0:T(8,128)(2,1)S(1)}, u32[]{:S(2)}, u32[]{:S(2)}) collective-permute-start(bf16[144,512]{1,0:T(8,128)(2,1)S(1)} %concatenate.3), channel_id=1, source_target_pairs={{0,2},{2,0},{1,3},{3,1},{4,6},{6,4},{5,7},{7,5},{8,10},{10,8},{9,1... | collective-permute-start | bytes 442376 | tf_op jit(solution)/shard_map/ppermute | solution.py:60
  9.1 0.0 copy-start
  9.1 0.1 pad_add_fusion.info
  9.2 0.0 copy-start.6
  9.2 0.0 copy-start.7
  9.2 0.0 copy-done.5
  9.2 0.6 %copy-done = s32[2,8,8]{2,1,0:T(8,128)S(1)} copy-done((s32[2,8,8]{2,1,0:T(8,128)S(1)}, s32[2,8,8]{2,1,0:T(8,128)}, u32[]{:S(2)}) %copy-start) | copy-done | bytes 536
  9.8 0.0 copy-done.6
  9.8 0.0 copy-done.7
  9.9 0.0 copy-start.1
  9.9 1.2 %copy-done.1 = bf16[2,512,512]{2,1,0:T(8,128)(2,1)S(1)} copy-done((bf16[2,512,512]{2,1,0:T(8,128)(2,1)S(1)}, bf16[2,512,512]{2,1,0:T(8,128)(2,1)}, u32[]{:S(2)}) %copy-start.1) | copy-done | bytes 1048600
  11.1 1.6 %build.1 = (bf16[512,640]{1,0:T(8,128)(2,1)S(1)}, bf16[512,512]{1,0:T(8,128)(2,1)S(1)}) custom-call(s32[12]{0:T(128)S(1)} %bitcast.28, s32[12]{0:T(128)S(1)} %bitcast.29, s32[4]{0:T(128)S(1)} %pad_add_fusion.info, bf16[12,128,128]{2,1,0:T(8,128)(2,1)S(1)} %bitcast.27, bf16[2,512,512]{2,1,0:T(8,128)(2,1)S(1)} %copy-done.1, s32[2,8,8]{2,1,0:T(8,128)S(1)} %copy-done), custom_call_target="tpu_custom_call" | custom-call | flops 10000000 | bytes 2622064 | tf_op jit(solution)/shard_map/build/pallas_call | solution.py:21
  12.7 0.0 collective-permute-done.refs_1_.refs_0_
  12.7 1.1 %collective-permute-done.1.refs_2_.refs_1_ = bf16[144,512]{1,0:T(8,128)(2,1)S(1)} collective-permute-done((bf16[144,512]{1,0:T(8,128)(2,1)S(1)}, bf16[144,512]{1,0:T(8,128)(2,1)S(1)}, u32[]{:S(2)}, u32[]{:S(2)}) %collective-permute-start.1) | collective-permute-done | bytes 147488 | tf_op jit(solution)/shard_map/ppermute | solution.py:57
  13.8 0.0 collective-permute-done.2.refs_3_.refs_2_
  13.8 0.0 copy-done.3
  13.8 0.6 %gather.8 = (bf16[256,512]{1,0:T(8,128)(2,1)S(1)}, bf16[256,512]{1,0:T(8,128)(2,1)S(1)}) custom-call(bf16[512,640]{1,0:T(8,128)(2,1)S(1)} %get-tuple-element.26.matrix, bf16[256,512]{1,0:T(8,128)(2,1)S(1)} %bitcast.21, bf16[144,512]{1,0:T(8,128)(2,1)S(1)} %collective-permute-done.refs_1_.refs_0_, ...), custom_call_target="tpu_custom_call" | custom-call | flops 335544320 | bytes 1884160 | tf_op jit(solution)/shard_map/gather/pallas_call | solution.py:21
  14.4 0.1 collective-permute-start.3
  14.5 1.5 %collective-permute-done.3.other = bf16[256,512]{1,0:T(8,128)(2,1)S(1)} collective-permute-done((bf16[256,512]{1,0:T(8,128)(2,1)S(1)}, bf16[256,512]{1,0:T(8,128)(2,1)S(1)}, u32[]{:S(2)}, u32[]{:S(2)}) %collective-permute-start.3) | collective-permute-done | bytes 262176 | tf_op jit(solution)/shard_map/ppermute | solution.py:53
  16.0 0.1 edge.1
  16.1 1.2 %collective-permute-start.4 = (bf16[128,512]{1,0:T(8,128)(2,1)S(1)}, bf16[128,512]{1,0:T(8,128)(2,1)S(1)}, u32[]{:S(2)}, u32[]{:S(2)}) collective-permute-start(bf16[128,512]{1,0:T(8,128)(2,1)S(1)} %edge.1), channel_id=1, source_target_pairs={{0,4},{4,8},{8,12},{12,0},{1,5},{5,9},{9,13},{13,1},{2,6},{6,10},{... | collective-permute-start | bytes 393224 | tf_op jit(solution)/shard_map/ppermute | solution.py:58
  17.3 2.7 %collective-permute-start.5 = (bf16[128,512]{1,0:T(8,128)(2,1)S(1)}, bf16[128,512]{1,0:T(8,128)(2,1)S(1)}, u32[]{:S(2)}, u32[]{:S(2)}) collective-permute-start(bf16[128,512]{1,0:T(8,128)(2,1)S(1)} %edge.1), channel_id=1, source_target_pairs={{0,12},{4,0},{8,4},{12,8},{1,13},{5,1},{9,5},{13,9},{2,14},{6,2},{... | collective-permute-start | bytes 393224 | tf_op jit(solution)/shard_map/ppermute | solution.py:57
  19.9 1.5 %collective-permute-start.6 = (bf16[128,512]{1,0:T(8,128)(2,1)S(1)}, bf16[128,512]{1,0:T(8,128)(2,1)S(1)}, u32[]{:S(2)}, u32[]{:S(2)}) collective-permute-start(bf16[128,512]{1,0:T(8,128)(2,1)S(1)} %edge.1), channel_id=1, source_target_pairs={{0,2},{2,0},{1,3},{3,1},{4,6},{6,4},{5,7},{7,5},{8,10},{10,8},{9,1... | collective-permute-start | bytes 393224 | tf_op jit(solution)/shard_map/ppermute | solution.py:60
  21.4 1.0 %forward.1 = (bf16[256,512]{1,0:T(8,128)(2,1)S(1)}, bf16[256,512]{1,0:T(8,128)(2,1)S(1)}, f32[256,512]{1,0:T(8,128)S(1)}) custom-call(s32[4]{0:T(128)S(1)} %pad_add_fusion.info, bf16[256,512]{1,0:T(8,128)(2,1)S(1)} %bitcast.23, bf16[256,512]{1,0:T(8,128)(2,1)S(1)} %get-tuple-element.27.own, bf16[256,512]{1,0:T(8,128)(2,1)S(1)} %collective-permute-done.3.other, ...), custom_call_target="tpu_custom_call" | custom-call | flops 134217728 | bytes 2359312 | tf_op jit(solution)/shard_map/forward/pallas_call | solution.py:21
  22.5 1.8 %collective-permute-done.4.refs_3_.refs_0_ = bf16[128,512]{1,0:T(8,128)(2,1)S(1)} collective-permute-done((bf16[128,512]{1,0:T(8,128)(2,1)S(1)}, bf16[128,512]{1,0:T(8,128)(2,1)S(1)}, u32[]{:S(2)}, u32[]{:S(2)}) %collective-permute-start.4) | collective-permute-done | bytes 131104 | tf_op jit(solution)/shard_map/ppermute | solution.py:58
  24.3 1.0 %collective-permute-done.5.refs_4_.refs_1_ = bf16[128,512]{1,0:T(8,128)(2,1)S(1)} collective-permute-done((bf16[128,512]{1,0:T(8,128)(2,1)S(1)}, bf16[128,512]{1,0:T(8,128)(2,1)S(1)}, u32[]{:S(2)}, u32[]{:S(2)}) %collective-permute-start.5) | collective-permute-done | bytes 131104 | tf_op jit(solution)/shard_map/ppermute | solution.py:57
  25.3 0.0 collective-permute-done.6.refs_5_.refs_2_
  25.3 1.0 %rim.1 = (bf16[256,512]{1,0:T(8,128)(2,1)S(1)}, bf16[256,512]{1,0:T(8,128)(2,1)S(1)}, f32[384,512]{1,0:T(8,128)S(1)}) custom-call(bf16[512,640]{1,0:T(8,128)(2,1)S(1)} %get-tuple-element.26.matrix, bf16[512,512]{1,0:T(8,128)(2,1)S(1)} %get-tuple-element.29.weight, bf16[256,512]{1,0:T(8,128)(2,1)S(1)} %get-tuple-element.30.new.state, ...), custom_call_target="tpu_custom_call" | custom-call | flops 603979776 | bytes 3588096 | tf_op jit(solution)/shard_map/rim/pallas_call | solution.py:21
  26.3 0.0 copy-start.4
  26.3 0.1 collective-permute-start.7
  26.4 0.1 copy-done.2
  26.6 0.4 later.1
  27.0 1.0 %collective-permute-done.7.other = bf16[256,512]{1,0:T(8,128)(2,1)S(1)} collective-permute-done((bf16[256,512]{1,0:T(8,128)(2,1)S(1)}, bf16[256,512]{1,0:T(8,128)(2,1)S(1)}, u32[]{:S(2)}, u32[]{:S(2)}) %collective-permute-start.7) | collective-permute-done | bytes 262176 | tf_op jit(solution)/shard_map/ppermute | solution.py:53
  27.9 0.0 copy-done.4
  27.9 1.8 %last.1 = (bf16[256,512]{1,0:T(8,128)(2,1)S(1)}, bf16[256,512]{1,0:T(8,128)(2,1)}, bf16[256,512]{1,0:T(8,128)(2,1)S(1)}, bf16[256,512]{1,0:T(8,128)(2,1)S(1)}) custom-call(s32[4]{0:T(128)S(1)} %pad_add_fusion.info, bf16[256,512]{1,0:T(8,128)(2,1)S(1)} %get-tuple-element.30.new.state, bf16[256,512]{1,0:T(8,128)(2,1)S(1)} %get-tuple-element.31.own, ...), custom_call_target="tpu_custom_call" | custom-call | flops 268435456 | bytes 2621456 | tf_op jit(solution)/shard_map/last/pallas_call | solution.py:21
  29.8 0.1 collective-permute-start.8
  29.9 0.9 %grad.1 = (f32[512,256]{1,0:T(8,128)S(1)}, bf16[512,256]{1,0:T(8,128)(2,1)S(1)}) custom-call(s32[4]{0:T(128)S(1)} %pad_add_fusion.info, bf16[256,512]{1,0:T(8,128)(2,1)S(1)} %get-tuple-element.42.x, bf16[256,512]{1,0:T(8,128)(2,1)S(1)} %get-tuple-element.43.dz), custom_call_target="tpu_custom_call" | custom-call | flops 134217728 | bytes 1310736 | tf_op jit(solution)/shard_map/grad/pallas_call | solution.py:21
  30.8 0.4 collective-permute-start.10
  31.2 0.1 collective-permute-done.8.dx_other
  31.3 1.5 %back.1 = (f32[512,256]{1,0:T(8,128)S(1)}, bf16[512,256]{1,0:T(8,128)(2,1)S(1)}) custom-call(s32[4]{0:T(128)S(1)} %pad_add_fusion.info, bf16[640,512]{1,0:T(8,128)(2,1)S(1)} %get-tuple-element.35.mt, bf16[256,512]{1,0:T(8,128)(2,1)S(1)} %get-tuple-element.36.dx, bf16[256,512]{1,0:T(8,128)(2,1)S(1)} %collective-permute-done.8.dx_other, ...), custom_call_target="tpu_custom_call" | custom-call | flops 671088640 | bytes 4194320 | tf_op jit(solution)/shard_map/back/pallas_call | solution.py:21
  32.9 0.2 collective-permute-start.9
  33.0 0.0 collective-permute-done.10.refs_3_
  33.1 1.4 %collective-permute-done.9.refs_1_ = bf16[512,256]{1,0:T(8,128)(2,1)S(1)} collective-permute-done((bf16[512,256]{1,0:T(8,128)(2,1)S(1)}, bf16[512,256]{1,0:T(8,128)(2,1)S(1)}, u32[]{:S(2)}, u32[]{:S(2)}) %collective-permute-start.9) | collective-permute-done | bytes 262176 | tf_op jit(solution)/shard_map/ppermute | solution.py:53
  34.5 0.7 %share.1 = (f32[256,256]{1,0:T(8,128)S(1)}, bf16[256,256]{1,0:T(8,128)(2,1)S(1)}, bf16[256,256]{1,0:T(8,128)(2,1)S(1)}, bf16[256,256]{1,0:T(8,128)(2,1)S(1)}) custom-call(s32[4]{0:T(128)S(1)} %pad_add_fusion.info, f32[512,256]{1,0:T(8,128)S(1)} %get-tuple-element.40.refs_0_, bf16[512,256]{1,0:T(8,128)(2,1)S(1)} %collective-permute-done.9.refs_1_, ...), custom_call_target="tpu_custom_call" | custom-call | bytes 2228240 | tf_op jit(solution)/shard_map/share/pallas_call | solution.py:21
  35.1 0.8 %collective-permute-start.11 = (bf16[256,256]{1,0:T(8,128)(2,1)S(1)}, bf16[256,256]{1,0:T(8,128)(2,1)S(1)}, u32[]{:S(2)}, u32[]{:S(2)}) collective-permute-start(bf16[256,256]{1,0:T(8,128)(2,1)S(1)} %get-tuple-element.47), channel_id=1, source_target_pairs={{0,4},{4,8},{8,12},{12,0},{1,5},{5,9},{9,13},{13,1},{2,6},{6,10},{... | collective-permute-start | bytes 393224 | tf_op jit(solution)/shard_map/ppermute | solution.py:265
  35.9 1.9 %collective-permute-start.12 = (bf16[256,256]{1,0:T(8,128)(2,1)S(1)}, bf16[256,256]{1,0:T(8,128)(2,1)S(1)}, u32[]{:S(2)}, u32[]{:S(2)}) collective-permute-start(bf16[256,256]{1,0:T(8,128)(2,1)S(1)} %get-tuple-element.48), channel_id=1, source_target_pairs={{0,8},{4,12},{8,0},{12,4},{1,9},{5,13},{9,1},{13,5},{2,10},{6,14},... | collective-permute-start | bytes 393224 | tf_op jit(solution)/shard_map/ppermute | solution.py:265
  37.8 1.8 %collective-permute-start.13 = (bf16[256,256]{1,0:T(8,128)(2,1)S(1)}, bf16[256,256]{1,0:T(8,128)(2,1)S(1)}, u32[]{:S(2)}, u32[]{:S(2)}) collective-permute-start(bf16[256,256]{1,0:T(8,128)(2,1)S(1)} %get-tuple-element.49), channel_id=1, source_target_pairs={{0,12},{4,0},{8,4},{12,8},{1,13},{5,1},{9,5},{13,9},{2,14},{6,2},{... | collective-permute-start | bytes 393224 | tf_op jit(solution)/shard_map/ppermute | solution.py:265
  39.7 3.8 %collective-permute-done.11.refs_0_ = bf16[256,256]{1,0:T(8,128)(2,1)S(1)} collective-permute-done((bf16[256,256]{1,0:T(8,128)(2,1)S(1)}, bf16[256,256]{1,0:T(8,128)(2,1)S(1)}, u32[]{:S(2)}, u32[]{:S(2)}) %collective-permute-start.11) | collective-permute-done | bytes 131104 | tf_op jit(solution)/shard_map/ppermute | solution.py:265
  43.4 4.8 %collective-permute-done.12.refs_1_ = bf16[256,256]{1,0:T(8,128)(2,1)S(1)} collective-permute-done((bf16[256,256]{1,0:T(8,128)(2,1)S(1)}, bf16[256,256]{1,0:T(8,128)(2,1)S(1)}, u32[]{:S(2)}, u32[]{:S(2)}) %collective-permute-start.12) | collective-permute-done | bytes 131104 | tf_op jit(solution)/shard_map/ppermute | solution.py:265
  48.3 0.0 collective-permute-done.13.refs_2_
  48.3 0.1 phi_sum.1.own
  48.3 1.6 %collective-permute-start.14 = (bf16[256,256]{1,0:T(8,128)(2,1)S(1)}, bf16[256,256]{1,0:T(8,128)(2,1)S(1)}, u32[]{:S(2)}, u32[]{:S(2)}) collective-permute-start(bf16[256,256]{1,0:T(8,128)(2,1)S(1)} %phi_sum.1.own), channel_id=1, source_target_pairs={{0,2},{2,0},{1,3},{3,1},{4,6},{6,4},{5,7},{7,5},{8,10},{10,8},{9,1... | collective-permute-start | bytes 393224 | tf_op jit(solution)/shard_map/ppermute | solution.py:272
  49.9 0.7 %gather_fusion = s32[128,2,8]{2,0,1:T(8,128)S(1)} fusion(s32[2,8,8]{2,1,0:T(8,128)S(1)} %copy-done, s32[1024]{0:T(1024)S(1)} %pad_clamp_fusion), kind=kCustom, calls=%fused_computation | custom fusion | bytes 16896 | tf_op jit(solution)/shard_map/jit(_take)/gather | solution.py:377
  50.7 2.7 %collective-permute-done.14.refs_0_ = bf16[256,256]{1,0:T(8,128)(2,1)S(1)} collective-permute-done((bf16[256,256]{1,0:T(8,128)(2,1)S(1)}, bf16[256,256]{1,0:T(8,128)(2,1)S(1)}, u32[]{:S(2)}, u32[]{:S(2)}) %collective-permute-start.14) | collective-permute-done | bytes 131104 | tf_op jit(solution)/shard_map/ppermute | solution.py:272
  53.4 0.1 collective-permute-start.15
  53.5 0.1 convert_bitcast_fusion
  53.6 0.1 copy.10
  53.7 0.2 copy.11.keep
  53.9 0.9 %collective-permute-done.15.theirs_ref = bf16[256,256]{1,0:T(8,128)(2,1)S(1)} collective-permute-done((bf16[256,256]{1,0:T(8,128)(2,1)S(1)}, bf16[256,256]{1,0:T(8,128)(2,1)S(1)}, u32[]{:S(2)}, u32[]{:S(2)}) %collective-permute-start.15) | collective-permute-done | bytes 131104 | tf_op jit(solution)/shard_map/ppermute | solution.py:53
  54.8 1.4 %finish.1 = f32[2,128,512]{2,1,0:T(8,128)} custom-call(s32[4]{0:T(128)S(1)} %pad_add_fusion.info, bf16[256,256]{1,0:T(8,128)(2,1)S(1)} %eta_sum.1.mine_ref, bf16[256,256]{1,0:T(8,128)(2,1)S(1)} %collective-permute-done.15.theirs_ref, f32[2,128,512]{2,1,0:T(8,128)S(1)} %copy.11.keep), custom_call_target="tpu_custom_call" | custom-call | bytes 1310736 | tf_op jit(solution)/shard_map/finish/pallas_call | solution.py:21
  (8 shorter events, 0.1 us)
Async XLA Ops:
  0.6 8.6 %copy-start.5 = (bf16[1,1,12,128,128]{4,3,2,1,0:T(8,128)(2,1)S(1)}, bf16[1,1,12,128,128]{4,3,2,1,0:T(8,128)(2,1)}, u32[]{:S(2)}) copy-start(bf16[1,1,12,128,128]{4,3,2,1,0:T(8,128)(2,1)} %param.10) | copy-start | bytes 1179652
  2.3 10.4 %collective-permute-start = (bf16[144,512]{1,0:T(8,128)(2,1)S(1)}, bf16[144,512]{1,0:T(8,128)(2,1)S(1)}, u32[]{:S(2)}, u32[]{:S(2)}) collective-permute-start(bf16[144,512]{1,0:T(8,128)(2,1)S(1)} %concatenate.3), channel_id=1, source_target_pairs={{0,4},{4,8},{8,12},{12,0},{1,5},{5,9},{9,13},{13,1},{2,6},{6,10},{... | collective-permute-start | bytes 442376 | tf_op jit(solution)/shard_map/ppermute | solution.py:58
  5.4 8.5 %collective-permute-start.1 = (bf16[144,512]{1,0:T(8,128)(2,1)S(1)}, bf16[144,512]{1,0:T(8,128)(2,1)S(1)}, u32[]{:S(2)}, u32[]{:S(2)}) collective-permute-start(bf16[144,512]{1,0:T(8,128)(2,1)S(1)} %concatenate.3), channel_id=1, source_target_pairs={{0,12},{4,0},{8,4},{12,8},{1,13},{5,1},{9,5},{13,9},{2,14},{6,2},{... | collective-permute-start | bytes 442376 | tf_op jit(solution)/shard_map/ppermute | solution.py:57
  7.5 6.4 %collective-permute-start.2 = (bf16[144,512]{1,0:T(8,128)(2,1)S(1)}, bf16[144,512]{1,0:T(8,128)(2,1)S(1)}, u32[]{:S(2)}, u32[]{:S(2)}) collective-permute-start(bf16[144,512]{1,0:T(8,128)(2,1)S(1)} %concatenate.3), channel_id=1, source_target_pairs={{0,2},{2,0},{1,3},{3,1},{4,6},{6,4},{5,7},{7,5},{8,10},{10,8},{9,1... | collective-permute-start | bytes 442376 | tf_op jit(solution)/shard_map/ppermute | solution.py:60
  9.1 0.7 %copy-start = (s32[2,8,8]{2,1,0:T(8,128)S(1)}, s32[2,8,8]{2,1,0:T(8,128)}, u32[]{:S(2)}) copy-start(s32[2,8,8]{2,1,0:T(8,128)} %mask.3) | copy-start | bytes 1540
  9.2 0.7 %copy-start.6 = (s32[1,1,12]{2,1,0:T(1,128)S(1)}, s32[1,1,12]{2,1,0:T(1,128)}, u32[]{:S(2)}) copy-start(s32[1,1,12]{2,1,0:T(1,128)} %param.11) | copy-start | bytes 148
  9.2 0.7 %copy-start.7 = (s32[1,1,12]{2,1,0:T(1,128)S(1)}, s32[1,1,12]{2,1,0:T(1,128)}, u32[]{:S(2)}) copy-start(s32[1,1,12]{2,1,0:T(1,128)} %param.12) | copy-start | bytes 148
  9.9 1.2 %copy-start.1 = (bf16[2,512,512]{2,1,0:T(8,128)(2,1)S(1)}, bf16[2,512,512]{2,1,0:T(8,128)(2,1)}, u32[]{:S(2)}) copy-start(bf16[2,512,512]{2,1,0:T(8,128)(2,1)} %weights.3) | copy-start | bytes 3145732
  11.1 2.8 %copy-start.3 = (bf16[1,1,256,512]{3,2,1,0:T(8,128)(2,1)S(1)}, bf16[1,1,256,512]{3,2,1,0:T(8,128)(2,1)}, u32[]{:S(2)}) copy-start(bf16[1,1,256,512]{3,2,1,0:T(8,128)(2,1)} %param.8) | copy-start | bytes 786436
  14.4 1.6 %collective-permute-start.3 = (bf16[256,512]{1,0:T(8,128)(2,1)S(1)}, bf16[256,512]{1,0:T(8,128)(2,1)S(1)}, u32[]{:S(2)}, u32[]{:S(2)}) collective-permute-start(bf16[256,512]{1,0:T(8,128)(2,1)S(1)} %get-tuple-element.28), channel_id=1, source_target_pairs={{0,1},{1,0},{2,3},{3,2},{4,5},{5,4},{6,7},{7,6},{8,9},{9,8},{10,11... | collective-permute-start | bytes 786440 | tf_op jit(solution)/shard_map/ppermute | solution.py:53
  16.1 8.2 %collective-permute-start.4 = (bf16[128,512]{1,0:T(8,128)(2,1)S(1)}, bf16[128,512]{1,0:T(8,128)(2,1)S(1)}, u32[]{:S(2)}, u32[]{:S(2)}) collective-permute-start(bf16[128,512]{1,0:T(8,128)(2,1)S(1)} %edge.1), channel_id=1, source_target_pairs={{0,4},{4,8},{8,12},{12,0},{1,5},{5,9},{9,13},{13,1},{2,6},{6,10},{... | collective-permute-start | bytes 393224 | tf_op jit(solution)/shard_map/ppermute | solution.py:58
  17.3 8.1 %collective-permute-start.5 = (bf16[128,512]{1,0:T(8,128)(2,1)S(1)}, bf16[128,512]{1,0:T(8,128)(2,1)S(1)}, u32[]{:S(2)}, u32[]{:S(2)}) collective-permute-start(bf16[128,512]{1,0:T(8,128)(2,1)S(1)} %edge.1), channel_id=1, source_target_pairs={{0,12},{4,0},{8,4},{12,8},{1,13},{5,1},{9,5},{13,9},{2,14},{6,2},{... | collective-permute-start | bytes 393224 | tf_op jit(solution)/shard_map/ppermute | solution.py:57
  19.9 5.4 %collective-permute-start.6 = (bf16[128,512]{1,0:T(8,128)(2,1)S(1)}, bf16[128,512]{1,0:T(8,128)(2,1)S(1)}, u32[]{:S(2)}, u32[]{:S(2)}) collective-permute-start(bf16[128,512]{1,0:T(8,128)(2,1)S(1)} %edge.1), channel_id=1, source_target_pairs={{0,2},{2,0},{1,3},{3,1},{4,6},{6,4},{5,7},{7,5},{8,10},{10,8},{9,1... | collective-permute-start | bytes 393224 | tf_op jit(solution)/shard_map/ppermute | solution.py:60
  25.3 1.2 %copy-start.2 = (bf16[2,512,512]{2,1,0:T(8,128)(2,1)S(1)}, bf16[2,512,512]{2,1,0:T(8,128)(2,1)}, u32[]{:S(2)}) copy-start(bf16[2,512,512]{2,1,0:T(8,128)(2,1)} %weights.3) | copy-start | bytes 3145732
  26.3 1.6 %copy-start.4 = (bf16[1,1,256,512]{3,2,1,0:T(8,128)(2,1)S(1)}, bf16[1,1,256,512]{3,2,1,0:T(8,128)(2,1)}, u32[]{:S(2)}) copy-start(bf16[1,1,256,512]{3,2,1,0:T(8,128)(2,1)} %param.9) | copy-start | bytes 786436
  26.3 1.6 %collective-permute-start.7 = (bf16[256,512]{1,0:T(8,128)(2,1)S(1)}, bf16[256,512]{1,0:T(8,128)(2,1)S(1)}, u32[]{:S(2)}, u32[]{:S(2)}) collective-permute-start(bf16[256,512]{1,0:T(8,128)(2,1)S(1)} %get-tuple-element.32), channel_id=1, source_target_pairs={{0,1},{1,0},{2,3},{3,2},{4,5},{5,4},{6,7},{7,6},{8,9},{9,8},{10,11... | collective-permute-start | bytes 786440 | tf_op jit(solution)/shard_map/ppermute | solution.py:53
  29.8 1.5 %collective-permute-start.8 = (bf16[256,512]{1,0:T(8,128)(2,1)S(1)}, bf16[256,512]{1,0:T(8,128)(2,1)S(1)}, u32[]{:S(2)}, u32[]{:S(2)}) collective-permute-start(bf16[256,512]{1,0:T(8,128)(2,1)S(1)} %get-tuple-element.36.dx), channel_id=1, source_target_pairs={{0,1},{1,0},{2,3},{3,2},{4,5},{5,4},{6,7},{7,6},{8,9},{9,8},{10,11... | collective-permute-start | bytes 786440 | tf_op jit(solution)/shard_map/ppermute | solution.py:53
  30.8 2.3 %collective-permute-start.10 = (bf16[512,256]{1,0:T(8,128)(2,1)S(1)}, bf16[512,256]{1,0:T(8,128)(2,1)S(1)}, u32[]{:S(2)}, u32[]{:S(2)}) collective-permute-start(bf16[512,256]{1,0:T(8,128)(2,1)S(1)} %get-tuple-element.45), channel_id=1, source_target_pairs={{0,1},{1,0},{2,3},{3,2},{4,5},{5,4},{6,7},{7,6},{8,9},{9,8},{10,11... | collective-permute-start | bytes 786440 | tf_op jit(solution)/shard_map/ppermute | solution.py:53
  32.9 1.6 %collective-permute-start.9 = (bf16[512,256]{1,0:T(8,128)(2,1)S(1)}, bf16[512,256]{1,0:T(8,128)(2,1)S(1)}, u32[]{:S(2)}, u32[]{:S(2)}) collective-permute-start(bf16[512,256]{1,0:T(8,128)(2,1)S(1)} %get-tuple-element.41), channel_id=1, source_target_pairs={{0,1},{1,0},{2,3},{3,2},{4,5},{5,4},{6,7},{7,6},{8,9},{9,8},{10,11... | collective-permute-start | bytes 786440 | tf_op jit(solution)/shard_map/ppermute | solution.py:53
  35.1 8.3 %collective-permute-start.11 = (bf16[256,256]{1,0:T(8,128)(2,1)S(1)}, bf16[256,256]{1,0:T(8,128)(2,1)S(1)}, u32[]{:S(2)}, u32[]{:S(2)}) collective-permute-start(bf16[256,256]{1,0:T(8,128)(2,1)S(1)} %get-tuple-element.47), channel_id=1, source_target_pairs={{0,4},{4,8},{8,12},{12,0},{1,5},{5,9},{9,13},{13,1},{2,6},{6,10},{... | collective-permute-start | bytes 393224 | tf_op jit(solution)/shard_map/ppermute | solution.py:265
  35.9 12.4 %collective-permute-start.12 = (bf16[256,256]{1,0:T(8,128)(2,1)S(1)}, bf16[256,256]{1,0:T(8,128)(2,1)S(1)}, u32[]{:S(2)}, u32[]{:S(2)}) collective-permute-start(bf16[256,256]{1,0:T(8,128)(2,1)S(1)} %get-tuple-element.48), channel_id=1, source_target_pairs={{0,8},{4,12},{8,0},{12,4},{1,9},{5,13},{9,1},{13,5},{2,10},{6,14},... | collective-permute-start | bytes 393224 | tf_op jit(solution)/shard_map/ppermute | solution.py:265
  37.8 10.5 %collective-permute-start.13 = (bf16[256,256]{1,0:T(8,128)(2,1)S(1)}, bf16[256,256]{1,0:T(8,128)(2,1)S(1)}, u32[]{:S(2)}, u32[]{:S(2)}) collective-permute-start(bf16[256,256]{1,0:T(8,128)(2,1)S(1)} %get-tuple-element.49), channel_id=1, source_target_pairs={{0,12},{4,0},{8,4},{12,8},{1,13},{5,1},{9,5},{13,9},{2,14},{6,2},{... | collective-permute-start | bytes 393224 | tf_op jit(solution)/shard_map/ppermute | solution.py:265
  48.3 5.0 %collective-permute-start.14 = (bf16[256,256]{1,0:T(8,128)(2,1)S(1)}, bf16[256,256]{1,0:T(8,128)(2,1)S(1)}, u32[]{:S(2)}, u32[]{:S(2)}) collective-permute-start(bf16[256,256]{1,0:T(8,128)(2,1)S(1)} %phi_sum.1.own), channel_id=1, source_target_pairs={{0,2},{2,0},{1,3},{3,1},{4,6},{6,4},{5,7},{7,5},{8,10},{10,8},{9,1... | collective-permute-start | bytes 393224 | tf_op jit(solution)/shard_map/ppermute | solution.py:272
  53.4 1.4 %collective-permute-start.15 = (bf16[256,256]{1,0:T(8,128)(2,1)S(1)}, bf16[256,256]{1,0:T(8,128)(2,1)S(1)}, u32[]{:S(2)}, u32[]{:S(2)}) collective-permute-start(bf16[256,256]{1,0:T(8,128)(2,1)S(1)} %eta_sum.1.mine_ref), channel_id=1, source_target_pairs={{0,1},{1,0},{2,3},{3,2},{4,5},{5,4},{6,7},{7,6},{8,9},{9,8},{10,11... | collective-permute-start | bytes 393224 | tf_op jit(solution)/shard_map/ppermute | solution.py:53

commit v3 on v2

v3 whole, which is shorter than its diff:
```python
import functools

import jax
import jax.numpy as jnp
from jax import lax
from jax.experimental import pallas as pl
from jax.experimental.pallas import tpu as pltpu
from jax.sharding import PartitionSpec as P

BF16 = jnp.bfloat16
F32 = jnp.float32
VMEM = pl.BlockSpec(memory_space=pltpu.VMEM)
FAR = pl.BlockSpec(memory_space=pltpu.HBM)
DEAD = 2.0**100


def call(kernel, ins, outs, scratch=(), flops=0, name=None, far=False):
    moved = sum(a.size * a.dtype.itemsize for a in ins)
    moved += sum(a.size * a.dtype.itemsize for a in outs)
    if far:
        ins = [pltpu.with_memory_space_constraint(a, pltpu.HBM) for a in ins]
    return pl.pallas_call(
        kernel,
        out_shape=outs,
        in_specs=[FAR if far else VMEM] * len(ins),
        out_specs=[VMEM] * len(outs),
        scratch_shapes=list(scratch),
        compiler_params=pltpu.CompilerParams(vmem_limit_bytes=32 << 20),
        cost_estimate=pl.CostEstimate(flops=flops, bytes_accessed=moved, transcendentals=0),
        name=name,
    )(*ins)


def shaped(shape, dtype):
    return jax.ShapeDtypeStruct(shape, dtype)


def dot(a, b, contract=((1,), (0,))):
    return lax.dot_general(a, b, (contract, ((), ())), preferred_element_type=F32)


def ring(axis, step, periodic):
    count = lax.axis_size(axis)
    pairs = [(i, i + step) for i in range(count) if 0 <= i + step < count]
    if periodic:
        pairs = [(i, (i + step) % count) for i in range(count)]
    return pairs


def swap_half(value):
    return lax.ppermute(value, "half", [(0, 1), (1, 0)])


def to_neighbours(low_phi, high_phi, low_eta, high_eta):
    from_high = lax.ppermute(low_phi, "phi", ring("phi", -1, True))
    from_low = lax.ppermute(high_phi, "phi", ring("phi", 1, True))
    if lax.axis_size("eta") == 2:
        return [from_low, from_high, lax.ppermute(low_eta, "eta", [(0, 1), (1, 0)])]
    from_upper = lax.ppermute(low_eta, "eta", ring("eta", -1, False))
    from_lower = lax.ppermute(high_eta, "eta", ring("eta", 1, False))
    return [from_low, from_high, from_lower, from_upper]


def keep_full(mask, side):
    grid = mask.shape[0]
    width = grid * side
    spread = (
        lax.broadcasted_iota(jnp.int32, (width, grid), 0) // side
        == lax.broadcasted_iota(jnp.int32, (width, grid), 1)
    ).astype(F32)
    return dot(dot(spread, mask.astype(F32)), spread, ((1,), (1,)))


def build_kernel(own, pair, *refs):
    srcs, (m_out, w_out), bufs = refs[:5], refs[5:7], refs[7:12]
    acc, sem = refs[12:]
    src, dst, tbuf, kbuf, wbuf = bufs
    copies = [
        pltpu.make_async_copy(a.at[0] if i == 4 else a, b, sem.at[i])
        for i, (a, b) in enumerate(zip(srcs, bufs))
    ]
    for copy in copies:
        copy.start()
    slots, block = tbuf.shape[0], tbuf.shape[1]
    acc[...] = jnp.zeros_like(acc)
    half = lax.axis_index("half")
    eta = lax.axis_index("eta")
    for copy in copies[:3]:
        copy.wait()
    for t in range(slots):
        source = src[t]
        target = dst[t]
        column = jnp.where(source > own + 2, own + 2, source) if pair else source
        live = target >= 0
        if pair:
            outside = ((source == own + 2) & (eta == 0)) | ((source == own + 3) & (eta == 1))
            live = live & jnp.logical_not(outside)
        row = jnp.where(target >= half * own, target - half * own, target - half * own + 2 * own)

        @pl.when(live)
        def _():
            rows = pl.ds(pl.multiple_of(row * block, block), block)
            columns = pl.ds(pl.multiple_of(column * block, block), block)
            acc[rows, columns] += tbuf[t].astype(F32)

    m_out[...] = acc[...].astype(BF16)
    copies[3].wait()
    full = keep_full(kbuf[0], wbuf.shape[0] // kbuf.shape[1])
    copies[4].wait()
    w_out[...] = (wbuf[...].astype(F32) * full).astype(BF16)


def later_kernel(matrix, weights, mask, mt_out, w_out):
    mt_out[...] = matrix[...].T
    layers, width = weights.shape[0], weights.shape[1]
    for layer in range(1, layers):
        full = keep_full(mask[layer], width // mask.shape[1])
        w_out[layer - 1] = (weights[layer].astype(F32) * full).astype(BF16)


def gather_kernel(count, matrix, *refs):
    sources, (own_out, other_out) = refs[:count], refs[count:]
    rows = own_out.shape[0]
    stacked = jnp.concatenate([r[...] for r in sources], axis=0)
    total = dot(matrix[...], stacked).astype(BF16)
    own_out[...] = total[:rows]
    other_out[...] = total[rows:]


def mix(state, own, other):
    hfloat = state.astype(F32)
    return hfloat, (hfloat + own.astype(F32) + other.astype(F32)).astype(BF16)


def edge_kernel(count, state, own, other, out):
    block, width = out.shape
    mixed = mix(state[:block, :], own[:block, :], other[:block, :])[1].astype(F32)
    row = lax.broadcasted_iota(jnp.int32, (block, width), 0)
    out[...] = jnp.where(row < count[:1, :1], mixed, DEAD).astype(BF16)


def read_rim(ref):
    value = ref[...].astype(F32)
    live = value < 0.5 * DEAD
    return live.astype(F32), jnp.where(live, value, 0.0).astype(BF16)


def live_rows(count, rows, width):
    row = lax.broadcasted_iota(jnp.int32, (rows, width), 0)
    return (row < count[:1, :1]).astype(F32)


def forward_kernel(count, state, own, other, weight, x_out, new_out, slope_out):
    rows, width = x_out.shape
    hfloat, mixed = mix(state[...], own[...], other[...])
    x_out[...] = mixed
    pre = dot(mixed, weight[...])
    live = live_rows(count, rows, width)
    sigma = jax.nn.sigmoid(pre)
    new_out[...] = (live * (hfloat + pre * sigma)).astype(BF16)
    slope_out[...] = live * sigma * (1.0 + pre * (1.0 - sigma))


def rim_kernel(count, matrix, weight, new, *refs):
    starts, mixes = refs[:count], refs[count : 2 * count]
    own_out, other_out, slope_out = refs[2 * count :]
    block, width = mixes[0].shape
    rows = own_out.shape[0]
    rims = [read_rim(r) for r in mixes]
    pre_all = dot(jnp.concatenate([r[1] for r in rims], axis=0), weight[...])
    parts = [new[...]]
    for i in range(count):
        pre = pre_all[i * block : (i + 1) * block]
        live = rims[i][0]
        sigma = jax.nn.sigmoid(pre)
        hfloat = starts[i][...].astype(F32)
        parts.append((live * (hfloat + pre * sigma)).astype(BF16))
        slope_out[i * block : (i + 1) * block, :] = live * sigma * (1.0 + pre * (1.0 - sigma))
    total = dot(matrix[...], jnp.concatenate(parts, axis=0)).astype(BF16)
    own_out[...] = total[:rows]
    other_out[...] = total[rows:]


def last_kernel(count, state, own, other, weight, cot, x_out, final_out, dz_out, dx_out):
    rows, width = x_out.shape
    hfloat, mixed = mix(state[...], own[...], other[...])
    x_out[...] = mixed
    pre = dot(mixed, weight[...])
    live = live_rows(count, rows, width)
    sigma = jax.nn.sigmoid(pre)
    delta = cot[...].astype(F32) * live * sigma * (1.0 + pre * (1.0 - sigma))
    delta = delta.astype(BF16)
    dz_out[...] = delta
    dx_out[...] = dot(delta, weight[...], ((1,), (1,))).astype(BF16)
    final_out[...] = (live * (hfloat + pre * sigma)).astype(BF16)


def split_columns(value, mine_out, theirs_out):
    middle = value.shape[1] // 2
    first = lax.axis_index("half") == 0
    left, right = value[:, :middle], value[:, middle:]
    mine_out[...] = jnp.where(first, left, right)
    theirs_out[...] = jnp.where(first, right, left).astype(BF16)


def grad_kernel(x, dz, mine_out, theirs_out):
    split_columns(dot(x[...], dz[...], ((0,), (0,))), mine_out, theirs_out)


def turn_kernel(x, *refs):
    rims = [read_rim(r)[1] for r in refs[:-1]]
    refs[-1][...] = jnp.concatenate([x[...]] + rims, axis=0).T


def back_kernel(mt, dx, dx_other, cot, slope, slope_rim, xt, mine_out, theirs_out):
    rows = dx.shape[0]
    whole = jnp.concatenate([dx[...], dx_other[...]], axis=0)
    total = dot(mt[...], whole)
    upstream = cot[...].astype(F32) + dx[...].astype(F32) + total[:rows]
    delta = (upstream * slope[...]).astype(BF16)
    delta_rim = (total[rows:] * slope_rim[...]).astype(BF16)
    deltas = jnp.concatenate([delta, delta_rim], axis=0)
    split_columns(dot(xt[...], deltas), mine_out, theirs_out)


def fold_kernel(level, own, arrived, keep_out, send_out):
    parts = lax.axis_size("phi") >> level
    span = own.shape[0] // parts
    bit = lax.rem(lax.axis_index("phi") // (1 << level), 2)
    for pair in range(parts // 2):
        rows = slice(pair * span, (pair + 1) * span)
        for mine, out in ((bit, keep_out), (1 - bit, send_out)):
            place = pl.ds(pl.multiple_of((2 * pair + mine) * span, span), span)
            part = own[place, :] + arrived[place, :].astype(F32)
            out[rows, :] = part.astype(out.dtype)


def sum_kernel(own, *refs):
    total = own[...].astype(F32)
    for r in refs[:-1]:
        total = total + r[...].astype(F32)
    refs[-1][...] = total.astype(BF16)


def finish_kernel(*refs):
    keep, out = refs[-2:]
    layers, rows, width = out.shape
    middle = width // 2
    first = lax.axis_index("half") == 0
    for layer in range(layers):
        mine, theirs = refs[2 * layer][...].astype(F32), refs[2 * layer + 1][...].astype(F32)
        kept = keep[layer]
        out[layer, :, :middle] = jnp.where(first, mine, theirs) * kept[:, :middle]
        out[layer, :, middle:] = jnp.where(first, theirs, mine) * kept[:, middle:]


def phi_share(mine, theirs):
    arrived = swap_half(theirs)
    parts = lax.axis_size("phi")
    if parts & (parts - 1):
        total = (mine + arrived.astype(F32)).astype(BF16)
        return lax.psum_scatter(total, "phi", scatter_dimension=0, tiled=True)
    own = mine
    for level in range(parts.bit_length() - 1):
        shape = (own.shape[0] // 2, own.shape[1])
        own, send = call(
            functools.partial(fold_kernel, level),
            (own, arrived),
            [shaped(shape, F32), shaped(shape, BF16)],
            name="fold",
        )
        arrived = lax.ppermute(send, "phi", [(i, i ^ (1 << level)) for i in range(parts)])
    return call(sum_kernel, (own, arrived), [shaped(own.shape, BF16)], name="phi_sum")[0]


def eta_sum(share):
    if lax.axis_size("eta") == 2:
        arrived = lax.ppermute(share, "eta", [(0, 1), (1, 0)])
        return call(sum_kernel, (share, arrived), [shaped(share.shape, BF16)], name="eta_sum")[0]
    gathered = lax.all_gather(share, "eta", axis=0)
    return jnp.sum(gathered.astype(F32), axis=0).astype(BF16)


def body(feats, cotangent, tiles, tile_src, tile_dst, weights, mask, counts):
    rows, width = feats.shape[2], feats.shape[3]
    block = tiles.shape[3]
    own = rows // block
    pair = lax.axis_size("eta") == 2
    rims = 3 if pair else 4
    layers, grid = weights.shape[0], mask.shape[1]
    side = width // grid
    live_here = counts[0, 0] - lax.axis_index("half").astype(jnp.int32) * rows
    count = jnp.full((8, 128), live_here, jnp.int32)
    state = feats[0, 0]
    cot = cotangent[0, 0]
    height, depth = 2 * rows, rows + rims * block

    edge = state[:block]
    starts = to_neighbours(edge, edge, edge, edge)
    matrix, masked0 = call(
        functools.partial(build_kernel, own, pair),
        (tile_src[0, 0], tile_dst[0, 0], tiles[0, 0], mask, weights),
        [shaped((height, depth), BF16), shaped((width, width), BF16)],
        [
            pltpu.SMEM(tile_src.shape[2:], jnp.int32),
            pltpu.SMEM(tile_dst.shape[2:], jnp.int32),
            pltpu.VMEM(tiles.shape[2:], BF16),
            pltpu.VMEM(mask.shape, jnp.int32),
            pltpu.VMEM((width, width), BF16),
            pltpu.VMEM((height, depth), F32),
            pltpu.SemaphoreType.DMA((5,)),
        ],
        10_000_000,
        "build",
        True,
    )
    agg_flops = 2 * height * depth * width
    dense_flops = 2 * rows * width * width
    wide = shaped((rows, width), BF16)

    own_part, other_part = call(
        functools.partial(gather_kernel, 1 + rims),
        (matrix, state, *starts),
        [wide, wide],
        flops=agg_flops,
        name="gather",
    )
    received = swap_half(other_part)
    edge = call(
        edge_kernel, (count, state, own_part, received), [shaped((block, width), BF16)], name="edge"
    )[0]
    mixes = to_neighbours(edge, edge, edge, edge)
    x0, new, slope0 = call(
        forward_kernel,
        (count, state, own_part, received, masked0),
        [wide, wide, shaped((rows, width), F32)],
        flops=dense_flops,
        name="forward",
    )
    matrix_t, masked = call(
        later_kernel,
        (matrix, weights, mask),
        [shaped((depth, height), BF16), shaped((layers - 1, width, width), BF16)],
        flops=10_000_000,
        name="later",
    )
    own_part, other_part, slope_rim = call(
        functools.partial(rim_kernel, rims),
        (matrix, masked0, new, *starts, *mixes),
        [wide, wide, shaped((rims * block, width), F32)],
        flops=agg_flops + 2 * dense_flops,
        name="rim",
    )
    received = swap_half(other_part)
    x1, final, dz1, dx = call(
        last_kernel,
        (count, new, own_part, received, masked[0], cot),
        [wide, wide, wide, wide],
        flops=2 * dense_flops,
        name="last",
    )
    dx_other = swap_half(dx)
    halves = [shaped((width, width // 2), F32), shaped((width, width // 2), BF16)]
    mine1, theirs1 = call(
        grad_kernel, (x1, dz1), halves, flops=dense_flops, name="grad"
    )
    share1 = phi_share(mine1, theirs1)
    xt = call(
        turn_kernel, (x0, *mixes), [shaped((width, depth), BF16)], flops=1_000_000, name="turn"
    )[0]
    mine0, theirs0 = call(
        back_kernel,
        (matrix_t, dx, dx_other, cot, slope0, slope_rim, xt),
        halves,
        flops=2 * agg_flops,
        name="back",
    )
    share0 = phi_share(mine0, theirs0)
    total1 = eta_sum(share1)
    other1 = swap_half(total1)
    total0 = eta_sum(share0)
    other0 = swap_half(total0)

    span = width // lax.axis_size("phi")
    row_ids = (lax.axis_index("phi") * span + jnp.arange(span, dtype=jnp.int32)) // side
    chosen = jnp.take(mask, row_ids, axis=1)
    keep = jnp.broadcast_to(chosen[..., None], (layers, span, grid, side)).reshape(
        layers, span, width
    )
    result = call(
        finish_kernel,
        (total0, other0, total1, other1, keep.astype(F32)),
        [shaped((layers, span, width), F32)],
        name="finish",
    )[0]
    return final[None, None], result


def solution(mesh):
    in_specs = (
        P(("group", "phi"), "eta", "half", None),
        P(("group", "phi"), "eta", "half", None),
        P(("group", "phi"), "eta", "half", None, None),
        P(("group", "phi"), "eta", "half"),
        P(("group", "phi"), "eta", "half"),
        P(),
        P(),
        P(("group", "phi"), "eta"),
    )
    out_specs = (P(("group", "phi"), "eta", "half", None), P("group", "phi", None))
    return jax.shard_map(body, mesh=mesh, in_specs=in_specs, out_specs=out_specs, check_vma=False)
```

time: 56.6 us -> 52.5 us (0.928)
  Pallas kernels: 11 us -> 8 us
  starting transfers between devices: 19.3 us -> 21.6 us
  local copies, waits for them, and re-layouts: 4.03 us -> 2.13 us
  waiting for transfers between devices: 20.2 us -> 18.9 us
    pallas_call x13 -> x19, Pallas kernels: 11 us -> 8 us  [call(): pl.pallas_call(kernel, out_shape=outs, in_specs=[FAR if far else VMEM] *...]
    unnamed x16 -> x8, local copies, waits for them, and re-layouts: 2.06 us -> 0.17 us
    ppermute x3 -> x4, waiting for transfers between devices: 8.6 us -> 6.9 us  [phi_share(): lax.ppermute(send, 'phi', [(i, i ^ 1 << level) for i in range(parts)])]
    ppermute x1 -> x2, starting transfers between devices: 1.56 us -> 3.09 us  [eta_sum(): arrived = lax.ppermute(share, 'eta', [(0, 1), (1, 0)])]
    ppermute x2, waiting for transfers between devices: 1.85 us -> 3.35 us  [to_neighbours(): from_low = lax.ppermute(high_phi, 'phi', ring('phi', 1, True))]
    ppermute x6 -> x7, waiting for transfers between devices: 4.91 us -> 3.58 us  [swap_half(): return lax.ppermute(value, 'half', [(0, 1), (1, 0)])]
    ppermute x3 -> x4, starting transfers between devices: 4.53 us -> 5.29 us  [phi_share(): lax.ppermute(send, 'phi', [(i, i ^ 1 << level) for i in range(parts)])]
    ppermute x1 -> x2, waiting for transfers between devices: 2.69 us -> 2.67 us  [eta_sum(): arrived = lax.ppermute(share, 'eta', [(0, 1), (1, 0)])]
  transfers between devices with their start and end apart: 16 -> 19, of which waited for: 11 -> 15; matrix products, arithmetic and copies ran while one was open for 2% -> 2% of each run, Pallas kernels for 10% -> 8%
where the time goes in v3:
time: 52.5 us; the launch traced here: 52.3 us
  starting transfers between devices  21.6 us (41%)
  waiting for transfers between devices  18.9 us (36%)
  Pallas kernels  8 us (15%)
  local copies, waits for them, and re-layouts  2.13 us (4%)
  between operations  1.48 us (3%)
    pallas_call x19, Pallas kernels, call(): pl.pallas_call(kernel, out_shape=outs, in_specs=[FAR if far else VMEM] *...  8 us
    ppermute x4, waiting for transfers between devices, phi_share(): lax.ppermute(send, 'phi', [(i, i ^ 1 << level) for i in range(parts)])  6.9 us
    ppermute x4, starting transfers between devices, phi_share(): lax.ppermute(send, 'phi', [(i, i ^ 1 << level) for i in range(parts)])  5.29 us
    ppermute x2, starting transfers between devices, to_neighbours(): from_high = lax.ppermute(low_phi, 'phi', ring('phi', -1, True))  4.79 us
    ppermute x2, starting transfers between devices, to_neighbours(): from_low = lax.ppermute(high_phi, 'phi', ring('phi', 1, True))  4.26 us
    ppermute x7, waiting for transfers between devices, swap_half(): return lax.ppermute(value, 'half', [(0, 1), (1, 0)])  3.58 us
    ppermute x2, waiting for transfers between devices, to_neighbours(): from_low = lax.ppermute(high_phi, 'phi', ring('phi', 1, True))  3.35 us
    ppermute x2, starting transfers between devices, to_neighbours(): return [from_low, from_high, lax.ppermute(low_eta, 'eta', [(0, 1), (1, 0)])]  3.14 us
  transfers between devices with their start and end apart: 19, of which 15 were waited for; matrix products, arithmetic and copies ran while one was open for 2% of the time, Pallas kernels for 8%

profile of v3, /device:TPU:0, one launch (start us, length us, event | category | flops | bytes accessed | tf_op | source)
XLA Modules:
  0.0 52.3 jit_solution(16585544922813878476)
XLA Ops:
  0.6 0.9 %slice_bitcast_fusion = bf16[128,512]{1,0:T(8,128)(2,1)S(1)} fusion(bf16[1,1,256,512]{3,2,1,0:T(8,128)(2,1)} %param.8), kind=kLoop, calls=%fused_computation.2 | loop fusion | bytes 262144 | tf_op jit(solution)/shard_map/slice | solution.py:298
  1.5 3.1 %collective-permute-start = (bf16[128,512]{1,0:T(8,128)(2,1)S(1)}, bf16[128,512]{1,0:T(8,128)(2,1)S(1)}, u32[]{:S(2)}, u32[]{:S(2)}) collective-permute-start(bf16[128,512]{1,0:T(8,128)(2,1)S(1)} %slice_bitcast_fusion), channel_id=1, source_target_pairs={{0,4},{4,8},{8,12},{12,0},{1,5},{5,9},{9,13},{13,1},{2,6},{6,10},{... | collective-permute-start | bytes 393224 | tf_op jit(solution)/shard_map/ppermute | solution.py:56
  4.6 2.1 %collective-permute-start.1 = (bf16[128,512]{1,0:T(8,128)(2,1)S(1)}, bf16[128,512]{1,0:T(8,128)(2,1)S(1)}, u32[]{:S(2)}, u32[]{:S(2)}) collective-permute-start(bf16[128,512]{1,0:T(8,128)(2,1)S(1)} %slice_bitcast_fusion), channel_id=1, source_target_pairs={{0,12},{4,0},{8,4},{12,8},{1,13},{5,1},{9,5},{13,9},{2,14},{6,2},{... | collective-permute-start | bytes 393224 | tf_op jit(solution)/shard_map/ppermute | solution.py:55
  6.7 1.6 %collective-permute-start.2 = (bf16[128,512]{1,0:T(8,128)(2,1)S(1)}, bf16[128,512]{1,0:T(8,128)(2,1)S(1)}, u32[]{:S(2)}, u32[]{:S(2)}) collective-permute-start(bf16[128,512]{1,0:T(8,128)(2,1)S(1)} %slice_bitcast_fusion), channel_id=1, source_target_pairs={{0,2},{2,0},{1,3},{3,1},{4,6},{6,4},{5,7},{7,5},{8,10},{10,8},{9,1... | collective-permute-start | bytes 393224 | tf_op jit(solution)/shard_map/ppermute | solution.py:58
  8.4 0.0 copy-start.2
  8.4 1.6 %build.1 = (bf16[512,640]{1,0:T(8,128)(2,1)S(1)}, bf16[512,512]{1,0:T(8,128)(2,1)S(1)}) custom-call(s32[12]{0:T(128)} %bitcast.24, s32[12]{0:T(128)} %bitcast.25, bf16[12,128,128]{2,1,0:T(8,128)(2,1)} %bitcast.23, s32[2,8,8]{2,1,0:T(8,128)} %mask.1, bf16[2,512,512]{2,1,0:T(8,128)(2,1)} %weights.1), custom_call_target="tpu_custom_call" | custom-call | flops 10000000 | bytes 2622048 | tf_op jit(solution)/shard_map/build/pallas_call | solution.py:22
  10.0 1.0 %collective-permute-done.refs_1_.refs_0_ = bf16[128,512]{1,0:T(8,128)(2,1)S(1)} collective-permute-done((bf16[128,512]{1,0:T(8,128)(2,1)S(1)}, bf16[128,512]{1,0:T(8,128)(2,1)S(1)}, u32[]{:S(2)}, u32[]{:S(2)}) %collective-permute-start) | collective-permute-done | bytes 131104 | tf_op jit(solution)/shard_map/ppermute | solution.py:56
  11.0 1.4 %collective-permute-done.1.refs_2_.refs_1_ = bf16[128,512]{1,0:T(8,128)(2,1)S(1)} collective-permute-done((bf16[128,512]{1,0:T(8,128)(2,1)S(1)}, bf16[128,512]{1,0:T(8,128)(2,1)S(1)}, u32[]{:S(2)}, u32[]{:S(2)}) %collective-permute-start.1) | collective-permute-done | bytes 131104 | tf_op jit(solution)/shard_map/ppermute | solution.py:55
  12.4 0.0 collective-permute-done.2.refs_3_.refs_2_
  12.4 0.0 copy-done.2
  12.4 0.6 %gather.8 = (bf16[256,512]{1,0:T(8,128)(2,1)S(1)}, bf16[256,512]{1,0:T(8,128)(2,1)S(1)}) custom-call(bf16[512,640]{1,0:T(8,128)(2,1)S(1)} %get-tuple-element.30.matrix, bf16[256,512]{1,0:T(8,128)(2,1)S(1)} %bitcast.16, bf16[128,512]{1,0:T(8,128)(2,1)S(1)} %collective-permute-done.refs_1_.refs_0_, ...), custom_call_target="tpu_custom_call" | custom-call | flops 335544320 | bytes 1835008 | tf_op jit(solution)/shard_map/gather/pallas_call | solution.py:22
  13.0 0.1 collective-permute-start.3
  13.7 0.9 %collective-permute-done.3.other = bf16[256,512]{1,0:T(8,128)(2,1)S(1)} collective-permute-done((bf16[256,512]{1,0:T(8,128)(2,1)S(1)}, bf16[256,512]{1,0:T(8,128)(2,1)S(1)}, u32[]{:S(2)}, u32[]{:S(2)}) %collective-permute-start.3) | collective-permute-done | bytes 262176 | tf_op jit(solution)/shard_map/ppermute | solution.py:51
  14.6 0.1 edge.1
  14.7 1.2 %collective-permute-start.4 = (bf16[128,512]{1,0:T(8,128)(2,1)S(1)}, bf16[128,512]{1,0:T(8,128)(2,1)S(1)}, u32[]{:S(2)}, u32[]{:S(2)}) collective-permute-start(bf16[128,512]{1,0:T(8,128)(2,1)S(1)} %edge.1), channel_id=1, source_target_pairs={{0,4},{4,8},{8,12},{12,0},{1,5},{5,9},{9,13},{13,1},{2,6},{6,10},{... | collective-permute-start | bytes 393224 | tf_op jit(solution)/shard_map/ppermute | solution.py:56
  15.9 2.7 %collective-permute-start.5 = (bf16[128,512]{1,0:T(8,128)(2,1)S(1)}, bf16[128,512]{1,0:T(8,128)(2,1)S(1)}, u32[]{:S(2)}, u32[]{:S(2)}) collective-permute-start(bf16[128,512]{1,0:T(8,128)(2,1)S(1)} %edge.1), channel_id=1, source_target_pairs={{0,12},{4,0},{8,4},{12,8},{1,13},{5,1},{9,5},{13,9},{2,14},{6,2},{... | collective-permute-start | bytes 393224 | tf_op jit(solution)/shard_map/ppermute | solution.py:55
  18.5 1.5 %collective-permute-start.6 = (bf16[128,512]{1,0:T(8,128)(2,1)S(1)}, bf16[128,512]{1,0:T(8,128)(2,1)S(1)}, u32[]{:S(2)}, u32[]{:S(2)}) collective-permute-start(bf16[128,512]{1,0:T(8,128)(2,1)S(1)} %edge.1), channel_id=1, source_target_pairs={{0,2},{2,0},{1,3},{3,1},{4,6},{6,4},{5,7},{7,5},{8,10},{10,8},{9,1... | collective-permute-start | bytes 393224 | tf_op jit(solution)/shard_map/ppermute | solution.py:58
  20.0 0.5 forward.1
  20.5 2.4 %collective-permute-done.4.refs_3_.refs_0_ = bf16[128,512]{1,0:T(8,128)(2,1)S(1)} collective-permute-done((bf16[128,512]{1,0:T(8,128)(2,1)S(1)}, bf16[128,512]{1,0:T(8,128)(2,1)S(1)}, u32[]{:S(2)}, u32[]{:S(2)}) %collective-permute-start.4) | collective-permute-done | bytes 131104 | tf_op jit(solution)/shard_map/ppermute | solution.py:56
  22.9 1.0 %collective-permute-done.5.refs_4_.refs_1_ = bf16[128,512]{1,0:T(8,128)(2,1)S(1)} collective-permute-done((bf16[128,512]{1,0:T(8,128)(2,1)S(1)}, bf16[128,512]{1,0:T(8,128)(2,1)S(1)}, u32[]{:S(2)}, u32[]{:S(2)}) %collective-permute-start.5) | collective-permute-done | bytes 131104 | tf_op jit(solution)/shard_map/ppermute | solution.py:55
  23.9 0.0 collective-permute-done.6.refs_5_.refs_2_
  23.9 0.0 copy-start
  23.9 0.0 copy-start.1
  23.9 1.0 %rim.1 = (bf16[256,512]{1,0:T(8,128)(2,1)S(1)}, bf16[256,512]{1,0:T(8,128)(2,1)S(1)}, f32[384,512]{1,0:T(8,128)S(1)}) custom-call(bf16[512,640]{1,0:T(8,128)(2,1)S(1)} %get-tuple-element.30.matrix, bf16[512,512]{1,0:T(8,128)(2,1)S(1)} %get-tuple-element.33.weight, bf16[256,512]{1,0:T(8,128)(2,1)S(1)} %get-tuple-element.34.new.state, ...), custom_call_target="tpu_custom_call" | custom-call | flops 603979776 | bytes 3538944 | tf_op jit(solution)/shard_map/rim/pallas_call | solution.py:22
  24.9 0.0 copy-start.3
  24.9 0.1 collective-permute-start.7
  25.0 0.0 copy-done
  25.0 0.2 copy-done.1
  25.2 0.4 later.1
  25.6 1.0 %collective-permute-done.7.other = bf16[256,512]{1,0:T(8,128)(2,1)S(1)} collective-permute-done((bf16[256,512]{1,0:T(8,128)(2,1)S(1)}, bf16[256,512]{1,0:T(8,128)(2,1)S(1)}, u32[]{:S(2)}, u32[]{:S(2)}) %collective-permute-start.7) | collective-permute-done | bytes 262176 | tf_op jit(solution)/shard_map/ppermute | solution.py:51
  26.5 0.0 copy-done.3
  26.5 1.3 %last.1 = (bf16[256,512]{1,0:T(8,128)(2,1)S(1)}, bf16[256,512]{1,0:T(8,128)(2,1)}, bf16[256,512]{1,0:T(8,128)(2,1)S(1)}, bf16[256,512]{1,0:T(8,128)(2,1)S(1)}) custom-call(s32[8,128]{1,0:T(8,128)S(1)} %broadcast_in_dim.22.count, bf16[256,512]{1,0:T(8,128)(2,1)S(1)} %get-tuple-element.34.new.state, bf16[256,512]{1,0:T(8,128)(2,1)S(1)} %get-tuple-element.35.own, ...), custom_call_target="tpu_custom_call" | custom-call | flops 268435456 | bytes 2625536 | tf_op jit(solution)/shard_map/last/pallas_call | solution.py:22
  27.8 0.1 collective-permute-start.8
  28.0 0.2 turn.1.xt
  28.2 0.3 grad.1
  28.5 0.4 collective-permute-start.14
  29.0 0.4 collective-permute-done.8.dx_other
  29.4 0.9 %back.1 = (f32[512,256]{1,0:T(8,128)S(1)}, bf16[512,256]{1,0:T(8,128)(2,1)S(1)}) custom-call(bf16[640,512]{1,0:T(8,128)(2,1)S(1)} %get-tuple-element.39.mt, bf16[256,512]{1,0:T(8,128)(2,1)S(1)} %get-tuple-element.40.dx, bf16[256,512]{1,0:T(8,128)(2,1)S(1)} %collective-permute-done.8.dx_other, bf16[256,512]{1,0:T(8,128)(2,1)S(1)} %bitcast.20, ...), custom_call_target="tpu_custom_call" | custom-call | flops 671088640 | bytes 4194304 | tf_op jit(solution)/shard_map/back/pallas_call | solution.py:22
  30.3 0.2 collective-permute-start.9
  30.5 0.0 collective-permute-done.14.arrived
  30.6 0.8 %collective-permute-start.15 = (bf16[256,256]{1,0:T(8,128)(2,1)S(1)}, bf16[256,256]{1,0:T(8,128)(2,1)S(1)}, u32[]{:S(2)}, u32[]{:S(2)}) collective-permute-start(bf16[256,256]{1,0:T(8,128)(2,1)S(1)} %get-tuple-element.55), channel_id=1, source_target_pairs={{0,4},{4,0},{8,12},{12,8},{1,5},{5,1},{9,13},{13,9},{2,6},{6,2},{1... | collective-permute-start | bytes 393224 | tf_op jit(solution)/shard_map/ppermute | solution.py:272
  31.4 0.5 %collective-permute-done.9.arrived = bf16[512,256]{1,0:T(8,128)(2,1)S(1)} collective-permute-done((bf16[512,256]{1,0:T(8,128)(2,1)S(1)}, bf16[512,256]{1,0:T(8,128)(2,1)S(1)}, u32[]{:S(2)}, u32[]{:S(2)}) %collective-permute-start.9) | collective-permute-done | bytes 262176 | tf_op jit(solution)/shard_map/ppermute | solution.py:51
  32.0 0.8 %collective-permute-start.10 = (bf16[256,256]{1,0:T(8,128)(2,1)S(1)}, bf16[256,256]{1,0:T(8,128)(2,1)S(1)}, u32[]{:S(2)}, u32[]{:S(2)}) collective-permute-start(bf16[256,256]{1,0:T(8,128)(2,1)S(1)} %get-tuple-element.47), channel_id=1, source_target_pairs={{0,4},{4,0},{8,12},{12,8},{1,5},{5,1},{9,13},{13,9},{2,6},{6,2},{1... | collective-permute-start | bytes 393224 | tf_op jit(solution)/shard_map/ppermute | solution.py:272
  32.8 4.2 %collective-permute-done.15.arrived = bf16[256,256]{1,0:T(8,128)(2,1)S(1)} collective-permute-done((bf16[256,256]{1,0:T(8,128)(2,1)S(1)}, bf16[256,256]{1,0:T(8,128)(2,1)S(1)}, u32[]{:S(2)}, u32[]{:S(2)}) %collective-permute-start.15) | collective-permute-done | bytes 131104 | tf_op jit(solution)/shard_map/ppermute | solution.py:272
  37.0 1.6 %collective-permute-start.16 = (bf16[128,256]{1,0:T(8,128)(2,1)S(1)}, bf16[128,256]{1,0:T(8,128)(2,1)S(1)}, u32[]{:S(2)}, u32[]{:S(2)}) collective-permute-start(bf16[128,256]{1,0:T(8,128)(2,1)S(1)} %get-tuple-element.57), channel_id=1, source_target_pairs={{0,8},{4,12},{8,0},{12,4},{1,9},{5,13},{9,1},{13,5},{2,10},{6,14},... | collective-permute-start | bytes 196616 | tf_op jit(solution)/shard_map/ppermute | solution.py:272
  38.6 0.6 %collective-permute-done.10.arrived = bf16[256,256]{1,0:T(8,128)(2,1)S(1)} collective-permute-done((bf16[256,256]{1,0:T(8,128)(2,1)S(1)}, bf16[256,256]{1,0:T(8,128)(2,1)S(1)}, u32[]{:S(2)}, u32[]{:S(2)}) %collective-permute-start.10) | collective-permute-done | bytes 131104 | tf_op jit(solution)/shard_map/ppermute | solution.py:272
  39.2 2.0 %collective-permute-start.11 = (bf16[128,256]{1,0:T(8,128)(2,1)S(1)}, bf16[128,256]{1,0:T(8,128)(2,1)S(1)}, u32[]{:S(2)}, u32[]{:S(2)}) collective-permute-start(bf16[128,256]{1,0:T(8,128)(2,1)S(1)} %get-tuple-element.49), channel_id=1, source_target_pairs={{0,8},{4,12},{8,0},{12,4},{1,9},{5,13},{9,1},{13,5},{2,10},{6,14},... | collective-permute-start | bytes 196616 | tf_op jit(solution)/shard_map/ppermute | solution.py:272
  41.3 0.7 %gather_fusion = s32[128,2,8]{2,0,1:T(8,128)S(1)} fusion(s32[2,8,8]{2,1,0:T(8,128)S(1)} %copy-done, s32[1024]{0:T(1024)S(1)} %pad_clamp_fusion), kind=kCustom, calls=%fused_computation | custom fusion | bytes 16896 | tf_op jit(solution)/shard_map/jit(_take)/gather | solution.py:386
  42.0 2.0 %collective-permute-done.16.refs_0_ = bf16[128,256]{1,0:T(8,128)(2,1)S(1)} collective-permute-done((bf16[128,256]{1,0:T(8,128)(2,1)S(1)}, bf16[128,256]{1,0:T(8,128)(2,1)S(1)}, u32[]{:S(2)}, u32[]{:S(2)}) %collective-permute-start.16) | collective-permute-done | bytes 65568 | tf_op jit(solution)/shard_map/ppermute | solution.py:272
  44.1 1.5 %collective-permute-start.17 = (bf16[128,256]{1,0:T(8,128)(2,1)S(1)}, bf16[128,256]{1,0:T(8,128)(2,1)S(1)}, u32[]{:S(2)}, u32[]{:S(2)}) collective-permute-start(bf16[128,256]{1,0:T(8,128)(2,1)S(1)} %phi_sum.3.own), channel_id=1, source_target_pairs={{0,2},{2,0},{1,3},{3,1},{4,6},{6,4},{5,7},{7,5},{8,10},{10,8},{9,1... | collective-permute-start | bytes 196616 | tf_op jit(solution)/shard_map/ppermute | solution.py:278
  45.6 0.1 collective-permute-done.11.refs_0_
  45.7 1.5 %collective-permute-start.12 = (bf16[128,256]{1,0:T(8,128)(2,1)S(1)}, bf16[128,256]{1,0:T(8,128)(2,1)S(1)}, u32[]{:S(2)}, u32[]{:S(2)}) collective-permute-start(bf16[128,256]{1,0:T(8,128)(2,1)S(1)} %phi_sum.2.own), channel_id=1, source_target_pairs={{0,2},{2,0},{1,3},{3,1},{4,6},{6,4},{5,7},{7,5},{8,10},{10,8},{9,1... | collective-permute-start | bytes 196616 | tf_op jit(solution)/shard_map/ppermute | solution.py:278
  47.3 1.5 %collective-permute-done.17.refs_0_ = bf16[128,256]{1,0:T(8,128)(2,1)S(1)} collective-permute-done((bf16[128,256]{1,0:T(8,128)(2,1)S(1)}, bf16[128,256]{1,0:T(8,128)(2,1)S(1)}, u32[]{:S(2)}, u32[]{:S(2)}) %collective-permute-start.17) | collective-permute-done | bytes 65568 | tf_op jit(solution)/shard_map/ppermute | solution.py:278
  48.8 0.1 collective-permute-start.18
  48.9 1.2 %collective-permute-done.12.refs_0_ = bf16[128,256]{1,0:T(8,128)(2,1)S(1)} collective-permute-done((bf16[128,256]{1,0:T(8,128)(2,1)S(1)}, bf16[128,256]{1,0:T(8,128)(2,1)S(1)}, u32[]{:S(2)}, u32[]{:S(2)}) %collective-permute-start.12) | collective-permute-done | bytes 65568 | tf_op jit(solution)/shard_map/ppermute | solution.py:278
  50.1 0.1 collective-permute-start.13
  50.2 0.1 convert_bitcast_fusion
  50.3 0.1 copy.10
  50.4 0.2 copy.11.refs_4_
  50.6 0.0 collective-permute-done.18.refs_3_
  50.6 0.8 %collective-permute-done.13.refs_1_ = bf16[128,256]{1,0:T(8,128)(2,1)S(1)} collective-permute-done((bf16[128,256]{1,0:T(8,128)(2,1)S(1)}, bf16[128,256]{1,0:T(8,128)(2,1)S(1)}, u32[]{:S(2)}, u32[]{:S(2)}) %collective-permute-start.13) | collective-permute-done | bytes 65568 | tf_op jit(solution)/shard_map/ppermute | solution.py:51
  51.4 0.9 %finish.1 = f32[2,128,512]{2,1,0:T(8,128)} custom-call(bf16[128,256]{1,0:T(8,128)(2,1)S(1)} %eta_sum.2.refs_0_, bf16[128,256]{1,0:T(8,128)(2,1)S(1)} %collective-permute-done.13.refs_1_, bf16[128,256]{1,0:T(8,128)(2,1)S(1)} %eta_sum.3.refs_2_, bf16[128,256]{1,0:T(8,128)(2,1)S(1)} %collective-permute-done.18.refs_3_, f32[2,128,512]{2,1,0:T(8,128)S(1)} %copy.11.refs_4_), custom_call_target="tpu_custom_call" | custom-call | bytes 1310720 | tf_op jit(solution)/shard_map/finish/pallas_call | solution.py:22
  (13 shorter events, 0.3 us)
Async XLA Ops:
  1.5 9.4 %collective-permute-start = (bf16[128,512]{1,0:T(8,128)(2,1)S(1)}, bf16[128,512]{1,0:T(8,128)(2,1)S(1)}, u32[]{:S(2)}, u32[]{:S(2)}) collective-permute-start(bf16[128,512]{1,0:T(8,128)(2,1)S(1)} %slice_bitcast_fusion), channel_id=1, source_target_pairs={{0,4},{4,8},{8,12},{12,0},{1,5},{5,9},{9,13},{13,1},{2,6},{6,10},{... | collective-permute-start | bytes 393224 | tf_op jit(solution)/shard_map/ppermute | solution.py:56
  4.6 7.8 %collective-permute-start.1 = (bf16[128,512]{1,0:T(8,128)(2,1)S(1)}, bf16[128,512]{1,0:T(8,128)(2,1)S(1)}, u32[]{:S(2)}, u32[]{:S(2)}) collective-permute-start(bf16[128,512]{1,0:T(8,128)(2,1)S(1)} %slice_bitcast_fusion), channel_id=1, source_target_pairs={{0,12},{4,0},{8,4},{12,8},{1,13},{5,1},{9,5},{13,9},{2,14},{6,2},{... | collective-permute-start | bytes 393224 | tf_op jit(solution)/shard_map/ppermute | solution.py:55
  6.7 5.7 %collective-permute-start.2 = (bf16[128,512]{1,0:T(8,128)(2,1)S(1)}, bf16[128,512]{1,0:T(8,128)(2,1)S(1)}, u32[]{:S(2)}, u32[]{:S(2)}) collective-permute-start(bf16[128,512]{1,0:T(8,128)(2,1)S(1)} %slice_bitcast_fusion), channel_id=1, source_target_pairs={{0,2},{2,0},{1,3},{3,1},{4,6},{6,4},{5,7},{7,5},{8,10},{10,8},{9,1... | collective-permute-start | bytes 393224 | tf_op jit(solution)/shard_map/ppermute | solution.py:58
  8.4 4.0 %copy-start.2 = (bf16[1,1,256,512]{3,2,1,0:T(8,128)(2,1)S(1)}, bf16[1,1,256,512]{3,2,1,0:T(8,128)(2,1)}, u32[]{:S(2)}) copy-start(bf16[1,1,256,512]{3,2,1,0:T(8,128)(2,1)} %param.8) | copy-start | bytes 786436
  13.0 1.6 %collective-permute-start.3 = (bf16[256,512]{1,0:T(8,128)(2,1)S(1)}, bf16[256,512]{1,0:T(8,128)(2,1)S(1)}, u32[]{:S(2)}, u32[]{:S(2)}) collective-permute-start(bf16[256,512]{1,0:T(8,128)(2,1)S(1)} %get-tuple-element.32), channel_id=1, source_target_pairs={{0,1},{1,0},{2,3},{3,2},{4,5},{5,4},{6,7},{7,6},{8,9},{9,8},{10,11... | collective-permute-start | bytes 786440 | tf_op jit(solution)/shard_map/ppermute | solution.py:51
  14.7 8.2 %collective-permute-start.4 = (bf16[128,512]{1,0:T(8,128)(2,1)S(1)}, bf16[128,512]{1,0:T(8,128)(2,1)S(1)}, u32[]{:S(2)}, u32[]{:S(2)}) collective-permute-start(bf16[128,512]{1,0:T(8,128)(2,1)S(1)} %edge.1), channel_id=1, source_target_pairs={{0,4},{4,8},{8,12},{12,0},{1,5},{5,9},{9,13},{13,1},{2,6},{6,10},{... | collective-permute-start | bytes 393224 | tf_op jit(solution)/shard_map/ppermute | solution.py:56
  15.9 8.1 %collective-permute-start.5 = (bf16[128,512]{1,0:T(8,128)(2,1)S(1)}, bf16[128,512]{1,0:T(8,128)(2,1)S(1)}, u32[]{:S(2)}, u32[]{:S(2)}) collective-permute-start(bf16[128,512]{1,0:T(8,128)(2,1)S(1)} %edge.1), channel_id=1, source_target_pairs={{0,12},{4,0},{8,4},{12,8},{1,13},{5,1},{9,5},{13,9},{2,14},{6,2},{... | collective-permute-start | bytes 393224 | tf_op jit(solution)/shard_map/ppermute | solution.py:55
  18.5 5.4 %collective-permute-start.6 = (bf16[128,512]{1,0:T(8,128)(2,1)S(1)}, bf16[128,512]{1,0:T(8,128)(2,1)S(1)}, u32[]{:S(2)}, u32[]{:S(2)}) collective-permute-start(bf16[128,512]{1,0:T(8,128)(2,1)S(1)} %edge.1), channel_id=1, source_target_pairs={{0,2},{2,0},{1,3},{3,1},{4,6},{6,4},{5,7},{7,5},{8,10},{10,8},{9,1... | collective-permute-start | bytes 393224 | tf_op jit(solution)/shard_map/ppermute | solution.py:58
  23.9 1.1 %copy-start = (s32[2,8,8]{2,1,0:T(8,128)S(1)}, s32[2,8,8]{2,1,0:T(8,128)}, u32[]{:S(2)}) copy-start(s32[2,8,8]{2,1,0:T(8,128)} %mask.1) | copy-start | bytes 1540
  23.9 1.2 %copy-start.1 = (bf16[2,512,512]{2,1,0:T(8,128)(2,1)S(1)}, bf16[2,512,512]{2,1,0:T(8,128)(2,1)}, u32[]{:S(2)}) copy-start(bf16[2,512,512]{2,1,0:T(8,128)(2,1)} %weights.1) | copy-start | bytes 3145732
  24.9 1.6 %copy-start.3 = (bf16[1,1,256,512]{3,2,1,0:T(8,128)(2,1)S(1)}, bf16[1,1,256,512]{3,2,1,0:T(8,128)(2,1)}, u32[]{:S(2)}) copy-start(bf16[1,1,256,512]{3,2,1,0:T(8,128)(2,1)} %param.9) | copy-start | bytes 786436
  24.9 1.6 %collective-permute-start.7 = (bf16[256,512]{1,0:T(8,128)(2,1)S(1)}, bf16[256,512]{1,0:T(8,128)(2,1)S(1)}, u32[]{:S(2)}, u32[]{:S(2)}) collective-permute-start(bf16[256,512]{1,0:T(8,128)(2,1)S(1)} %get-tuple-element.36), channel_id=1, source_target_pairs={{0,1},{1,0},{2,3},{3,2},{4,5},{5,4},{6,7},{7,6},{8,9},{9,8},{10,11... | collective-permute-start | bytes 786440 | tf_op jit(solution)/shard_map/ppermute | solution.py:51
  27.8 1.5 %collective-permute-start.8 = (bf16[256,512]{1,0:T(8,128)(2,1)S(1)}, bf16[256,512]{1,0:T(8,128)(2,1)S(1)}, u32[]{:S(2)}, u32[]{:S(2)}) collective-permute-start(bf16[256,512]{1,0:T(8,128)(2,1)S(1)} %get-tuple-element.40.dx), channel_id=1, source_target_pairs={{0,1},{1,0},{2,3},{3,2},{4,5},{5,4},{6,7},{7,6},{8,9},{9,8},{10,11... | collective-permute-start | bytes 786440 | tf_op jit(solution)/shard_map/ppermute | solution.py:51
  28.5 2.0 %collective-permute-start.14 = (bf16[512,256]{1,0:T(8,128)(2,1)S(1)}, bf16[512,256]{1,0:T(8,128)(2,1)S(1)}, u32[]{:S(2)}, u32[]{:S(2)}) collective-permute-start(bf16[512,256]{1,0:T(8,128)(2,1)S(1)} %get-tuple-element.53), channel_id=1, source_target_pairs={{0,1},{1,0},{2,3},{3,2},{4,5},{5,4},{6,7},{7,6},{8,9},{9,8},{10,11... | collective-permute-start | bytes 786440 | tf_op jit(solution)/shard_map/ppermute | solution.py:51
  30.3 1.6 %collective-permute-start.9 = (bf16[512,256]{1,0:T(8,128)(2,1)S(1)}, bf16[512,256]{1,0:T(8,128)(2,1)S(1)}, u32[]{:S(2)}, u32[]{:S(2)}) collective-permute-start(bf16[512,256]{1,0:T(8,128)(2,1)S(1)} %get-tuple-element.45), channel_id=1, source_target_pairs={{0,1},{1,0},{2,3},{3,2},{4,5},{5,4},{6,7},{7,6},{8,9},{9,8},{10,11... | collective-permute-start | bytes 786440 | tf_op jit(solution)/shard_map/ppermute | solution.py:51
  30.6 6.4 %collective-permute-start.15 = (bf16[256,256]{1,0:T(8,128)(2,1)S(1)}, bf16[256,256]{1,0:T(8,128)(2,1)S(1)}, u32[]{:S(2)}, u32[]{:S(2)}) collective-permute-start(bf16[256,256]{1,0:T(8,128)(2,1)S(1)} %get-tuple-element.55), channel_id=1, source_target_pairs={{0,4},{4,0},{8,12},{12,8},{1,5},{5,1},{9,13},{13,9},{2,6},{6,2},{1... | collective-permute-start | bytes 393224 | tf_op jit(solution)/shard_map/ppermute | solution.py:272
  32.0 7.3 %collective-permute-start.10 = (bf16[256,256]{1,0:T(8,128)(2,1)S(1)}, bf16[256,256]{1,0:T(8,128)(2,1)S(1)}, u32[]{:S(2)}, u32[]{:S(2)}) collective-permute-start(bf16[256,256]{1,0:T(8,128)(2,1)S(1)} %get-tuple-element.47), channel_id=1, source_target_pairs={{0,4},{4,0},{8,12},{12,8},{1,5},{5,1},{9,13},{13,9},{2,6},{6,2},{1... | collective-permute-start | bytes 393224 | tf_op jit(solution)/shard_map/ppermute | solution.py:272
  37.0 7.1 %collective-permute-start.16 = (bf16[128,256]{1,0:T(8,128)(2,1)S(1)}, bf16[128,256]{1,0:T(8,128)(2,1)S(1)}, u32[]{:S(2)}, u32[]{:S(2)}) collective-permute-start(bf16[128,256]{1,0:T(8,128)(2,1)S(1)} %get-tuple-element.57), channel_id=1, source_target_pairs={{0,8},{4,12},{8,0},{12,4},{1,9},{5,13},{9,1},{13,5},{2,10},{6,14},... | collective-permute-start | bytes 196616 | tf_op jit(solution)/shard_map/ppermute | solution.py:272
  39.2 6.5 %collective-permute-start.11 = (bf16[128,256]{1,0:T(8,128)(2,1)S(1)}, bf16[128,256]{1,0:T(8,128)(2,1)S(1)}, u32[]{:S(2)}, u32[]{:S(2)}) collective-permute-start(bf16[128,256]{1,0:T(8,128)(2,1)S(1)} %get-tuple-element.49), channel_id=1, source_target_pairs={{0,8},{4,12},{8,0},{12,4},{1,9},{5,13},{9,1},{13,5},{2,10},{6,14},... | collective-permute-start | bytes 196616 | tf_op jit(solution)/shard_map/ppermute | solution.py:272
  44.1 4.7 %collective-permute-start.17 = (bf16[128,256]{1,0:T(8,128)(2,1)S(1)}, bf16[128,256]{1,0:T(8,128)(2,1)S(1)}, u32[]{:S(2)}, u32[]{:S(2)}) collective-permute-start(bf16[128,256]{1,0:T(8,128)(2,1)S(1)} %phi_sum.3.own), channel_id=1, source_target_pairs={{0,2},{2,0},{1,3},{3,1},{4,6},{6,4},{5,7},{7,5},{8,10},{10,8},{9,1... | collective-permute-start | bytes 196616 | tf_op jit(solution)/shard_map/ppermute | solution.py:278
  45.7 4.3 %collective-permute-start.12 = (bf16[128,256]{1,0:T(8,128)(2,1)S(1)}, bf16[128,256]{1,0:T(8,128)(2,1)S(1)}, u32[]{:S(2)}, u32[]{:S(2)}) collective-permute-start(bf16[128,256]{1,0:T(8,128)(2,1)S(1)} %phi_sum.2.own), channel_id=1, source_target_pairs={{0,2},{2,0},{1,3},{3,1},{4,6},{6,4},{5,7},{7,5},{8,10},{10,8},{9,1... | collective-permute-start | bytes 196616 | tf_op jit(solution)/shard_map/ppermute | solution.py:278
  48.8 1.8 %collective-permute-start.18 = (bf16[128,256]{1,0:T(8,128)(2,1)S(1)}, bf16[128,256]{1,0:T(8,128)(2,1)S(1)}, u32[]{:S(2)}, u32[]{:S(2)}) collective-permute-start(bf16[128,256]{1,0:T(8,128)(2,1)S(1)} %eta_sum.3.refs_2_), channel_id=1, source_target_pairs={{0,1},{1,0},{2,3},{3,2},{4,5},{5,4},{6,7},{7,6},{8,9},{9,8},{10,11... | collective-permute-start | bytes 196616 | tf_op jit(solution)/shard_map/ppermute | solution.py:51
  50.1 1.3 %collective-permute-start.13 = (bf16[128,256]{1,0:T(8,128)(2,1)S(1)}, bf16[128,256]{1,0:T(8,128)(2,1)S(1)}, u32[]{:S(2)}, u32[]{:S(2)}) collective-permute-start(bf16[128,256]{1,0:T(8,128)(2,1)S(1)} %eta_sum.2.refs_0_), channel_id=1, source_target_pairs={{0,1},{1,0},{2,3},{3,2},{4,5},{5,4},{6,7},{7,6},{8,9},{9,8},{10,11... | collective-permute-start | bytes 196616 | tf_op jit(solution)/shard_map/ppermute | solution.py:51

commit v4 on v3

--- a/solution.py
+++ b/solution.py
@@ -195,6 +195,10 @@
     final_out[...] = (live * (hfloat + pre * sigma)).astype(BF16)
 
 
+def emit_kernel(value, out):
+    out[...] = value[...]
+
+
 def split_columns(value, mine_out, theirs_out):
     middle = value.shape[1] // 2
     first = lax.axis_index("half") == 0
@@ -360,6 +364,7 @@
         name="last",
     )
     dx_other = swap_half(dx)
+    final = call(emit_kernel, (final,), [wide], name="emit")[0]
     halves = [shaped((width, width // 2), F32), shaped((width, width // 2), BF16)]
     mine1, theirs1 = call(
         grad_kernel, (x1, dz1), halves, flops=dense_flops, name="grad"

time: 52.5 us -> 52 us (level)
  waiting for transfers between devices: 18.9 us -> 18.1 us
    ppermute x7, waiting for transfers between devices: 3.58 us -> 2.86 us  [swap_half(): return lax.ppermute(value, 'half', [(0, 1), (1, 0)])]
    pallas_call x19 -> x20, Pallas kernels: 8 us -> 8.29 us  [call(): pl.pallas_call(kernel, out_shape=outs, in_specs=[FAR if far else VMEM] *...]
  transfers between devices with their start and end apart: 19 -> 19, of which waited for: 15 -> 15; matrix products, arithmetic and copies ran while one was open for 2% -> 2% of each run, Pallas kernels for 8% -> 10%
where the time goes in v4:
time: 52 us; the launch traced here: 51.8 us
  starting transfers between devices  21.7 us (42%)
  waiting for transfers between devices  18.1 us (35%)
  Pallas kernels  8.29 us (16%)
  local copies, waits for them, and re-layouts  2.13 us (4%)
  between operations  1.47 us (3%)
    pallas_call x20, Pallas kernels, call(): pl.pallas_call(kernel, out_shape=outs, in_specs=[FAR if far else VMEM] *...  8.29 us
    ppermute x4, waiting for transfers between devices, phi_share(): lax.ppermute(send, 'phi', [(i, i ^ 1 << level) for i in range(parts)])  6.9 us
    ppermute x4, starting transfers between devices, phi_share(): lax.ppermute(send, 'phi', [(i, i ^ 1 << level) for i in range(parts)])  5.28 us
    ppermute x2, starting transfers between devices, to_neighbours(): from_high = lax.ppermute(low_phi, 'phi', ring('phi', -1, True))  4.79 us
    ppermute x2, starting transfers between devices, to_neighbours(): from_low = lax.ppermute(high_phi, 'phi', ring('phi', 1, True))  4.26 us
    ppermute x2, waiting for transfers between devices, to_neighbours(): from_low = lax.ppermute(high_phi, 'phi', ring('phi', 1, True))  3.24 us
    ppermute x2, starting transfers between devices, to_neighbours(): return [from_low, from_high, lax.ppermute(low_eta, 'eta', [(0, 1), (1, 0)])]  3.14 us
    ppermute x2, starting transfers between devices, eta_sum(): arrived = lax.ppermute(share, 'eta', [(0, 1), (1, 0)])  3.09 us
  transfers between devices with their start and end apart: 19, of which 15 were waited for; matrix products, arithmetic and copies ran while one was open for 2% of the time, Pallas kernels for 10%

profile of v4, /device:TPU:0, one launch (start us, length us, event | category | flops | bytes accessed | tf_op | source)
XLA Modules:
  0.0 51.8 jit_solution(1416352899763116711)
XLA Ops:
  0.6 0.9 %slice_bitcast_fusion = bf16[128,512]{1,0:T(8,128)(2,1)S(1)} fusion(bf16[1,1,256,512]{3,2,1,0:T(8,128)(2,1)} %param.8), kind=kLoop, calls=%fused_computation.2 | loop fusion | bytes 262144 | tf_op jit(solution)/shard_map/slice | solution.py:302
  1.5 3.1 %collective-permute-start = (bf16[128,512]{1,0:T(8,128)(2,1)S(1)}, bf16[128,512]{1,0:T(8,128)(2,1)S(1)}, u32[]{:S(2)}, u32[]{:S(2)}) collective-permute-start(bf16[128,512]{1,0:T(8,128)(2,1)S(1)} %slice_bitcast_fusion), channel_id=1, source_target_pairs={{0,4},{4,8},{8,12},{12,0},{1,5},{5,9},{9,13},{13,1},{2,6},{6,10},{... | collective-permute-start | bytes 393224 | tf_op jit(solution)/shard_map/ppermute | solution.py:56
  4.6 2.1 %collective-permute-start.1 = (bf16[128,512]{1,0:T(8,128)(2,1)S(1)}, bf16[128,512]{1,0:T(8,128)(2,1)S(1)}, u32[]{:S(2)}, u32[]{:S(2)}) collective-permute-start(bf16[128,512]{1,0:T(8,128)(2,1)S(1)} %slice_bitcast_fusion), channel_id=1, source_target_pairs={{0,12},{4,0},{8,4},{12,8},{1,13},{5,1},{9,5},{13,9},{2,14},{6,2},{... | collective-permute-start | bytes 393224 | tf_op jit(solution)/shard_map/ppermute | solution.py:55
  6.7 1.6 %collective-permute-start.2 = (bf16[128,512]{1,0:T(8,128)(2,1)S(1)}, bf16[128,512]{1,0:T(8,128)(2,1)S(1)}, u32[]{:S(2)}, u32[]{:S(2)}) collective-permute-start(bf16[128,512]{1,0:T(8,128)(2,1)S(1)} %slice_bitcast_fusion), channel_id=1, source_target_pairs={{0,2},{2,0},{1,3},{3,1},{4,6},{6,4},{5,7},{7,5},{8,10},{10,8},{9,1... | collective-permute-start | bytes 393224 | tf_op jit(solution)/shard_map/ppermute | solution.py:58
  8.4 0.0 copy-start.2
  8.4 1.8 %build.1 = (bf16[512,640]{1,0:T(8,128)(2,1)S(1)}, bf16[512,512]{1,0:T(8,128)(2,1)S(1)}) custom-call(s32[12]{0:T(128)} %bitcast.25, s32[12]{0:T(128)} %bitcast.26, bf16[12,128,128]{2,1,0:T(8,128)(2,1)} %bitcast.23, s32[2,8,8]{2,1,0:T(8,128)} %mask.1, bf16[2,512,512]{2,1,0:T(8,128)(2,1)} %weights.1), custom_call_target="tpu_custom_call" | custom-call | flops 10000000 | bytes 2622048 | tf_op jit(solution)/shard_map/build/pallas_call | solution.py:22
  10.1 0.8 %collective-permute-done.refs_1_.refs_0_ = bf16[128,512]{1,0:T(8,128)(2,1)S(1)} collective-permute-done((bf16[128,512]{1,0:T(8,128)(2,1)S(1)}, bf16[128,512]{1,0:T(8,128)(2,1)S(1)}, u32[]{:S(2)}, u32[]{:S(2)}) %collective-permute-start) | collective-permute-done | bytes 131104 | tf_op jit(solution)/shard_map/ppermute | solution.py:56
  11.0 1.4 %collective-permute-done.1.refs_2_.refs_1_ = bf16[128,512]{1,0:T(8,128)(2,1)S(1)} collective-permute-done((bf16[128,512]{1,0:T(8,128)(2,1)S(1)}, bf16[128,512]{1,0:T(8,128)(2,1)S(1)}, u32[]{:S(2)}, u32[]{:S(2)}) %collective-permute-start.1) | collective-permute-done | bytes 131104 | tf_op jit(solution)/shard_map/ppermute | solution.py:55
  12.4 0.0 collective-permute-done.2.refs_3_.refs_2_
  12.4 0.0 copy-done.2
  12.4 0.6 %gather.8 = (bf16[256,512]{1,0:T(8,128)(2,1)S(1)}, bf16[256,512]{1,0:T(8,128)(2,1)S(1)}) custom-call(bf16[512,640]{1,0:T(8,128)(2,1)S(1)} %get-tuple-element.30.matrix, bf16[256,512]{1,0:T(8,128)(2,1)S(1)} %bitcast.16, bf16[128,512]{1,0:T(8,128)(2,1)S(1)} %collective-permute-done.refs_1_.refs_0_, ...), custom_call_target="tpu_custom_call" | custom-call | flops 335544320 | bytes 1835008 | tf_op jit(solution)/shard_map/gather/pallas_call | solution.py:22
  13.0 0.1 collective-permute-start.3
  13.7 0.9 %collective-permute-done.3.other = bf16[256,512]{1,0:T(8,128)(2,1)S(1)} collective-permute-done((bf16[256,512]{1,0:T(8,128)(2,1)S(1)}, bf16[256,512]{1,0:T(8,128)(2,1)S(1)}, u32[]{:S(2)}, u32[]{:S(2)}) %collective-permute-start.3) | collective-permute-done | bytes 262176 | tf_op jit(solution)/shard_map/ppermute | solution.py:51
  14.6 0.1 edge.1
  14.7 1.2 %collective-permute-start.4 = (bf16[128,512]{1,0:T(8,128)(2,1)S(1)}, bf16[128,512]{1,0:T(8,128)(2,1)S(1)}, u32[]{:S(2)}, u32[]{:S(2)}) collective-permute-start(bf16[128,512]{1,0:T(8,128)(2,1)S(1)} %edge.1), channel_id=1, source_target_pairs={{0,4},{4,8},{8,12},{12,0},{1,5},{5,9},{9,13},{13,1},{2,6},{6,10},{... | collective-permute-start | bytes 393224 | tf_op jit(solution)/shard_map/ppermute | solution.py:56
  15.9 2.7 %collective-permute-start.5 = (bf16[128,512]{1,0:T(8,128)(2,1)S(1)}, bf16[128,512]{1,0:T(8,128)(2,1)S(1)}, u32[]{:S(2)}, u32[]{:S(2)}) collective-permute-start(bf16[128,512]{1,0:T(8,128)(2,1)S(1)} %edge.1), channel_id=1, source_target_pairs={{0,12},{4,0},{8,4},{12,8},{1,13},{5,1},{9,5},{13,9},{2,14},{6,2},{... | collective-permute-start | bytes 393224 | tf_op jit(solution)/shard_map/ppermute | solution.py:55
  18.5 1.5 %collective-permute-start.6 = (bf16[128,512]{1,0:T(8,128)(2,1)S(1)}, bf16[128,512]{1,0:T(8,128)(2,1)S(1)}, u32[]{:S(2)}, u32[]{:S(2)}) collective-permute-start(bf16[128,512]{1,0:T(8,128)(2,1)S(1)} %edge.1), channel_id=1, source_target_pairs={{0,2},{2,0},{1,3},{3,1},{4,6},{6,4},{5,7},{7,5},{8,10},{10,8},{9,1... | collective-permute-start | bytes 393224 | tf_op jit(solution)/shard_map/ppermute | solution.py:58
  20.0 0.5 forward.1
  20.5 2.4 %collective-permute-done.4.refs_3_.refs_0_ = bf16[128,512]{1,0:T(8,128)(2,1)S(1)} collective-permute-done((bf16[128,512]{1,0:T(8,128)(2,1)S(1)}, bf16[128,512]{1,0:T(8,128)(2,1)S(1)}, u32[]{:S(2)}, u32[]{:S(2)}) %collective-permute-start.4) | collective-permute-done | bytes 131104 | tf_op jit(solution)/shard_map/ppermute | solution.py:56
  22.9 1.0 %collective-permute-done.5.refs_4_.refs_1_ = bf16[128,512]{1,0:T(8,128)(2,1)S(1)} collective-permute-done((bf16[128,512]{1,0:T(8,128)(2,1)S(1)}, bf16[128,512]{1,0:T(8,128)(2,1)S(1)}, u32[]{:S(2)}, u32[]{:S(2)}) %collective-permute-start.5) | collective-permute-done | bytes 131104 | tf_op jit(solution)/shard_map/ppermute | solution.py:55
  23.9 0.0 collective-permute-done.6.refs_5_.refs_2_
  23.9 0.0 copy-start
  23.9 0.0 copy-start.1
  23.9 1.0 %rim.1 = (bf16[256,512]{1,0:T(8,128)(2,1)S(1)}, bf16[256,512]{1,0:T(8,128)(2,1)S(1)}, f32[384,512]{1,0:T(8,128)S(1)}) custom-call(bf16[512,640]{1,0:T(8,128)(2,1)S(1)} %get-tuple-element.30.matrix, bf16[512,512]{1,0:T(8,128)(2,1)S(1)} %get-tuple-element.33.weight, bf16[256,512]{1,0:T(8,128)(2,1)S(1)} %get-tuple-element.34.new.state, ...), custom_call_target="tpu_custom_call" | custom-call | flops 603979776 | bytes 3538944 | tf_op jit(solution)/shard_map/rim/pallas_call | solution.py:22
  24.9 0.0 copy-start.3
  24.9 0.1 collective-permute-start.7
  25.0 0.0 copy-done
  25.0 0.2 copy-done.1
  25.2 0.4 later.1
  25.6 1.0 %collective-permute-done.7.other = bf16[256,512]{1,0:T(8,128)(2,1)S(1)} collective-permute-done((bf16[256,512]{1,0:T(8,128)(2,1)S(1)}, bf16[256,512]{1,0:T(8,128)(2,1)S(1)}, u32[]{:S(2)}, u32[]{:S(2)}) %collective-permute-start.7) | collective-permute-done | bytes 262176 | tf_op jit(solution)/shard_map/ppermute | solution.py:51
  26.5 0.0 copy-done.3
  26.5 0.7 %last.1 = (bf16[256,512]{1,0:T(8,128)(2,1)S(1)}, bf16[256,512]{1,0:T(8,128)(2,1)S(1)}, bf16[256,512]{1,0:T(8,128)(2,1)S(1)}, bf16[256,512]{1,0:T(8,128)(2,1)S(1)}) custom-call(s32[8,128]{1,0:T(8,128)S(1)} %broadcast_in_dim.22.count, bf16[256,512]{1,0:T(8,128)(2,1)S(1)} %get-tuple-element.34.new.state, bf16[256,512]{1,0:T(8,128)(2,1)S(1)} %get-tuple-element.35.own, ...), custom_call_target="tpu_custom_call" | custom-call | flops 268435456 | bytes 2625536 | tf_op jit(solution)/shard_map/last/pallas_call | solution.py:22
  27.3 0.2 collective-permute-start.8
  27.5 0.2 turn.1.xt
  27.7 0.3 grad.1
  28.0 0.4 collective-permute-start.14
  28.5 0.4 collective-permute-done.8.dx_other
  28.9 0.9 %back.1 = (f32[512,256]{1,0:T(8,128)S(1)}, bf16[512,256]{1,0:T(8,128)(2,1)S(1)}) custom-call(bf16[640,512]{1,0:T(8,128)(2,1)S(1)} %get-tuple-element.39.mt, bf16[256,512]{1,0:T(8,128)(2,1)S(1)} %get-tuple-element.40.dx, bf16[256,512]{1,0:T(8,128)(2,1)S(1)} %collective-permute-done.8.dx_other, bf16[256,512]{1,0:T(8,128)(2,1)S(1)} %bitcast.20, ...), custom_call_target="tpu_custom_call" | custom-call | flops 671088640 | bytes 4194304 | tf_op jit(solution)/shard_map/back/pallas_call | solution.py:22
  29.8 0.2 collective-permute-start.9
  30.0 0.0 collective-permute-done.14.arrived
  30.1 0.8 %collective-permute-start.15 = (bf16[256,256]{1,0:T(8,128)(2,1)S(1)}, bf16[256,256]{1,0:T(8,128)(2,1)S(1)}, u32[]{:S(2)}, u32[]{:S(2)}) collective-permute-start(bf16[256,256]{1,0:T(8,128)(2,1)S(1)} %get-tuple-element.55), channel_id=1, source_target_pairs={{0,4},{4,0},{8,12},{12,8},{1,5},{5,1},{9,13},{13,9},{2,6},{6,2},{1... | collective-permute-start | bytes 393224 | tf_op jit(solution)/shard_map/ppermute | solution.py:276
  30.9 0.5 %collective-permute-done.9.arrived = bf16[512,256]{1,0:T(8,128)(2,1)S(1)} collective-permute-done((bf16[512,256]{1,0:T(8,128)(2,1)S(1)}, bf16[512,256]{1,0:T(8,128)(2,1)S(1)}, u32[]{:S(2)}, u32[]{:S(2)}) %collective-permute-start.9) | collective-permute-done | bytes 262176 | tf_op jit(solution)/shard_map/ppermute | solution.py:51
  31.5 0.8 %collective-permute-start.10 = (bf16[256,256]{1,0:T(8,128)(2,1)S(1)}, bf16[256,256]{1,0:T(8,128)(2,1)S(1)}, u32[]{:S(2)}, u32[]{:S(2)}) collective-permute-start(bf16[256,256]{1,0:T(8,128)(2,1)S(1)} %get-tuple-element.47), channel_id=1, source_target_pairs={{0,4},{4,0},{8,12},{12,8},{1,5},{5,1},{9,13},{13,9},{2,6},{6,2},{1... | collective-permute-start | bytes 393224 | tf_op jit(solution)/shard_map/ppermute | solution.py:276
  32.3 4.2 %collective-permute-done.15.arrived = bf16[256,256]{1,0:T(8,128)(2,1)S(1)} collective-permute-done((bf16[256,256]{1,0:T(8,128)(2,1)S(1)}, bf16[256,256]{1,0:T(8,128)(2,1)S(1)}, u32[]{:S(2)}, u32[]{:S(2)}) %collective-permute-start.15) | collective-permute-done | bytes 131104 | tf_op jit(solution)/shard_map/ppermute | solution.py:276
  36.5 1.6 %collective-permute-start.16 = (bf16[128,256]{1,0:T(8,128)(2,1)S(1)}, bf16[128,256]{1,0:T(8,128)(2,1)S(1)}, u32[]{:S(2)}, u32[]{:S(2)}) collective-permute-start(bf16[128,256]{1,0:T(8,128)(2,1)S(1)} %get-tuple-element.57), channel_id=1, source_target_pairs={{0,8},{4,12},{8,0},{12,4},{1,9},{5,13},{9,1},{13,5},{2,10},{6,14},... | collective-permute-start | bytes 196616 | tf_op jit(solution)/shard_map/ppermute | solution.py:276
  38.1 0.6 %collective-permute-done.10.arrived = bf16[256,256]{1,0:T(8,128)(2,1)S(1)} collective-permute-done((bf16[256,256]{1,0:T(8,128)(2,1)S(1)}, bf16[256,256]{1,0:T(8,128)(2,1)S(1)}, u32[]{:S(2)}, u32[]{:S(2)}) %collective-permute-start.10) | collective-permute-done | bytes 131104 | tf_op jit(solution)/shard_map/ppermute | solution.py:276
  38.7 2.0 %collective-permute-start.11 = (bf16[128,256]{1,0:T(8,128)(2,1)S(1)}, bf16[128,256]{1,0:T(8,128)(2,1)S(1)}, u32[]{:S(2)}, u32[]{:S(2)}) collective-permute-start(bf16[128,256]{1,0:T(8,128)(2,1)S(1)} %get-tuple-element.49), channel_id=1, source_target_pairs={{0,8},{4,12},{8,0},{12,4},{1,9},{5,13},{9,1},{13,5},{2,10},{6,14},... | collective-permute-start | bytes 196616 | tf_op jit(solution)/shard_map/ppermute | solution.py:276
  40.8 0.7 %gather_fusion = s32[128,2,8]{2,0,1:T(8,128)S(1)} fusion(s32[2,8,8]{2,1,0:T(8,128)S(1)} %copy-done, s32[1024]{0:T(1024)S(1)} %pad_clamp_fusion), kind=kCustom, calls=%fused_computation | custom fusion | bytes 16896 | tf_op jit(solution)/shard_map/jit(_take)/gather | solution.py:391
  41.5 2.0 %collective-permute-done.16.refs_0_ = bf16[128,256]{1,0:T(8,128)(2,1)S(1)} collective-permute-done((bf16[128,256]{1,0:T(8,128)(2,1)S(1)}, bf16[128,256]{1,0:T(8,128)(2,1)S(1)}, u32[]{:S(2)}, u32[]{:S(2)}) %collective-permute-start.16) | collective-permute-done | bytes 65568 | tf_op jit(solution)/shard_map/ppermute | solution.py:276
  43.6 1.5 %collective-permute-start.17 = (bf16[128,256]{1,0:T(8,128)(2,1)S(1)}, bf16[128,256]{1,0:T(8,128)(2,1)S(1)}, u32[]{:S(2)}, u32[]{:S(2)}) collective-permute-start(bf16[128,256]{1,0:T(8,128)(2,1)S(1)} %phi_sum.3.own), channel_id=1, source_target_pairs={{0,2},{2,0},{1,3},{3,1},{4,6},{6,4},{5,7},{7,5},{8,10},{10,8},{9,1... | collective-permute-start | bytes 196616 | tf_op jit(solution)/shard_map/ppermute | solution.py:282
  45.1 0.1 collective-permute-done.11.refs_0_
  45.2 1.5 %collective-permute-start.12 = (bf16[128,256]{1,0:T(8,128)(2,1)S(1)}, bf16[128,256]{1,0:T(8,128)(2,1)S(1)}, u32[]{:S(2)}, u32[]{:S(2)}) collective-permute-start(bf16[128,256]{1,0:T(8,128)(2,1)S(1)} %phi_sum.2.own), channel_id=1, source_target_pairs={{0,2},{2,0},{1,3},{3,1},{4,6},{6,4},{5,7},{7,5},{8,10},{10,8},{9,1... | collective-permute-start | bytes 196616 | tf_op jit(solution)/shard_map/ppermute | solution.py:282
  46.8 1.5 %collective-permute-done.17.refs_0_ = bf16[128,256]{1,0:T(8,128)(2,1)S(1)} collective-permute-done((bf16[128,256]{1,0:T(8,128)(2,1)S(1)}, bf16[128,256]{1,0:T(8,128)(2,1)S(1)}, u32[]{:S(2)}, u32[]{:S(2)}) %collective-permute-start.17) | collective-permute-done | bytes 65568 | tf_op jit(solution)/shard_map/ppermute | solution.py:282
  48.3 0.1 collective-permute-start.18
  48.4 1.2 %collective-permute-done.12.refs_0_ = bf16[128,256]{1,0:T(8,128)(2,1)S(1)} collective-permute-done((bf16[128,256]{1,0:T(8,128)(2,1)S(1)}, bf16[128,256]{1,0:T(8,128)(2,1)S(1)}, u32[]{:S(2)}, u32[]{:S(2)}) %collective-permute-start.12) | collective-permute-done | bytes 65568 | tf_op jit(solution)/shard_map/ppermute | solution.py:282
  49.6 0.1 collective-permute-start.13
  49.7 0.1 convert_bitcast_fusion
  49.8 0.1 copy.10
  49.9 0.2 copy.11.refs_4_
  50.1 0.7 %emit.1 = bf16[256,512]{1,0:T(8,128)(2,1)} custom-call(bf16[256,512]{1,0:T(8,128)(2,1)S(1)} %get-tuple-element.38.value), custom_call_target="tpu_custom_call" | custom-call | bytes 524288 | tf_op jit(solution)/shard_map/emit/pallas_call | solution.py:22
  50.8 0.0 collective-permute-done.18.refs_3_
  50.8 0.1 collective-permute-done.13.refs_1_
  50.9 0.9 %finish.1 = f32[2,128,512]{2,1,0:T(8,128)} custom-call(bf16[128,256]{1,0:T(8,128)(2,1)S(1)} %eta_sum.2.refs_0_, bf16[128,256]{1,0:T(8,128)(2,1)S(1)} %collective-permute-done.13.refs_1_, bf16[128,256]{1,0:T(8,128)(2,1)S(1)} %eta_sum.3.refs_2_, bf16[128,256]{1,0:T(8,128)(2,1)S(1)} %collective-permute-done.18.refs_3_, f32[2,128,512]{2,1,0:T(8,128)S(1)} %copy.11.refs_4_), custom_call_target="tpu_custom_call" | custom-call | bytes 1310720 | tf_op jit(solution)/shard_map/finish/pallas_call | solution.py:22
  (13 shorter events, 0.3 us)
Async XLA Ops:
  1.5 9.4 %collective-permute-start = (bf16[128,512]{1,0:T(8,128)(2,1)S(1)}, bf16[128,512]{1,0:T(8,128)(2,1)S(1)}, u32[]{:S(2)}, u32[]{:S(2)}) collective-permute-start(bf16[128,512]{1,0:T(8,128)(2,1)S(1)} %slice_bitcast_fusion), channel_id=1, source_target_pairs={{0,4},{4,8},{8,12},{12,0},{1,5},{5,9},{9,13},{13,1},{2,6},{6,10},{... | collective-permute-start | bytes 393224 | tf_op jit(solution)/shard_map/ppermute | solution.py:56
  4.6 7.8 %collective-permute-start.1 = (bf16[128,512]{1,0:T(8,128)(2,1)S(1)}, bf16[128,512]{1,0:T(8,128)(2,1)S(1)}, u32[]{:S(2)}, u32[]{:S(2)}) collective-permute-start(bf16[128,512]{1,0:T(8,128)(2,1)S(1)} %slice_bitcast_fusion), channel_id=1, source_target_pairs={{0,12},{4,0},{8,4},{12,8},{1,13},{5,1},{9,5},{13,9},{2,14},{6,2},{... | collective-permute-start | bytes 393224 | tf_op jit(solution)/shard_map/ppermute | solution.py:55
  6.7 5.7 %collective-permute-start.2 = (bf16[128,512]{1,0:T(8,128)(2,1)S(1)}, bf16[128,512]{1,0:T(8,128)(2,1)S(1)}, u32[]{:S(2)}, u32[]{:S(2)}) collective-permute-start(bf16[128,512]{1,0:T(8,128)(2,1)S(1)} %slice_bitcast_fusion), channel_id=1, source_target_pairs={{0,2},{2,0},{1,3},{3,1},{4,6},{6,4},{5,7},{7,5},{8,10},{10,8},{9,1... | collective-permute-start | bytes 393224 | tf_op jit(solution)/shard_map/ppermute | solution.py:58
  8.4 4.0 %copy-start.2 = (bf16[1,1,256,512]{3,2,1,0:T(8,128)(2,1)S(1)}, bf16[1,1,256,512]{3,2,1,0:T(8,128)(2,1)}, u32[]{:S(2)}) copy-start(bf16[1,1,256,512]{3,2,1,0:T(8,128)(2,1)} %param.8) | copy-start | bytes 786436
  13.0 1.6 %collective-permute-start.3 = (bf16[256,512]{1,0:T(8,128)(2,1)S(1)}, bf16[256,512]{1,0:T(8,128)(2,1)S(1)}, u32[]{:S(2)}, u32[]{:S(2)}) collective-permute-start(bf16[256,512]{1,0:T(8,128)(2,1)S(1)} %get-tuple-element.32), channel_id=1, source_target_pairs={{0,1},{1,0},{2,3},{3,2},{4,5},{5,4},{6,7},{7,6},{8,9},{9,8},{10,11... | collective-permute-start | bytes 786440 | tf_op jit(solution)/shard_map/ppermute | solution.py:51
  14.7 8.2 %collective-permute-start.4 = (bf16[128,512]{1,0:T(8,128)(2,1)S(1)}, bf16[128,512]{1,0:T(8,128)(2,1)S(1)}, u32[]{:S(2)}, u32[]{:S(2)}) collective-permute-start(bf16[128,512]{1,0:T(8,128)(2,1)S(1)} %edge.1), channel_id=1, source_target_pairs={{0,4},{4,8},{8,12},{12,0},{1,5},{5,9},{9,13},{13,1},{2,6},{6,10},{... | collective-permute-start | bytes 393224 | tf_op jit(solution)/shard_map/ppermute | solution.py:56
  15.9 8.1 %collective-permute-start.5 = (bf16[128,512]{1,0:T(8,128)(2,1)S(1)}, bf16[128,512]{1,0:T(8,128)(2,1)S(1)}, u32[]{:S(2)}, u32[]{:S(2)}) collective-permute-start(bf16[128,512]{1,0:T(8,128)(2,1)S(1)} %edge.1), channel_id=1, source_target_pairs={{0,12},{4,0},{8,4},{12,8},{1,13},{5,1},{9,5},{13,9},{2,14},{6,2},{... | collective-permute-start | bytes 393224 | tf_op jit(solution)/shard_map/ppermute | solution.py:55
  18.5 5.4 %collective-permute-start.6 = (bf16[128,512]{1,0:T(8,128)(2,1)S(1)}, bf16[128,512]{1,0:T(8,128)(2,1)S(1)}, u32[]{:S(2)}, u32[]{:S(2)}) collective-permute-start(bf16[128,512]{1,0:T(8,128)(2,1)S(1)} %edge.1), channel_id=1, source_target_pairs={{0,2},{2,0},{1,3},{3,1},{4,6},{6,4},{5,7},{7,5},{8,10},{10,8},{9,1... | collective-permute-start | bytes 393224 | tf_op jit(solution)/shard_map/ppermute | solution.py:58
  23.9 1.1 %copy-start = (s32[2,8,8]{2,1,0:T(8,128)S(1)}, s32[2,8,8]{2,1,0:T(8,128)}, u32[]{:S(2)}) copy-start(s32[2,8,8]{2,1,0:T(8,128)} %mask.1) | copy-start | bytes 1540
  23.9 1.2 %copy-start.1 = (bf16[2,512,512]{2,1,0:T(8,128)(2,1)S(1)}, bf16[2,512,512]{2,1,0:T(8,128)(2,1)}, u32[]{:S(2)}) copy-start(bf16[2,512,512]{2,1,0:T(8,128)(2,1)} %weights.1) | copy-start | bytes 3145732
  24.9 1.6 %copy-start.3 = (bf16[1,1,256,512]{3,2,1,0:T(8,128)(2,1)S(1)}, bf16[1,1,256,512]{3,2,1,0:T(8,128)(2,1)}, u32[]{:S(2)}) copy-start(bf16[1,1,256,512]{3,2,1,0:T(8,128)(2,1)} %param.9) | copy-start | bytes 786436
  24.9 1.6 %collective-permute-start.7 = (bf16[256,512]{1,0:T(8,128)(2,1)S(1)}, bf16[256,512]{1,0:T(8,128)(2,1)S(1)}, u32[]{:S(2)}, u32[]{:S(2)}) collective-permute-start(bf16[256,512]{1,0:T(8,128)(2,1)S(1)} %get-tuple-element.36), channel_id=1, source_target_pairs={{0,1},{1,0},{2,3},{3,2},{4,5},{5,4},{6,7},{7,6},{8,9},{9,8},{10,11... | collective-permute-start | bytes 786440 | tf_op jit(solution)/shard_map/ppermute | solution.py:51
  27.3 1.6 %collective-permute-start.8 = (bf16[256,512]{1,0:T(8,128)(2,1)S(1)}, bf16[256,512]{1,0:T(8,128)(2,1)S(1)}, u32[]{:S(2)}, u32[]{:S(2)}) collective-permute-start(bf16[256,512]{1,0:T(8,128)(2,1)S(1)} %get-tuple-element.40.dx), channel_id=1, source_target_pairs={{0,1},{1,0},{2,3},{3,2},{4,5},{5,4},{6,7},{7,6},{8,9},{9,8},{10,11... | collective-permute-start | bytes 786440 | tf_op jit(solution)/shard_map/ppermute | solution.py:51
  28.0 2.0 %collective-permute-start.14 = (bf16[512,256]{1,0:T(8,128)(2,1)S(1)}, bf16[512,256]{1,0:T(8,128)(2,1)S(1)}, u32[]{:S(2)}, u32[]{:S(2)}) collective-permute-start(bf16[512,256]{1,0:T(8,128)(2,1)S(1)} %get-tuple-element.53), channel_id=1, source_target_pairs={{0,1},{1,0},{2,3},{3,2},{4,5},{5,4},{6,7},{7,6},{8,9},{9,8},{10,11... | collective-permute-start | bytes 786440 | tf_op jit(solution)/shard_map/ppermute | solution.py:51
  29.8 1.6 %collective-permute-start.9 = (bf16[512,256]{1,0:T(8,128)(2,1)S(1)}, bf16[512,256]{1,0:T(8,128)(2,1)S(1)}, u32[]{:S(2)}, u32[]{:S(2)}) collective-permute-start(bf16[512,256]{1,0:T(8,128)(2,1)S(1)} %get-tuple-element.45), channel_id=1, source_target_pairs={{0,1},{1,0},{2,3},{3,2},{4,5},{5,4},{6,7},{7,6},{8,9},{9,8},{10,11... | collective-permute-start | bytes 786440 | tf_op jit(solution)/shard_map/ppermute | solution.py:51
  30.1 6.4 %collective-permute-start.15 = (bf16[256,256]{1,0:T(8,128)(2,1)S(1)}, bf16[256,256]{1,0:T(8,128)(2,1)S(1)}, u32[]{:S(2)}, u32[]{:S(2)}) collective-permute-start(bf16[256,256]{1,0:T(8,128)(2,1)S(1)} %get-tuple-element.55), channel_id=1, source_target_pairs={{0,4},{4,0},{8,12},{12,8},{1,5},{5,1},{9,13},{13,9},{2,6},{6,2},{1... | collective-permute-start | bytes 393224 | tf_op jit(solution)/shard_map/ppermute | solution.py:276
  31.5 7.3 %collective-permute-start.10 = (bf16[256,256]{1,0:T(8,128)(2,1)S(1)}, bf16[256,256]{1,0:T(8,128)(2,1)S(1)}, u32[]{:S(2)}, u32[]{:S(2)}) collective-permute-start(bf16[256,256]{1,0:T(8,128)(2,1)S(1)} %get-tuple-element.47), channel_id=1, source_target_pairs={{0,4},{4,0},{8,12},{12,8},{1,5},{5,1},{9,13},{13,9},{2,6},{6,2},{1... | collective-permute-start | bytes 393224 | tf_op jit(solution)/shard_map/ppermute | solution.py:276
  36.5 7.1 %collective-permute-start.16 = (bf16[128,256]{1,0:T(8,128)(2,1)S(1)}, bf16[128,256]{1,0:T(8,128)(2,1)S(1)}, u32[]{:S(2)}, u32[]{:S(2)}) collective-permute-start(bf16[128,256]{1,0:T(8,128)(2,1)S(1)} %get-tuple-element.57), channel_id=1, source_target_pairs={{0,8},{4,12},{8,0},{12,4},{1,9},{5,13},{9,1},{13,5},{2,10},{6,14},... | collective-permute-start | bytes 196616 | tf_op jit(solution)/shard_map/ppermute | solution.py:276
  38.7 6.5 %collective-permute-start.11 = (bf16[128,256]{1,0:T(8,128)(2,1)S(1)}, bf16[128,256]{1,0:T(8,128)(2,1)S(1)}, u32[]{:S(2)}, u32[]{:S(2)}) collective-permute-start(bf16[128,256]{1,0:T(8,128)(2,1)S(1)} %get-tuple-element.49), channel_id=1, source_target_pairs={{0,8},{4,12},{8,0},{12,4},{1,9},{5,13},{9,1},{13,5},{2,10},{6,14},... | collective-permute-start | bytes 196616 | tf_op jit(solution)/shard_map/ppermute | solution.py:276
  43.6 4.7 %collective-permute-start.17 = (bf16[128,256]{1,0:T(8,128)(2,1)S(1)}, bf16[128,256]{1,0:T(8,128)(2,1)S(1)}, u32[]{:S(2)}, u32[]{:S(2)}) collective-permute-start(bf16[128,256]{1,0:T(8,128)(2,1)S(1)} %phi_sum.3.own), channel_id=1, source_target_pairs={{0,2},{2,0},{1,3},{3,1},{4,6},{6,4},{5,7},{7,5},{8,10},{10,8},{9,1... | collective-permute-start | bytes 196616 | tf_op jit(solution)/shard_map/ppermute | solution.py:282
  45.2 4.3 %collective-permute-start.12 = (bf16[128,256]{1,0:T(8,128)(2,1)S(1)}, bf16[128,256]{1,0:T(8,128)(2,1)S(1)}, u32[]{:S(2)}, u32[]{:S(2)}) collective-permute-start(bf16[128,256]{1,0:T(8,128)(2,1)S(1)} %phi_sum.2.own), channel_id=1, source_target_pairs={{0,2},{2,0},{1,3},{3,1},{4,6},{6,4},{5,7},{7,5},{8,10},{10,8},{9,1... | collective-permute-start | bytes 196616 | tf_op jit(solution)/shard_map/ppermute | solution.py:282
  48.3 2.5 %collective-permute-start.18 = (bf16[128,256]{1,0:T(8,128)(2,1)S(1)}, bf16[128,256]{1,0:T(8,128)(2,1)S(1)}, u32[]{:S(2)}, u32[]{:S(2)}) collective-permute-start(bf16[128,256]{1,0:T(8,128)(2,1)S(1)} %eta_sum.3.refs_2_), channel_id=1, source_target_pairs={{0,1},{1,0},{2,3},{3,2},{4,5},{5,4},{6,7},{7,6},{8,9},{9,8},{10,11... | collective-permute-start | bytes 196616 | tf_op jit(solution)/shard_map/ppermute | solution.py:51
  49.6 1.3 %collective-permute-start.13 = (bf16[128,256]{1,0:T(8,128)(2,1)S(1)}, bf16[128,256]{1,0:T(8,128)(2,1)S(1)}, u32[]{:S(2)}, u32[]{:S(2)}) collective-permute-start(bf16[128,256]{1,0:T(8,128)(2,1)S(1)} %eta_sum.2.refs_0_), channel_id=1, source_target_pairs={{0,1},{1,0},{2,3},{3,2},{4,5},{5,4},{6,7},{7,6},{8,9},{9,8},{10,11... | collective-permute-start | bytes 196616 | tf_op jit(solution)/shard_map/ppermute | solution.py:51

commit v5 on v4

--- a/solution.py
+++ b/solution.py
@@ -211,7 +211,7 @@
     split_columns(dot(x[...], dz[...], ((0,), (0,))), mine_out, theirs_out)
 
 
-def turn_kernel(x, *refs):
+def turn_kernel(after, x, *refs):
     rims = [read_rim(r)[1] for r in refs[:-1]]
     refs[-1][...] = jnp.concatenate([x[...]] + rims, axis=0).T
 
@@ -371,7 +371,7 @@
     )
     share1 = phi_share(mine1, theirs1)
     xt = call(
-        turn_kernel, (x0, *mixes), [shaped((width, depth), BF16)], flops=1_000_000, name="turn"
+        turn_kernel, (mine1, x0, *mixes), [shaped((width, depth), BF16)], flops=1_000_000, name="turn"
     )[0]
     mine0, theirs0 = call(
         back_kernel,

time: 52 us -> 52.6 us (1.012)
  waiting for transfers between devices: 18.1 us -> 19.2 us
  starting transfers between devices: 21.7 us -> 21.1 us
    ppermute x4, waiting for transfers between devices: 6.9 us -> 7.51 us  [phi_share(): lax.ppermute(send, 'phi', [(i, i ^ 1 << level) for i in range(parts)])]
    ppermute x2, starting transfers between devices: 3.09 us -> 2.5 us  [eta_sum(): arrived = lax.ppermute(share, 'eta', [(0, 1), (1, 0)])]
    ppermute x2, waiting for transfers between devices: 2.67 us -> 3.26 us  [eta_sum(): arrived = lax.ppermute(share, 'eta', [(0, 1), (1, 0)])]
  transfers between devices with their start and end apart: 19 -> 19, of which waited for: 15 -> 14; matrix products, arithmetic and copies ran while one was open for 2% -> 2% of each run, Pallas kernels for 10% -> 10%
where the time goes in v5:
time: 52.6 us; the launch traced here: 52.4 us
  starting transfers between devices  21.1 us (40%)
  waiting for transfers between devices  19.2 us (37%)
  Pallas kernels  8.34 us (16%)
  local copies, waits for them, and re-layouts  2.13 us (4%)
  between operations  1.48 us (3%)
    pallas_call x20, Pallas kernels, call(): pl.pallas_call(kernel, out_shape=outs, in_specs=[FAR if far else VMEM] *...  8.34 us
    ppermute x4, waiting for transfers between devices, phi_share(): lax.ppermute(send, 'phi', [(i, i ^ 1 << level) for i in range(parts)])  7.51 us
    ppermute x4, starting transfers between devices, phi_share(): lax.ppermute(send, 'phi', [(i, i ^ 1 << level) for i in range(parts)])  5.27 us
    ppermute x2, starting transfers between devices, to_neighbours(): from_high = lax.ppermute(low_phi, 'phi', ring('phi', -1, True))  4.79 us
    ppermute x2, starting transfers between devices, to_neighbours(): from_low = lax.ppermute(high_phi, 'phi', ring('phi', 1, True))  4.26 us
    ppermute x2, waiting for transfers between devices, eta_sum(): arrived = lax.ppermute(share, 'eta', [(0, 1), (1, 0)])  3.26 us
    ppermute x2, waiting for transfers between devices, to_neighbours(): from_low = lax.ppermute(high_phi, 'phi', ring('phi', 1, True))  3.19 us
    ppermute x2, starting transfers between devices, to_neighbours(): return [from_low, from_high, lax.ppermute(low_eta, 'eta', [(0, 1), (1, 0)])]  3.14 us
  transfers between devices with their start and end apart: 19, of which 14 were waited for; matrix products, arithmetic and copies ran while one was open for 2% of the time, Pallas kernels for 10%

profile of v5, /device:TPU:0, one launch (start us, length us, event | category | flops | bytes accessed | tf_op | source)
XLA Modules:
  0.0 52.4 jit_solution(5042471982970994907)
XLA Ops:
  0.6 0.9 %slice_bitcast_fusion = bf16[128,512]{1,0:T(8,128)(2,1)S(1)} fusion(bf16[1,1,256,512]{3,2,1,0:T(8,128)(2,1)} %param.8), kind=kLoop, calls=%fused_computation.2 | loop fusion | bytes 262144 | tf_op jit(solution)/shard_map/slice | solution.py:302
  1.5 3.1 %collective-permute-start = (bf16[128,512]{1,0:T(8,128)(2,1)S(1)}, bf16[128,512]{1,0:T(8,128)(2,1)S(1)}, u32[]{:S(2)}, u32[]{:S(2)}) collective-permute-start(bf16[128,512]{1,0:T(8,128)(2,1)S(1)} %slice_bitcast_fusion), channel_id=1, source_target_pairs={{0,4},{4,8},{8,12},{12,0},{1,5},{5,9},{9,13},{13,1},{2,6},{6,10},{... | collective-permute-start | bytes 393224 | tf_op jit(solution)/shard_map/ppermute | solution.py:56
  4.6 2.1 %collective-permute-start.1 = (bf16[128,512]{1,0:T(8,128)(2,1)S(1)}, bf16[128,512]{1,0:T(8,128)(2,1)S(1)}, u32[]{:S(2)}, u32[]{:S(2)}) collective-permute-start(bf16[128,512]{1,0:T(8,128)(2,1)S(1)} %slice_bitcast_fusion), channel_id=1, source_target_pairs={{0,12},{4,0},{8,4},{12,8},{1,13},{5,1},{9,5},{13,9},{2,14},{6,2},{... | collective-permute-start | bytes 393224 | tf_op jit(solution)/shard_map/ppermute | solution.py:55
  6.7 1.6 %collective-permute-start.2 = (bf16[128,512]{1,0:T(8,128)(2,1)S(1)}, bf16[128,512]{1,0:T(8,128)(2,1)S(1)}, u32[]{:S(2)}, u32[]{:S(2)}) collective-permute-start(bf16[128,512]{1,0:T(8,128)(2,1)S(1)} %slice_bitcast_fusion), channel_id=1, source_target_pairs={{0,2},{2,0},{1,3},{3,1},{4,6},{6,4},{5,7},{7,5},{8,10},{10,8},{9,1... | collective-permute-start | bytes 393224 | tf_op jit(solution)/shard_map/ppermute | solution.py:58
  8.4 0.0 copy-start.2
  8.4 1.8 %build.1 = (bf16[512,640]{1,0:T(8,128)(2,1)S(1)}, bf16[512,512]{1,0:T(8,128)(2,1)S(1)}) custom-call(s32[12]{0:T(128)} %bitcast.25, s32[12]{0:T(128)} %bitcast.26, bf16[12,128,128]{2,1,0:T(8,128)(2,1)} %bitcast.23, s32[2,8,8]{2,1,0:T(8,128)} %mask.1, bf16[2,512,512]{2,1,0:T(8,128)(2,1)} %weights.1), custom_call_target="tpu_custom_call" | custom-call | flops 10000000 | bytes 2622048 | tf_op jit(solution)/shard_map/build/pallas_call | solution.py:22
  10.2 0.8 %collective-permute-done.refs_1_.refs_0_ = bf16[128,512]{1,0:T(8,128)(2,1)S(1)} collective-permute-done((bf16[128,512]{1,0:T(8,128)(2,1)S(1)}, bf16[128,512]{1,0:T(8,128)(2,1)S(1)}, u32[]{:S(2)}, u32[]{:S(2)}) %collective-permute-start) | collective-permute-done | bytes 131104 | tf_op jit(solution)/shard_map/ppermute | solution.py:56
  11.0 1.4 %collective-permute-done.1.refs_2_.refs_1_ = bf16[128,512]{1,0:T(8,128)(2,1)S(1)} collective-permute-done((bf16[128,512]{1,0:T(8,128)(2,1)S(1)}, bf16[128,512]{1,0:T(8,128)(2,1)S(1)}, u32[]{:S(2)}, u32[]{:S(2)}) %collective-permute-start.1) | collective-permute-done | bytes 131104 | tf_op jit(solution)/shard_map/ppermute | solution.py:55
  12.4 0.0 collective-permute-done.2.refs_3_.refs_2_
  12.4 0.0 copy-done.2
  12.4 0.6 %gather.8 = (bf16[256,512]{1,0:T(8,128)(2,1)S(1)}, bf16[256,512]{1,0:T(8,128)(2,1)S(1)}) custom-call(bf16[512,640]{1,0:T(8,128)(2,1)S(1)} %get-tuple-element.30.matrix, bf16[256,512]{1,0:T(8,128)(2,1)S(1)} %bitcast.16, bf16[128,512]{1,0:T(8,128)(2,1)S(1)} %collective-permute-done.refs_1_.refs_0_, ...), custom_call_target="tpu_custom_call" | custom-call | flops 335544320 | bytes 1835008 | tf_op jit(solution)/shard_map/gather/pallas_call | solution.py:22
  13.0 0.1 collective-permute-start.3
  13.7 0.9 %collective-permute-done.3.other = bf16[256,512]{1,0:T(8,128)(2,1)S(1)} collective-permute-done((bf16[256,512]{1,0:T(8,128)(2,1)S(1)}, bf16[256,512]{1,0:T(8,128)(2,1)S(1)}, u32[]{:S(2)}, u32[]{:S(2)}) %collective-permute-start.3) | collective-permute-done | bytes 262176 | tf_op jit(solution)/shard_map/ppermute | solution.py:51
  14.6 0.1 edge.1
  14.7 1.2 %collective-permute-start.4 = (bf16[128,512]{1,0:T(8,128)(2,1)S(1)}, bf16[128,512]{1,0:T(8,128)(2,1)S(1)}, u32[]{:S(2)}, u32[]{:S(2)}) collective-permute-start(bf16[128,512]{1,0:T(8,128)(2,1)S(1)} %edge.1), channel_id=1, source_target_pairs={{0,4},{4,8},{8,12},{12,0},{1,5},{5,9},{9,13},{13,1},{2,6},{6,10},{... | collective-permute-start | bytes 393224 | tf_op jit(solution)/shard_map/ppermute | solution.py:56
  15.9 2.7 %collective-permute-start.5 = (bf16[128,512]{1,0:T(8,128)(2,1)S(1)}, bf16[128,512]{1,0:T(8,128)(2,1)S(1)}, u32[]{:S(2)}, u32[]{:S(2)}) collective-permute-start(bf16[128,512]{1,0:T(8,128)(2,1)S(1)} %edge.1), channel_id=1, source_target_pairs={{0,12},{4,0},{8,4},{12,8},{1,13},{5,1},{9,5},{13,9},{2,14},{6,2},{... | collective-permute-start | bytes 393224 | tf_op jit(solution)/shard_map/ppermute | solution.py:55
  18.5 1.5 %collective-permute-start.6 = (bf16[128,512]{1,0:T(8,128)(2,1)S(1)}, bf16[128,512]{1,0:T(8,128)(2,1)S(1)}, u32[]{:S(2)}, u32[]{:S(2)}) collective-permute-start(bf16[128,512]{1,0:T(8,128)(2,1)S(1)} %edge.1), channel_id=1, source_target_pairs={{0,2},{2,0},{1,3},{3,1},{4,6},{6,4},{5,7},{7,5},{8,10},{10,8},{9,1... | collective-permute-start | bytes 393224 | tf_op jit(solution)/shard_map/ppermute | solution.py:58
  20.0 0.5 forward.1
  20.5 2.4 %collective-permute-done.4.refs_3_.refs_0_ = bf16[128,512]{1,0:T(8,128)(2,1)S(1)} collective-permute-done((bf16[128,512]{1,0:T(8,128)(2,1)S(1)}, bf16[128,512]{1,0:T(8,128)(2,1)S(1)}, u32[]{:S(2)}, u32[]{:S(2)}) %collective-permute-start.4) | collective-permute-done | bytes 131104 | tf_op jit(solution)/shard_map/ppermute | solution.py:56
  22.9 1.0 %collective-permute-done.5.refs_4_.refs_1_ = bf16[128,512]{1,0:T(8,128)(2,1)S(1)} collective-permute-done((bf16[128,512]{1,0:T(8,128)(2,1)S(1)}, bf16[128,512]{1,0:T(8,128)(2,1)S(1)}, u32[]{:S(2)}, u32[]{:S(2)}) %collective-permute-start.5) | collective-permute-done | bytes 131104 | tf_op jit(solution)/shard_map/ppermute | solution.py:55
  23.9 0.0 collective-permute-done.6.refs_5_.refs_2_
  23.9 0.0 copy-start
  23.9 0.0 copy-start.1
  23.9 1.0 %rim.1 = (bf16[256,512]{1,0:T(8,128)(2,1)S(1)}, bf16[256,512]{1,0:T(8,128)(2,1)S(1)}, f32[384,512]{1,0:T(8,128)S(1)}) custom-call(bf16[512,640]{1,0:T(8,128)(2,1)S(1)} %get-tuple-element.30.matrix, bf16[512,512]{1,0:T(8,128)(2,1)S(1)} %get-tuple-element.33.weight, bf16[256,512]{1,0:T(8,128)(2,1)S(1)} %get-tuple-element.34.new.state, ...), custom_call_target="tpu_custom_call" | custom-call | flops 603979776 | bytes 3538944 | tf_op jit(solution)/shard_map/rim/pallas_call | solution.py:22
  24.9 0.0 copy-start.3
  24.9 0.1 collective-permute-start.7
  25.0 0.0 copy-done
  25.0 0.2 copy-done.1
  25.2 0.4 later.1
  25.6 1.0 %collective-permute-done.7.other = bf16[256,512]{1,0:T(8,128)(2,1)S(1)} collective-permute-done((bf16[256,512]{1,0:T(8,128)(2,1)S(1)}, bf16[256,512]{1,0:T(8,128)(2,1)S(1)}, u32[]{:S(2)}, u32[]{:S(2)}) %collective-permute-start.7) | collective-permute-done | bytes 262176 | tf_op jit(solution)/shard_map/ppermute | solution.py:51
  26.5 0.0 copy-done.3
  26.5 0.7 %last.1 = (bf16[256,512]{1,0:T(8,128)(2,1)S(1)}, bf16[256,512]{1,0:T(8,128)(2,1)S(1)}, bf16[256,512]{1,0:T(8,128)(2,1)S(1)}, bf16[256,512]{1,0:T(8,128)(2,1)S(1)}) custom-call(s32[8,128]{1,0:T(8,128)S(1)} %broadcast_in_dim.22.count, bf16[256,512]{1,0:T(8,128)(2,1)S(1)} %get-tuple-element.34.new.state, bf16[256,512]{1,0:T(8,128)(2,1)S(1)} %get-tuple-element.35.own, ...), custom_call_target="tpu_custom_call" | custom-call | flops 268435456 | bytes 2625536 | tf_op jit(solution)/shard_map/last/pallas_call | solution.py:22
  27.2 0.2 collective-permute-start.8
  27.5 0.3 grad.1
  27.8 0.4 collective-permute-start.14
  28.2 0.2 turn.1.xt
  28.5 0.4 collective-permute-done.8.dx_other
  28.9 0.9 %back.1 = (f32[512,256]{1,0:T(8,128)S(1)}, bf16[512,256]{1,0:T(8,128)(2,1)S(1)}) custom-call(bf16[640,512]{1,0:T(8,128)(2,1)S(1)} %get-tuple-element.39.mt, bf16[256,512]{1,0:T(8,128)(2,1)S(1)} %get-tuple-element.40.dx, bf16[256,512]{1,0:T(8,128)(2,1)S(1)} %collective-permute-done.8.dx_other, bf16[256,512]{1,0:T(8,128)(2,1)S(1)} %bitcast.20, ...), custom_call_target="tpu_custom_call" | custom-call | flops 671088640 | bytes 4194304 | tf_op jit(solution)/shard_map/back/pallas_call | solution.py:22
  29.8 0.2 collective-permute-start.9
  30.0 0.0 collective-permute-done.14.arrived
  30.1 0.8 %collective-permute-start.15 = (bf16[256,256]{1,0:T(8,128)(2,1)S(1)}, bf16[256,256]{1,0:T(8,128)(2,1)S(1)}, u32[]{:S(2)}, u32[]{:S(2)}) collective-permute-start(bf16[256,256]{1,0:T(8,128)(2,1)S(1)} %get-tuple-element.55), channel_id=1, source_target_pairs={{0,4},{4,0},{8,12},{12,8},{1,5},{5,1},{9,13},{13,9},{2,6},{6,2},{1... | collective-permute-start | bytes 393224 | tf_op jit(solution)/shard_map/ppermute | solution.py:276
  30.9 0.5 %collective-permute-done.9.arrived = bf16[512,256]{1,0:T(8,128)(2,1)S(1)} collective-permute-done((bf16[512,256]{1,0:T(8,128)(2,1)S(1)}, bf16[512,256]{1,0:T(8,128)(2,1)S(1)}, u32[]{:S(2)}, u32[]{:S(2)}) %collective-permute-start.9) | collective-permute-done | bytes 262176 | tf_op jit(solution)/shard_map/ppermute | solution.py:51
  31.5 0.8 %collective-permute-start.10 = (bf16[256,256]{1,0:T(8,128)(2,1)S(1)}, bf16[256,256]{1,0:T(8,128)(2,1)S(1)}, u32[]{:S(2)}, u32[]{:S(2)}) collective-permute-start(bf16[256,256]{1,0:T(8,128)(2,1)S(1)} %get-tuple-element.50), channel_id=1, source_target_pairs={{0,4},{4,0},{8,12},{12,8},{1,5},{5,1},{9,13},{13,9},{2,6},{6,2},{1... | collective-permute-start | bytes 393224 | tf_op jit(solution)/shard_map/ppermute | solution.py:276
  32.3 4.2 %collective-permute-done.15.arrived = bf16[256,256]{1,0:T(8,128)(2,1)S(1)} collective-permute-done((bf16[256,256]{1,0:T(8,128)(2,1)S(1)}, bf16[256,256]{1,0:T(8,128)(2,1)S(1)}, u32[]{:S(2)}, u32[]{:S(2)}) %collective-permute-start.15) | collective-permute-done | bytes 131104 | tf_op jit(solution)/shard_map/ppermute | solution.py:276
  36.5 1.6 %collective-permute-start.16 = (bf16[128,256]{1,0:T(8,128)(2,1)S(1)}, bf16[128,256]{1,0:T(8,128)(2,1)S(1)}, u32[]{:S(2)}, u32[]{:S(2)}) collective-permute-start(bf16[128,256]{1,0:T(8,128)(2,1)S(1)} %get-tuple-element.57), channel_id=1, source_target_pairs={{0,8},{4,12},{8,0},{12,4},{1,9},{5,13},{9,1},{13,5},{2,10},{6,14},... | collective-permute-start | bytes 196616 | tf_op jit(solution)/shard_map/ppermute | solution.py:276
  38.1 0.6 %collective-permute-done.10.arrived = bf16[256,256]{1,0:T(8,128)(2,1)S(1)} collective-permute-done((bf16[256,256]{1,0:T(8,128)(2,1)S(1)}, bf16[256,256]{1,0:T(8,128)(2,1)S(1)}, u32[]{:S(2)}, u32[]{:S(2)}) %collective-permute-start.10) | collective-permute-done | bytes 131104 | tf_op jit(solution)/shard_map/ppermute | solution.py:276
  38.7 2.0 %collective-permute-start.11 = (bf16[128,256]{1,0:T(8,128)(2,1)S(1)}, bf16[128,256]{1,0:T(8,128)(2,1)S(1)}, u32[]{:S(2)}, u32[]{:S(2)}) collective-permute-start(bf16[128,256]{1,0:T(8,128)(2,1)S(1)} %get-tuple-element.52), channel_id=1, source_target_pairs={{0,8},{4,12},{8,0},{12,4},{1,9},{5,13},{9,1},{13,5},{2,10},{6,14},... | collective-permute-start | bytes 196616 | tf_op jit(solution)/shard_map/ppermute | solution.py:276
  40.8 0.7 %gather_fusion = s32[128,2,8]{2,0,1:T(8,128)S(1)} fusion(s32[2,8,8]{2,1,0:T(8,128)S(1)} %copy-done, s32[1024]{0:T(1024)S(1)} %pad_clamp_fusion), kind=kCustom, calls=%fused_computation | custom fusion | bytes 16896 | tf_op jit(solution)/shard_map/jit(_take)/gather | solution.py:391
  41.5 2.7 %collective-permute-done.16.refs_0_ = bf16[128,256]{1,0:T(8,128)(2,1)S(1)} collective-permute-done((bf16[128,256]{1,0:T(8,128)(2,1)S(1)}, bf16[128,256]{1,0:T(8,128)(2,1)S(1)}, u32[]{:S(2)}, u32[]{:S(2)}) %collective-permute-start.16) | collective-permute-done | bytes 65568 | tf_op jit(solution)/shard_map/ppermute | solution.py:276
  44.3 1.5 %collective-permute-start.17 = (bf16[128,256]{1,0:T(8,128)(2,1)S(1)}, bf16[128,256]{1,0:T(8,128)(2,1)S(1)}, u32[]{:S(2)}, u32[]{:S(2)}) collective-permute-start(bf16[128,256]{1,0:T(8,128)(2,1)S(1)} %phi_sum.3.own), channel_id=1, source_target_pairs={{0,2},{2,0},{1,3},{3,1},{4,6},{6,4},{5,7},{7,5},{8,10},{10,8},{9,1... | collective-permute-start | bytes 196616 | tf_op jit(solution)/shard_map/ppermute | solution.py:282
  45.8 0.0 collective-permute-done.11.refs_0_
  45.8 1.0 %collective-permute-start.12 = (bf16[128,256]{1,0:T(8,128)(2,1)S(1)}, bf16[128,256]{1,0:T(8,128)(2,1)S(1)}, u32[]{:S(2)}, u32[]{:S(2)}) collective-permute-start(bf16[128,256]{1,0:T(8,128)(2,1)S(1)} %phi_sum.2.own), channel_id=1, source_target_pairs={{0,2},{2,0},{1,3},{3,1},{4,6},{6,4},{5,7},{7,5},{8,10},{10,8},{9,1... | collective-permute-start | bytes 196616 | tf_op jit(solution)/shard_map/ppermute | solution.py:282
  46.8 2.2 %collective-permute-done.17.refs_0_ = bf16[128,256]{1,0:T(8,128)(2,1)S(1)} collective-permute-done((bf16[128,256]{1,0:T(8,128)(2,1)S(1)}, bf16[128,256]{1,0:T(8,128)(2,1)S(1)}, u32[]{:S(2)}, u32[]{:S(2)}) %collective-permute-start.17) | collective-permute-done | bytes 65568 | tf_op jit(solution)/shard_map/ppermute | solution.py:282
  49.0 0.1 collective-permute-start.18
  49.1 1.1 %collective-permute-done.12.refs_0_ = bf16[128,256]{1,0:T(8,128)(2,1)S(1)} collective-permute-done((bf16[128,256]{1,0:T(8,128)(2,1)S(1)}, bf16[128,256]{1,0:T(8,128)(2,1)S(1)}, u32[]{:S(2)}, u32[]{:S(2)}) %collective-permute-start.12) | collective-permute-done | bytes 65568 | tf_op jit(solution)/shard_map/ppermute | solution.py:282
  50.2 0.1 collective-permute-start.13
  50.3 0.1 convert_bitcast_fusion
  50.4 0.1 copy.10
  50.5 0.2 copy.11.refs_4_
  50.7 0.7 %emit.1 = bf16[256,512]{1,0:T(8,128)(2,1)} custom-call(bf16[256,512]{1,0:T(8,128)(2,1)S(1)} %get-tuple-element.38.value), custom_call_target="tpu_custom_call" | custom-call | bytes 524288 | tf_op jit(solution)/shard_map/emit/pallas_call | solution.py:22
  51.4 0.0 collective-permute-done.18.refs_3_
  51.4 0.1 collective-permute-done.13.refs_1_
  51.5 0.9 %finish.1 = f32[2,128,512]{2,1,0:T(8,128)} custom-call(bf16[128,256]{1,0:T(8,128)(2,1)S(1)} %eta_sum.2.refs_0_, bf16[128,256]{1,0:T(8,128)(2,1)S(1)} %collective-permute-done.13.refs_1_, bf16[128,256]{1,0:T(8,128)(2,1)S(1)} %eta_sum.3.refs_2_, bf16[128,256]{1,0:T(8,128)(2,1)S(1)} %collective-permute-done.18.refs_3_, f32[2,128,512]{2,1,0:T(8,128)S(1)} %copy.11.refs_4_), custom_call_target="tpu_custom_call" | custom-call | bytes 1310720 | tf_op jit(solution)/shard_map/finish/pallas_call | solution.py:22
  (13 shorter events, 0.3 us)
Async XLA Ops:
  1.5 9.4 %collective-permute-start = (bf16[128,512]{1,0:T(8,128)(2,1)S(1)}, bf16[128,512]{1,0:T(8,128)(2,1)S(1)}, u32[]{:S(2)}, u32[]{:S(2)}) collective-permute-start(bf16[128,512]{1,0:T(8,128)(2,1)S(1)} %slice_bitcast_fusion), channel_id=1, source_target_pairs={{0,4},{4,8},{8,12},{12,0},{1,5},{5,9},{9,13},{13,1},{2,6},{6,10},{... | collective-permute-start | bytes 393224 | tf_op jit(solution)/shard_map/ppermute | solution.py:56
  4.6 7.8 %collective-permute-start.1 = (bf16[128,512]{1,0:T(8,128)(2,1)S(1)}, bf16[128,512]{1,0:T(8,128)(2,1)S(1)}, u32[]{:S(2)}, u32[]{:S(2)}) collective-permute-start(bf16[128,512]{1,0:T(8,128)(2,1)S(1)} %slice_bitcast_fusion), channel_id=1, source_target_pairs={{0,12},{4,0},{8,4},{12,8},{1,13},{5,1},{9,5},{13,9},{2,14},{6,2},{... | collective-permute-start | bytes 393224 | tf_op jit(solution)/shard_map/ppermute | solution.py:55
  6.7 5.7 %collective-permute-start.2 = (bf16[128,512]{1,0:T(8,128)(2,1)S(1)}, bf16[128,512]{1,0:T(8,128)(2,1)S(1)}, u32[]{:S(2)}, u32[]{:S(2)}) collective-permute-start(bf16[128,512]{1,0:T(8,128)(2,1)S(1)} %slice_bitcast_fusion), channel_id=1, source_target_pairs={{0,2},{2,0},{1,3},{3,1},{4,6},{6,4},{5,7},{7,5},{8,10},{10,8},{9,1... | collective-permute-start | bytes 393224 | tf_op jit(solution)/shard_map/ppermute | solution.py:58
  8.4 4.0 %copy-start.2 = (bf16[1,1,256,512]{3,2,1,0:T(8,128)(2,1)S(1)}, bf16[1,1,256,512]{3,2,1,0:T(8,128)(2,1)}, u32[]{:S(2)}) copy-start(bf16[1,1,256,512]{3,2,1,0:T(8,128)(2,1)} %param.8) | copy-start | bytes 786436
  13.0 1.6 %collective-permute-start.3 = (bf16[256,512]{1,0:T(8,128)(2,1)S(1)}, bf16[256,512]{1,0:T(8,128)(2,1)S(1)}, u32[]{:S(2)}, u32[]{:S(2)}) collective-permute-start(bf16[256,512]{1,0:T(8,128)(2,1)S(1)} %get-tuple-element.32), channel_id=1, source_target_pairs={{0,1},{1,0},{2,3},{3,2},{4,5},{5,4},{6,7},{7,6},{8,9},{9,8},{10,11... | collective-permute-start | bytes 786440 | tf_op jit(solution)/shard_map/ppermute | solution.py:51
  14.7 8.2 %collective-permute-start.4 = (bf16[128,512]{1,0:T(8,128)(2,1)S(1)}, bf16[128,512]{1,0:T(8,128)(2,1)S(1)}, u32[]{:S(2)}, u32[]{:S(2)}) collective-permute-start(bf16[128,512]{1,0:T(8,128)(2,1)S(1)} %edge.1), channel_id=1, source_target_pairs={{0,4},{4,8},{8,12},{12,0},{1,5},{5,9},{9,13},{13,1},{2,6},{6,10},{... | collective-permute-start | bytes 393224 | tf_op jit(solution)/shard_map/ppermute | solution.py:56
  15.9 8.1 %collective-permute-start.5 = (bf16[128,512]{1,0:T(8,128)(2,1)S(1)}, bf16[128,512]{1,0:T(8,128)(2,1)S(1)}, u32[]{:S(2)}, u32[]{:S(2)}) collective-permute-start(bf16[128,512]{1,0:T(8,128)(2,1)S(1)} %edge.1), channel_id=1, source_target_pairs={{0,12},{4,0},{8,4},{12,8},{1,13},{5,1},{9,5},{13,9},{2,14},{6,2},{... | collective-permute-start | bytes 393224 | tf_op jit(solution)/shard_map/ppermute | solution.py:55
  18.5 5.4 %collective-permute-start.6 = (bf16[128,512]{1,0:T(8,128)(2,1)S(1)}, bf16[128,512]{1,0:T(8,128)(2,1)S(1)}, u32[]{:S(2)}, u32[]{:S(2)}) collective-permute-start(bf16[128,512]{1,0:T(8,128)(2,1)S(1)} %edge.1), channel_id=1, source_target_pairs={{0,2},{2,0},{1,3},{3,1},{4,6},{6,4},{5,7},{7,5},{8,10},{10,8},{9,1... | collective-permute-start | bytes 393224 | tf_op jit(solution)/shard_map/ppermute | solution.py:58
  23.9 1.1 %copy-start = (s32[2,8,8]{2,1,0:T(8,128)S(1)}, s32[2,8,8]{2,1,0:T(8,128)}, u32[]{:S(2)}) copy-start(s32[2,8,8]{2,1,0:T(8,128)} %mask.1) | copy-start | bytes 1540
  23.9 1.2 %copy-start.1 = (bf16[2,512,512]{2,1,0:T(8,128)(2,1)S(1)}, bf16[2,512,512]{2,1,0:T(8,128)(2,1)}, u32[]{:S(2)}) copy-start(bf16[2,512,512]{2,1,0:T(8,128)(2,1)} %weights.1) | copy-start | bytes 3145732
  24.9 1.6 %copy-start.3 = (bf16[1,1,256,512]{3,2,1,0:T(8,128)(2,1)S(1)}, bf16[1,1,256,512]{3,2,1,0:T(8,128)(2,1)}, u32[]{:S(2)}) copy-start(bf16[1,1,256,512]{3,2,1,0:T(8,128)(2,1)} %param.9) | copy-start | bytes 786436
  24.9 1.6 %collective-permute-start.7 = (bf16[256,512]{1,0:T(8,128)(2,1)S(1)}, bf16[256,512]{1,0:T(8,128)(2,1)S(1)}, u32[]{:S(2)}, u32[]{:S(2)}) collective-permute-start(bf16[256,512]{1,0:T(8,128)(2,1)S(1)} %get-tuple-element.36), channel_id=1, source_target_pairs={{0,1},{1,0},{2,3},{3,2},{4,5},{5,4},{6,7},{7,6},{8,9},{9,8},{10,11... | collective-permute-start | bytes 786440 | tf_op jit(solution)/shard_map/ppermute | solution.py:51
  27.2 1.6 %collective-permute-start.8 = (bf16[256,512]{1,0:T(8,128)(2,1)S(1)}, bf16[256,512]{1,0:T(8,128)(2,1)S(1)}, u32[]{:S(2)}, u32[]{:S(2)}) collective-permute-start(bf16[256,512]{1,0:T(8,128)(2,1)S(1)} %get-tuple-element.40.dx), channel_id=1, source_target_pairs={{0,1},{1,0},{2,3},{3,2},{4,5},{5,4},{6,7},{7,6},{8,9},{9,8},{10,11... | collective-permute-start | bytes 786440 | tf_op jit(solution)/shard_map/ppermute | solution.py:51
  27.8 2.2 %collective-permute-start.14 = (bf16[512,256]{1,0:T(8,128)(2,1)S(1)}, bf16[512,256]{1,0:T(8,128)(2,1)S(1)}, u32[]{:S(2)}, u32[]{:S(2)}) collective-permute-start(bf16[512,256]{1,0:T(8,128)(2,1)S(1)} %get-tuple-element.53), channel_id=1, source_target_pairs={{0,1},{1,0},{2,3},{3,2},{4,5},{5,4},{6,7},{7,6},{8,9},{9,8},{10,11... | collective-permute-start | bytes 786440 | tf_op jit(solution)/shard_map/ppermute | solution.py:51
  29.8 1.6 %collective-permute-start.9 = (bf16[512,256]{1,0:T(8,128)(2,1)S(1)}, bf16[512,256]{1,0:T(8,128)(2,1)S(1)}, u32[]{:S(2)}, u32[]{:S(2)}) collective-permute-start(bf16[512,256]{1,0:T(8,128)(2,1)S(1)} %get-tuple-element.48), channel_id=1, source_target_pairs={{0,1},{1,0},{2,3},{3,2},{4,5},{5,4},{6,7},{7,6},{8,9},{9,8},{10,11... | collective-permute-start | bytes 786440 | tf_op jit(solution)/shard_map/ppermute | solution.py:51
  30.1 6.4 %collective-permute-start.15 = (bf16[256,256]{1,0:T(8,128)(2,1)S(1)}, bf16[256,256]{1,0:T(8,128)(2,1)S(1)}, u32[]{:S(2)}, u32[]{:S(2)}) collective-permute-start(bf16[256,256]{1,0:T(8,128)(2,1)S(1)} %get-tuple-element.55), channel_id=1, source_target_pairs={{0,4},{4,0},{8,12},{12,8},{1,5},{5,1},{9,13},{13,9},{2,6},{6,2},{1... | collective-permute-start | bytes 393224 | tf_op jit(solution)/shard_map/ppermute | solution.py:276
  31.5 7.3 %collective-permute-start.10 = (bf16[256,256]{1,0:T(8,128)(2,1)S(1)}, bf16[256,256]{1,0:T(8,128)(2,1)S(1)}, u32[]{:S(2)}, u32[]{:S(2)}) collective-permute-start(bf16[256,256]{1,0:T(8,128)(2,1)S(1)} %get-tuple-element.50), channel_id=1, source_target_pairs={{0,4},{4,0},{8,12},{12,8},{1,5},{5,1},{9,13},{13,9},{2,6},{6,2},{1... | collective-permute-start | bytes 393224 | tf_op jit(solution)/shard_map/ppermute | solution.py:276
  36.5 7.8 %collective-permute-start.16 = (bf16[128,256]{1,0:T(8,128)(2,1)S(1)}, bf16[128,256]{1,0:T(8,128)(2,1)S(1)}, u32[]{:S(2)}, u32[]{:S(2)}) collective-permute-start(bf16[128,256]{1,0:T(8,128)(2,1)S(1)} %get-tuple-element.57), channel_id=1, source_target_pairs={{0,8},{4,12},{8,0},{12,4},{1,9},{5,13},{9,1},{13,5},{2,10},{6,14},... | collective-permute-start | bytes 196616 | tf_op jit(solution)/shard_map/ppermute | solution.py:276
  38.7 7.1 %collective-permute-start.11 = (bf16[128,256]{1,0:T(8,128)(2,1)S(1)}, bf16[128,256]{1,0:T(8,128)(2,1)S(1)}, u32[]{:S(2)}, u32[]{:S(2)}) collective-permute-start(bf16[128,256]{1,0:T(8,128)(2,1)S(1)} %get-tuple-element.52), channel_id=1, source_target_pairs={{0,8},{4,12},{8,0},{12,4},{1,9},{5,13},{9,1},{13,5},{2,10},{6,14},... | collective-permute-start | bytes 196616 | tf_op jit(solution)/shard_map/ppermute | solution.py:276
  44.3 4.7 %collective-permute-start.17 = (bf16[128,256]{1,0:T(8,128)(2,1)S(1)}, bf16[128,256]{1,0:T(8,128)(2,1)S(1)}, u32[]{:S(2)}, u32[]{:S(2)}) collective-permute-start(bf16[128,256]{1,0:T(8,128)(2,1)S(1)} %phi_sum.3.own), channel_id=1, source_target_pairs={{0,2},{2,0},{1,3},{3,1},{4,6},{6,4},{5,7},{7,5},{8,10},{10,8},{9,1... | collective-permute-start | bytes 196616 | tf_op jit(solution)/shard_map/ppermute | solution.py:282
  45.8 4.3 %collective-permute-start.12 = (bf16[128,256]{1,0:T(8,128)(2,1)S(1)}, bf16[128,256]{1,0:T(8,128)(2,1)S(1)}, u32[]{:S(2)}, u32[]{:S(2)}) collective-permute-start(bf16[128,256]{1,0:T(8,128)(2,1)S(1)} %phi_sum.2.own), channel_id=1, source_target_pairs={{0,2},{2,0},{1,3},{3,1},{4,6},{6,4},{5,7},{7,5},{8,10},{10,8},{9,1... | collective-permute-start | bytes 196616 | tf_op jit(solution)/shard_map/ppermute | solution.py:282
  49.0 2.4 %collective-permute-start.18 = (bf16[128,256]{1,0:T(8,128)(2,1)S(1)}, bf16[128,256]{1,0:T(8,128)(2,1)S(1)}, u32[]{:S(2)}, u32[]{:S(2)}) collective-permute-start(bf16[128,256]{1,0:T(8,128)(2,1)S(1)} %eta_sum.3.refs_2_), channel_id=1, source_target_pairs={{0,1},{1,0},{2,3},{3,2},{4,5},{5,4},{6,7},{7,6},{8,9},{9,8},{10,11... | collective-permute-start | bytes 196616 | tf_op jit(solution)/shard_map/ppermute | solution.py:51
  50.2 1.3 %collective-permute-start.13 = (bf16[128,256]{1,0:T(8,128)(2,1)S(1)}, bf16[128,256]{1,0:T(8,128)(2,1)S(1)}, u32[]{:S(2)}, u32[]{:S(2)}) collective-permute-start(bf16[128,256]{1,0:T(8,128)(2,1)S(1)} %eta_sum.2.refs_0_), channel_id=1, source_target_pairs={{0,1},{1,0},{2,3},{3,2},{4,5},{5,4},{6,7},{7,6},{8,9},{9,8},{10,11... | collective-permute-start | bytes 196616 | tf_op jit(solution)/shard_map/ppermute | solution.py:51
